TPU v7x, 256 devices: a whole 4x4x8 slice. The times are simulated.
256 devices in a mesh: comp: 2 (over core), lat: 16 (over y, z_lo), lon: 8 (over z_hi, x).
Axes of the slice: x: 4, y: 4, z: 8 (z_hi: 2, z_lo: 4; z = z_hi * 4 + z_lo), core: 2. Of those that a mesh axis runs over, the one named last changes fastest.
Arguments:
- innovations: float32 [2, 3, 16384, 512], P('comp', None, ('lat', 'lon')), may hold values from -6 to 6
- obs_owner: int32 [2, 3, 16384, 1], P('comp', None, ('lat', 'lon')), may hold values from 0 to 127; in each aligned block of 128 rows (0 to 127, 128 to 255, ..., all dimensions but the last counted through in order) at most 2 rows name the same one
- obs_cell: int32 [2, 3, 16384], P('comp', None, ('lat', 'lon')), may hold values from 0 to 1023
- velocity: float32 [2, 3, 2, 128, 128, 1024], P('comp', None, None, None, 'lat', 'lon'), may hold values from -0.2 to 0.2
- diffusion: float32 [2, 3, 2, 128, 128, 1024], P('comp', None, None, None, 'lat', 'lon'), may hold values from 0.01 to 0.08
- mixing: float32 [2, 4, 4], P('comp'), may hold values from -0.15 to 0.15
- air_sea: float32 [4, 4], replicated, may hold values from -1 to 1
- sea_mask: int32 [128, 1024], P('lat', 'lon'), may hold values 0 or 1
Outputs:
- gradient: float32 [2, 4, 128, 128, 1024], P('comp', None, None, 'lat', 'lon')
Inputs may be any that keep to these rules, and one draw needn't show every extreme that they name: `obs_owner`: among the 128 rows of one device for one section and timestep, no owner is named more than 2 times, a bound that some block reaches.
All inputs are finite; a program needn't handle non-finite values. No bound on the sum of `sea_mask` on one device may be relied on, other than what follows from the above.
Results may differ from a plain program's by a relative error of at most 0.0001.
Values sent between devices are 32-bit elements; how exact they have to be, the bound alone decides.
No kernel may reach another device: no remote copies, remote signals or barrier semaphores. Data moves between devices by JAX's collectives and lax.ppermute only.
A program may use at most 320 MiB of HBM per device.

v0:
```python
import functools

import jax
import jax.numpy as jnp
from jax import lax
from jax.experimental import pallas as pl
from jax.experimental.pallas import tpu as pltpu
from jax.sharding import PartitionSpec as P

LANES = 128
SUBS = 8
VMEM_LIMIT = 40 * 1024 * 1024


def split3(x):
    hi = x.astype(jnp.bfloat16)
    rest = x - hi.astype(jnp.float32)
    mid = rest.astype(jnp.bfloat16)
    low = (rest - mid.astype(jnp.float32)).astype(jnp.bfloat16)
    return [hi, mid, low]


def pack_kernel(slots, rows_ref, owner_ref, cell_ref, out_ref):
    steps, count, width = rows_ref.shape
    owners = count
    parts = width // LANES
    stride = out_ref.shape[0] // owners
    dest = lax.broadcasted_iota(jnp.int32, (owners, count), 0)
    lane = lax.broadcasted_iota(jnp.int32, (owners, count), 1)
    before = (dest < lane).astype(jnp.bfloat16)
    cells = jnp.zeros((owners, LANES), jnp.float32)
    for step in range(steps):
        hits = owner_ref[step : step + 1, :] == dest
        hits_f = hits.astype(jnp.float32)
        prior = jnp.dot(hits_f.astype(jnp.bfloat16), before, preferred_element_type=jnp.float32)
        terms = jnp.concatenate(split3(rows_ref[step]), axis=0)
        marks = (cell_ref[step : step + 1, :] + 1).astype(jnp.float32)
        for k in range(slots):
            slot = step * slots + k
            pick = jnp.where(prior == float(k), hits_f, 0.0)
            pick_b = pick.astype(jnp.bfloat16)
            out = jnp.dot(
                jnp.concatenate([pick_b] * 3, axis=1), terms, preferred_element_type=jnp.float32
            )
            for part in range(parts):
                out_ref[pl.ds(slot * parts + part, owners, stride=stride), :] = out[
                    :, part * LANES : (part + 1) * LANES
                ]
            mark = jnp.sum(pick * marks, axis=1, keepdims=True)
            cells = jnp.where(lane == slot, mark, cells)
    out_ref[pl.ds(stride - 1, owners, stride=stride), :] = cells


def spread_rows(step, slots, got_ref, width):
    parts = width // LANES
    stride = parts * slots * 3 + 1
    sources = got_ref.shape[0] // stride
    marks = got_ref[pl.ds(stride - 1, sources, stride=stride), :]
    where_to = lax.broadcasted_iota(jnp.int32, (sources, SUBS * LANES), 1)
    terms, onehots = [], []
    for k in range(slots):
        slot = step * slots + k
        cols = []
        for part in range(parts):
            block = got_ref[pl.ds(slot * parts + part, sources, stride=stride), :]
            cols.append(block.T)
        turned = jnp.concatenate(cols, axis=0)
        terms += split3(turned)
        cell = marks[:, slot : slot + 1].astype(jnp.int32) - 1
        onehot = (cell == where_to).astype(jnp.float32).astype(jnp.bfloat16)
        onehots += [onehot] * 3
    return jnp.dot(
        jnp.concatenate(terms, axis=1),
        jnp.concatenate(onehots, axis=0),
        preferred_element_type=jnp.float32,
    )


def take_edges(m_ref, south_ref, north_ref, fields, levels):
    south_ref[...] = m_ref[pl.ds(0, fields * levels, stride=SUBS), :]
    north_ref[...] = m_ref[pl.ds(SUBS - 1, fields * levels, stride=SUBS), :]


def take_columns(m_ref, west_ref, east_ref, fields, levels):
    lane = lax.broadcasted_iota(jnp.int32, (SUBS, LANES), 1)
    for f in range(fields):

        def body(i, cols, f=f):
            west, east = cols
            for j in range(8):
                level = i * 8 + j
                plane = m_ref[pl.ds(pl.multiple_of((f * levels + level) * SUBS, SUBS), SUBS), :]
                west = jnp.where(lane == level, pltpu.roll(plane, level, 1), west)
                east = jnp.where(lane == level, pltpu.roll(plane, (level + 1) % LANES, 1), east)
            return west, east

        zero = jnp.zeros((SUBS, LANES), jnp.float32)
        west, east = lax.fori_loop(0, levels // 8, body, (zero, zero))
        west_ref[f * SUBS : (f + 1) * SUBS, :] = west
        east_ref[f * SUBS : (f + 1) * SUBS, :] = east


def first_kernel(step, slots, fields, levels, got_ref, mask_ref, m_ref, south_ref, north_ref, west_ref, east_ref):
    width = fields * levels
    out = spread_rows(step, slots, got_ref, width)
    for row in range(SUBS):
        m_ref[pl.ds(row, width, stride=SUBS), :] = (
            out[:, row * LANES : (row + 1) * LANES] * mask_ref[row : row + 1, :]
        )
    take_edges(m_ref, south_ref, north_ref, fields, levels)
    take_columns(m_ref, west_ref, east_ref, fields, levels)


def forcing_kernel(step, slots, width, got_ref, f_ref):
    out = spread_rows(step, slots, got_ref, width)
    for row in range(SUBS):
        f_ref[pl.ds(row, width, stride=SUBS), :] = out[:, row * LANES : (row + 1) * LANES]


def step_kernel(
    last,
    fields,
    levels,
    mix_ref,
    air_ref,
    m_ref,
    vel_ref,
    dif_ref,
    open_ref,
    sea_ref,
    mask_ref,
    from_south_ref,
    from_north_ref,
    from_west_ref,
    from_east_ref,
    low_ref,
    east_rim_ref,
    north_rim_ref,
    *rest,
):
    if last:
        (out_ref,) = rest
    else:
        f_ref, out_ref, south_ref, north_ref, west_ref, east_ref = rest
    lane = lax.broadcasted_iota(jnp.int32, (SUBS, LANES), 1)
    sub = lax.broadcasted_iota(jnp.int32, (SUBS, LANES), 0)
    at_west, at_east = lane == 0, lane == LANES - 1
    at_south, at_north = sub == 0, sub == SUBS - 1
    opened = open_ref[...]
    mask = mask_ref[...]
    mix = [[mix_ref[f, g] for g in range(fields)] for f in range(fields)]
    from_west = [from_west_ref[f * SUBS : (f + 1) * SUBS, :] for f in range(fields)]
    from_east = [from_east_ref[f * SUBS : (f + 1) * SUBS, :] for f in range(fields)]
    east_rim = east_rim_ref[...]

    def level_step(level):
        w_e, k_e, w_n, k_n = vel_ref[0, level], dif_ref[0, level], vel_ref[1, level], dif_ref[1, level]
        up_e = jnp.maximum(w_e, 0.0) + k_e
        down_e = jnp.minimum(w_e, 0.0) - k_e
        up_n = (jnp.maximum(w_n, 0.0) + k_n) * opened
        down_n = (jnp.minimum(w_n, 0.0) - k_n) * opened
        to_first = (LANES - level) % LANES
        to_last = LANES - 1 - level
        down_w = jnp.where(at_west, pltpu.roll(east_rim, to_first, 1), pltpu.roll(down_e, 1, 1))
        down_s = jnp.where(at_south, north_rim_ref[pl.ds(level, 1), :], pltpu.roll(down_n, 1, 0))
        planes = []
        for f in range(fields):
            at = pl.multiple_of((f * levels + level) * SUBS, SUBS)
            planes.append(m_ref[pl.ds(at, SUBS), :])
        for g in range(fields):
            m = planes[g]
            result = m
            for f in range(fields):
                result = result + mix[f][g] * planes[f]
            east = jnp.where(at_east, pltpu.roll(from_east[g], to_last, 1), pltpu.roll(m, LANES - 1, 1))
            west = jnp.where(at_west, pltpu.roll(from_west[g], to_first, 1), pltpu.roll(m, 1, 1))
            row = g * levels + level
            north = jnp.where(at_north, from_north_ref[pl.ds(row, 1), :], pltpu.roll(m, SUBS - 1, 0))
            south = jnp.where(at_south, from_south_ref[pl.ds(row, 1), :], pltpu.roll(m, 1, 0))
            result = result + up_e * (east - m) + down_w * (m - west)
            result = result + up_n * (north - m) + down_s * (m - south)
            at = pl.multiple_of(row * SUBS, SUBS)
            out_ref[pl.ds(at, SUBS), :] = result

    def body(i, carry):
        for j in range(4):
            level_step(i * 4 + j)
        return carry

    lax.fori_loop(0, levels // 4, body, 0)
    sea = sea_ref[...]
    for g in range(fields):
        coupled = jnp.zeros((SUBS, LANES), jnp.float32)
        for f in range(fields):
            coupled = coupled + air_ref[f, g] * low_ref[f * SUBS : (f + 1) * SUBS, :]
        at = g * levels * SUBS
        out_ref[at : at + SUBS, :] = out_ref[at : at + SUBS, :] + sea * coupled
    if not last:

        def add(i, carry):
            for j in range(8):
                at = pl.multiple_of((i * 8 + j) * SUBS, SUBS)
                out_ref[pl.ds(at, SUBS), :] = (
                    out_ref[pl.ds(at, SUBS), :] + f_ref[pl.ds(at, SUBS), :]
                ) * mask
            return carry

        lax.fori_loop(0, fields * levels // 8, add, 0)
        take_edges(out_ref, south_ref, north_ref, fields, levels)
        take_columns(out_ref, west_ref, east_ref, fields, levels)


def params():
    return pltpu.CompilerParams(vmem_limit_bytes=VMEM_LIMIT)


def ring(axis, by, closed):
    count = lax.axis_size(axis)
    return [(i, (i + by) % count) for i in range(count) if closed or 0 <= i + by < count]


def shards(innovations, obs_owner, obs_cell, velocity, diffusion, mixing, air_sea, sea_mask):
    lat_count = lax.axis_size("lat")
    lon_count = lax.axis_size("lon")
    owners = lat_count * lon_count
    steps, levels, lat_rows, lon_cols = (velocity.shape[i] for i in (1, 3, 4, 5))
    fields = mixing.shape[1]
    width = fields * levels
    count = innovations.shape[2]
    slots = 2
    assert (lat_rows, lon_cols, levels, count, owners, steps) == (SUBS, LANES, LANES, LANES, LANES, 3)
    f32 = functools.partial(jax.ShapeDtypeStruct, dtype=jnp.float32)
    stride = steps * slots * width // LANES + 1

    is_ocean = lax.axis_index("comp") == 1
    sea_float = sea_mask.astype(jnp.float32)
    mask = jnp.where(is_ocean, sea_float, jnp.ones_like(sea_float))
    global_rows = lax.axis_index("lat") * lat_rows + lax.broadcasted_iota(
        jnp.int32, (lat_rows, lon_cols), 0
    )
    opened = (global_rows < lat_count * lat_rows - 1).astype(jnp.float32)

    sent = pl.pallas_call(
        functools.partial(pack_kernel, slots),
        out_shape=f32((owners * stride, LANES)),
        compiler_params=params(),
        name="pack",
    )(innovations[0], obs_owner[0, :, :, 0], obs_cell[0])
    got = lax.all_to_all(
        sent.reshape(owners, 1, stride * LANES), ("lat", "lon"), split_axis=0, concat_axis=0, tiled=True
    ).reshape(owners * stride, LANES)

    speeds, diffuse = velocity[0], diffusion[0]
    last_col = jnp.minimum(speeds[:, 0, :, :, -1], 0.0) - diffuse[:, 0, :, :, -1]
    east_rims = lax.ppermute(
        jnp.swapaxes(last_col, 1, 2).reshape(steps * lat_rows, levels), "lon", ring("lon", 1, True)
    ).reshape(steps, lat_rows, levels)
    last_row = jnp.minimum(speeds[:, 1, :, -1, :], 0.0) - diffuse[:, 1, :, -1, :]
    north_rims = lax.ppermute(
        last_row.reshape(steps * levels, lon_cols), "lat", ring("lat", 1, False)
    ).reshape(steps, levels, lon_cols)

    edge_shapes = [
        f32((width * SUBS, LANES)),
        f32((width, LANES)),
        f32((width, LANES)),
        f32((fields * SUBS, LANES)),
        f32((fields * SUBS, LANES)),
    ]
    m, south, north, west, east = pl.pallas_call(
        functools.partial(first_kernel, steps - 1, slots, fields, levels),
        out_shape=edge_shapes,
        compiler_params=params(),
        name="first",
    )(got, mask)
    for step in reversed(range(steps)):
        low = lax.ppermute(
            m.reshape(fields, levels, SUBS, LANES)[:, -1].reshape(fields * SUBS, LANES), "comp", [(0, 1)]
        )
        from_south = lax.ppermute(north, "lat", ring("lat", 1, False))
        from_north = lax.ppermute(south, "lat", ring("lat", -1, False))
        from_west = lax.ppermute(east, "lon", ring("lon", 1, True))
        from_east = lax.ppermute(west, "lon", ring("lon", -1, True))
        last = step == 0
        operands = [
            mixing[0],
            air_sea,
            m,
            speeds[step],
            diffuse[step],
            opened,
            sea_float,
            mask,
            from_south,
            from_north,
            from_west,
            from_east,
            low,
            east_rims[step],
            north_rims[step],
        ]
        if not last:
            operands.append(
                pl.pallas_call(
                    functools.partial(forcing_kernel, step - 1, slots, width),
                    out_shape=f32((width * SUBS, LANES)),
                    compiler_params=params(),
                    cost_estimate=pl.CostEstimate(
                        flops=2 * 3 * width * 2 * LANES * SUBS * LANES,
                        bytes_accessed=4 * (owners * stride * LANES + width * SUBS * LANES),
                        transcendentals=0,
                    ),
                    name="forcing",
                )(got)
            )
        smem = pl.BlockSpec(memory_space=pltpu.SMEM)
        vmem = pl.BlockSpec(memory_space=pltpu.VMEM)
        result = pl.pallas_call(
            functools.partial(step_kernel, last, fields, levels),
            out_shape=edge_shapes[:1] if last else edge_shapes,
            in_specs=[smem, smem] + [vmem] * (len(operands) - 2),
            compiler_params=params(),
            name="step",
        )(*operands)
        if last:
            m = result[0]
        else:
            m, south, north, west, east = result
    return m.reshape(1, fields, levels, lat_rows, lon_cols)


def solution(mesh):
    return jax.shard_map(
        shards,
        mesh=mesh,
        in_specs=(
            P("comp", None, ("lat", "lon"), None),
            P("comp", None, ("lat", "lon"), None),
            P("comp", None, ("lat", "lon")),
            P("comp", None, None, None, "lat", "lon"),
            P("comp", None, None, None, "lat", "lon"),
            P("comp", None, None),
            P(),
            P("lat", "lon"),
        ),
        out_specs=P("comp", None, None, "lat", "lon"),
        check_vma=False,
    )
```

profile of v0, /device:TPU:8, one launch (start us, length us, event | category | flops | bytes accessed | tf_op | source)
XLA Modules:
  0.0 173.2 jit_solution(2672245353551394195)
XLA Ops:
  0.0 0.7 copy.41
  0.7 0.7 copy.42
  1.4 1.1 copy-done.5
  2.5 2.1 %pack.1 = f32[3200,128]{1,0:T(8,128)} custom-call(f32[3,128,512]{2,1,0:T(8,128)S(1)} %bitcast.52, s32[3,128]{1,0:T(4,128)S(1)} %bitcast.57, s32[3,128]{1,0:T(4,128)S(1)} %bitcast.56), custom_call_target="tpu_custom_call" | custom-call | tf_op jit(solution)/shard_map/pack/pallas_call | solution.py:243
  4.6 15.4 %all-to-all-start = ((f32[128,1,3200]{2,1,0:T(1,128)}), f32[128,1,3200]{2,1,0:T(1,128)S(1)}, u32[]{:S(2)}, u32[]{:S(2)}) async-start(f32[128,1,3200]{2,1,0:T(1,128)} %bitcast.2), calls=%async_computation | async-start | bytes 3276800 | tf_op jit(solution)/shard_map/all_to_all | solution.py:249
  20.1 3.9 %copy_bitcast_fusion = (f32[3,2,128,8,128]{4,2,3,1,0:T(8,128)S(1)}, f32[3,2,128,8,128]{4,2,3,1,0:T(8,128)S(1)}) fusion(f32[1,3,2,128,8,128]{5,4,3,2,1,0:T(8,128)} %param.12, f32[1,3,2,128,8,128]{5,4,3,2,1,0:T(8,128)} %param.11), kind=kLoop, calls=%fused_computation | loop fusion | bytes 12582912 | tf_op jit(solution)/shard_map/squeeze | solution.py:253
  24.1 3.4 %collective-permute-start.6 = (f32[384,128]{1,0:T(8,128)S(1)}, f32[384,128]{1,0:T(8,128)S(1)}, u32[]{:S(2)}, u32[]{:S(2)}) collective-permute-start(f32[384,128]{1,0:T(8,128)S(1)} %bitcast.58), channel_id=1, source_target_pairs={{0,8},{8,16},{16,24},{24,32},{32,40},{40,48},{48,56},{56,64},{64,7... | collective-permute-start | bytes 589832 | tf_op jit(solution)/shard_map/ppermute | solution.py:259
  27.5 1.4 fusion
  28.9 1.5 collective-permute-start.5
  30.5 5.2 %slice_bitcast_fusion = (f32[2,128,8,128]{3,2,1,0:T(8,128)S(1)}, f32[2,128,8,128]{3,2,1,0:T(8,128)}, f32[2,128,8,128]{3,2,1,0:T(8,128)}, f32[2,128,8,128]{3,2,1,...) fusion(f32[1,3,2,128,8,128]{5,4,3,2,1,0:T(8,128)} %param.12, f32[1,3,2,128,8,128]{5,4,3,2,1,0:T(8,128)} %param.11), kind=kLoop, calls=%fused_computation.5 | loop fusion | bytes 12582912 | tf_op jit(solution)/shard_map/squeeze | solution.py:290
  35.7 31.1 %collective-permute-done.5 = f32[24,128]{1,0:T(8,128)S(1)} collective-permute-done((f32[24,128]{1,0:T(8,128)S(1)}, f32[24,128]{1,0:T(8,128)S(1)}, u32[]{:S(2)}, u32[]{:S(2)}) %collective-permute-start.5) | collective-permute-done | bytes 12320 | tf_op jit(solution)/shard_map/ppermute | solution.py:255
  66.9 7.2 %first.1 = (f32[4096,128]{1,0:T(8,128)S(1)}, f32[512,128]{1,0:T(8,128)S(1)}, f32[512,128]{1,0:T(8,128)S(1)}, f32[32,128]{1,0:T(8,128)S(1)}, f32[32,128]{1,0:T(8,128)S(1)}) custom-call(f32[3200,128]{1,0:T(8,128)S(1)} %bitcast.46, f32[8,128]{1,0:T(8,128)S(1)} %broadcast_select_fusion.mask_ref), custom_call_target="tpu_custom_call" | custom-call | tf_op jit(solution)/shard_map/first/pallas_call | solution.py:270
  74.1 2.1 %collective-permute-start = (f32[512,128]{1,0:T(8,128)S(1)}, f32[512,128]{1,0:T(8,128)S(1)}, u32[]{:S(2)}, u32[]{:S(2)}) collective-permute-start(f32[512,128]{1,0:T(8,128)S(1)} %get-tuple-element.21), channel_id=1, source_target_pairs={{0,8},{8,16},{16,24},{24,32},{32,40},{40,48},{48,56},{56,64},{64,7... | collective-permute-start | bytes 786440 | tf_op jit(solution)/shard_map/ppermute | solution.py:280
  76.1 6.6 %collective-permute-start.1 = (f32[512,128]{1,0:T(8,128)S(1)}, f32[512,128]{1,0:T(8,128)S(1)}, u32[]{:S(2)}, u32[]{:S(2)}) collective-permute-start(f32[512,128]{1,0:T(8,128)S(1)} %get-tuple-element.22), channel_id=1, source_target_pairs={{8,0},{16,8},{24,16},{32,24},{40,32},{48,40},{56,48},{64,56},{72,6... | collective-permute-start | bytes 786440 | tf_op jit(solution)/shard_map/ppermute | solution.py:281
  82.8 1.3 collective-permute-start.4
  84.2 8.0 %collective-permute-start.3 = (f32[32,128]{1,0:T(8,128)S(1)}, f32[32,128]{1,0:T(8,128)S(1)}, u32[]{:S(2)}, u32[]{:S(2)}) collective-permute-start(f32[32,128]{1,0:T(8,128)S(1)} %get-tuple-element.24), channel_id=1, source_target_pairs={{0,7},{1,0},{2,1},{3,2},{4,3},{5,4},{6,5},{7,6},{8,15},{9,8},{10,9... | collective-permute-start | bytes 49160 | tf_op jit(solution)/shard_map/ppermute | solution.py:283
  92.2 1.2 forcing.2.rest_0_
  93.4 0.5 collective-permute-done.2.from_west_ref
  94.0 12.3 %step.3 = (f32[4096,128]{1,0:T(8,128)S(1)}, f32[512,128]{1,0:T(8,128)S(1)}, f32[512,128]{1,0:T(8,128)S(1)}, f32[32,128]{1,0:T(8,128)S(1)}, f32[32,128]{1,0:T(8,128)S(1)}) custom-call(f32[4,4]{1,0:T(4,128)S(1)} %bitcast.53, f32[4,4]{1,0:T(4,128)S(1)} %copy-done.7, f32[4096,128]{1,0:T(8,128)S(1)} %get-tuple-element.20.m_ref, f32[2,128,8,128]{3,2,1,0:T(8,128)S(1)} %copy-done.4, ...), custom_call_target="tpu_custom_call" | custom-call | tf_op jit(solution)/shard_map/step/pallas_call | solution.py:318
  106.3 2.1 %collective-permute-start.7 = (f32[512,128]{1,0:T(8,128)S(1)}, f32[512,128]{1,0:T(8,128)S(1)}, u32[]{:S(2)}, u32[]{:S(2)}) collective-permute-start(f32[512,128]{1,0:T(8,128)S(1)} %get-tuple-element.26), channel_id=1, source_target_pairs={{0,8},{8,16},{16,24},{24,32},{32,40},{40,48},{48,56},{56,64},{64,7... | collective-permute-start | bytes 786440 | tf_op jit(solution)/shard_map/ppermute | solution.py:280
  108.4 6.6 %collective-permute-start.8 = (f32[512,128]{1,0:T(8,128)S(1)}, f32[512,128]{1,0:T(8,128)S(1)}, u32[]{:S(2)}, u32[]{:S(2)}) collective-permute-start(f32[512,128]{1,0:T(8,128)S(1)} %get-tuple-element.27), channel_id=1, source_target_pairs={{8,0},{16,8},{24,16},{32,24},{40,32},{48,40},{56,48},{64,56},{72,6... | collective-permute-start | bytes 786440 | tf_op jit(solution)/shard_map/ppermute | solution.py:281
  115.0 1.3 collective-permute-start.11
  116.3 8.1 %collective-permute-start.10 = (f32[32,128]{1,0:T(8,128)S(1)}, f32[32,128]{1,0:T(8,128)S(1)}, u32[]{:S(2)}, u32[]{:S(2)}) collective-permute-start(f32[32,128]{1,0:T(8,128)S(1)} %get-tuple-element.29), channel_id=1, source_target_pairs={{0,7},{1,0},{2,1},{3,2},{4,3},{5,4},{6,5},{7,6},{8,15},{9,8},{10,9... | collective-permute-start | bytes 49160 | tf_op jit(solution)/shard_map/ppermute | solution.py:283
  124.4 1.2 forcing.3.rest_0_
  125.9 8.3 %collective-permute-done.9.from_west_ref = f32[32,128]{1,0:T(8,128)S(1)} collective-permute-done((f32[32,128]{1,0:T(8,128)S(1)}, f32[32,128]{1,0:T(8,128)S(1)}, u32[]{:S(2)}, u32[]{:S(2)}) %collective-permute-start.9) | collective-permute-done | bytes 16416 | tf_op jit(solution)/shard_map/ppermute | solution.py:282
  134.2 12.3 %step.4 = (f32[4096,128]{1,0:T(8,128)S(1)}, f32[512,128]{1,0:T(8,128)S(1)}, f32[512,128]{1,0:T(8,128)S(1)}, f32[32,128]{1,0:T(8,128)S(1)}, f32[32,128]{1,0:T(8,128)S(1)}) custom-call(f32[4,4]{1,0:T(4,128)S(1)} %bitcast.54, f32[4,4]{1,0:T(4,128)S(1)} %copy-done.7, f32[4096,128]{1,0:T(8,128)S(1)} %get-tuple-element.25.m_ref, f32[2,128,8,128]{3,2,1,0:T(8,128)S(1)} %copy-done.2, ...), custom_call_target="tpu_custom_call" | custom-call | tf_op jit(solution)/shard_map/step/pallas_call | solution.py:318
  146.5 1.9 %collective-permute-start.12 = (f32[512,128]{1,0:T(8,128)S(1)}, f32[512,128]{1,0:T(8,128)S(1)}, u32[]{:S(2)}, u32[]{:S(2)}) collective-permute-start(f32[512,128]{1,0:T(8,128)S(1)} %get-tuple-element.31), channel_id=1, source_target_pairs={{0,8},{8,16},{16,24},{24,32},{32,40},{40,48},{48,56},{56,64},{64,7... | collective-permute-start | bytes 786440 | tf_op jit(solution)/shard_map/ppermute | solution.py:280
  148.4 6.6 %collective-permute-start.13 = (f32[512,128]{1,0:T(8,128)S(1)}, f32[512,128]{1,0:T(8,128)S(1)}, u32[]{:S(2)}, u32[]{:S(2)}) collective-permute-start(f32[512,128]{1,0:T(8,128)S(1)} %get-tuple-element.32), channel_id=1, source_target_pairs={{8,0},{16,8},{24,16},{32,24},{40,32},{48,40},{56,48},{64,56},{72,6... | collective-permute-start | bytes 786440 | tf_op jit(solution)/shard_map/ppermute | solution.py:281
  155.1 1.3 collective-permute-start.16
  156.5 8.0 %collective-permute-start.15 = (f32[32,128]{1,0:T(8,128)S(1)}, f32[32,128]{1,0:T(8,128)S(1)}, u32[]{:S(2)}, u32[]{:S(2)}) collective-permute-start(f32[32,128]{1,0:T(8,128)S(1)} %get-tuple-element.34), channel_id=1, source_target_pairs={{0,7},{1,0},{2,1},{3,2},{4,3},{5,4},{6,5},{7,6},{8,15},{9,8},{10,9... | collective-permute-start | bytes 49160 | tf_op jit(solution)/shard_map/ppermute | solution.py:283
  164.5 1.7 collective-permute-done.14.from_west_ref
  166.2 6.9 %step.5 = f32[4096,128]{1,0:T(8,128)} custom-call(f32[4,4]{1,0:T(4,128)S(1)} %bitcast.55, f32[4,4]{1,0:T(4,128)S(1)} %copy-done.7, f32[4096,128]{1,0:T(8,128)S(1)} %get-tuple-element.30.m_ref, f32[2,128,8,128]{3,2,1,0:T(8,128)S(1)} %copy-done, f32[2,128,8,128]{3,2,1,0:T(8,128)S(1)} %get-tuple-element.35.dif_ref, f32[8,128]{1,0:T(8,128)S(1)} %iota.7.open_ref, ...), custom_call_target="tpu_custom_call" | custom-call | tf_op jit(solution)/shard_map/step/pallas_call | solution.py:318
  (44 shorter events, 0.6 us)
Async XLA Ops:
  1.4 1.1 copy-start.5
  4.6 62.2 %all-to-all-start = ((f32[128,1,3200]{2,1,0:T(1,128)}), f32[128,1,3200]{2,1,0:T(1,128)S(1)}, u32[]{:S(2)}, u32[]{:S(2)}) async-start(f32[128,1,3200]{2,1,0:T(1,128)} %bitcast.2), calls=%async_computation | async-start | bytes 3276800 | tf_op jit(solution)/shard_map/all_to_all | solution.py:249
  24.0 6.4 %copy-start.8 = (s32[8,128]{1,0:T(8,128)S(1)}, s32[8,128]{1,0:T(8,128)}, u32[]{:S(2)}) copy-start(s32[8,128]{1,0:T(8,128)} %param.15) | copy-start | bytes 12292
  24.1 42.7 %collective-permute-start.6 = (f32[384,128]{1,0:T(8,128)S(1)}, f32[384,128]{1,0:T(8,128)S(1)}, u32[]{:S(2)}, u32[]{:S(2)}) collective-permute-start(f32[384,128]{1,0:T(8,128)S(1)} %bitcast.58), channel_id=1, source_target_pairs={{0,8},{8,16},{16,24},{24,32},{32,40},{40,48},{48,56},{56,64},{64,7... | collective-permute-start | bytes 589832 | tf_op jit(solution)/shard_map/ppermute | solution.py:259
  28.9 37.9 %collective-permute-start.5 = (f32[24,128]{1,0:T(8,128)S(1)}, f32[24,128]{1,0:T(8,128)S(1)}, u32[]{:S(2)}, u32[]{:S(2)}) collective-permute-start(f32[24,128]{1,0:T(8,128)S(1)} %bitcast.59), channel_id=1, source_target_pairs={{0,1},{1,2},{2,3},{3,4},{4,5},{5,6},{6,7},{7,0},{8,9},{9,10},{10,1... | collective-permute-start | bytes 36872 | tf_op jit(solution)/shard_map/ppermute | solution.py:255
  74.0 20.0 %copy-start.3 = (f32[2,128,8,128]{3,2,1,0:T(8,128)S(1)}, f32[2,128,8,128]{3,2,1,0:T(8,128)}, u32[]{:S(2)}) copy-start(f32[2,128,8,128]{3,2,1,0:T(8,128)} %get-tuple-element.36.dif_ref) | copy-start | bytes 3145732
  74.0 20.0 %copy-start.4 = (f32[2,128,8,128]{3,2,1,0:T(8,128)S(1)}, f32[2,128,8,128]{3,2,1,0:T(8,128)}, u32[]{:S(2)}) copy-start(f32[2,128,8,128]{3,2,1,0:T(8,128)} %get-tuple-element.50.vel_ref) | copy-start | bytes 3145732
  74.0 19.9 %copy-start.6 = (f32[1,4,4]{2,1,0:T(4,128)S(1)}, f32[1,4,4]{2,1,0:T(4,128)}, u32[]{:S(2)}) copy-start(f32[1,4,4]{2,1,0:T(4,128)} %param.13) | copy-start | bytes 196
  74.0 19.9 %copy-start.7 = (f32[4,4]{1,0:T(4,128)S(1)}, f32[4,4]{1,0:T(4,128)}, u32[]{:S(2)}) copy-start(f32[4,4]{1,0:T(4,128)} %air_ref.5) | copy-start | bytes 196
  74.1 19.8 %collective-permute-start = (f32[512,128]{1,0:T(8,128)S(1)}, f32[512,128]{1,0:T(8,128)S(1)}, u32[]{:S(2)}, u32[]{:S(2)}) collective-permute-start(f32[512,128]{1,0:T(8,128)S(1)} %get-tuple-element.21), channel_id=1, source_target_pairs={{0,8},{8,16},{16,24},{24,32},{32,40},{40,48},{48,56},{56,64},{64,7... | collective-permute-start | bytes 786440 | tf_op jit(solution)/shard_map/ppermute | solution.py:280
  76.1 17.8 %collective-permute-start.1 = (f32[512,128]{1,0:T(8,128)S(1)}, f32[512,128]{1,0:T(8,128)S(1)}, u32[]{:S(2)}, u32[]{:S(2)}) collective-permute-start(f32[512,128]{1,0:T(8,128)S(1)} %get-tuple-element.22), channel_id=1, source_target_pairs={{8,0},{16,8},{24,16},{32,24},{40,32},{48,40},{56,48},{64,56},{72,6... | collective-permute-start | bytes 786440 | tf_op jit(solution)/shard_map/ppermute | solution.py:281
  82.8 10.6 %collective-permute-start.4 = (f32[32,128]{1,0:T(8,128)S(1)}, f32[32,128]{1,0:T(8,128)S(1)}, u32[]{:S(2)}, u32[]{:S(2)}) collective-permute-start(f32[32,128]{1,0:T(8,128)S(1)} %slice_bitcast_fusion.8), channel_id=1, source_target_pairs={{0,128},{1,129},{2,130},{3,131},{4,132},{5,133},{6,134},{7,135},{8... | collective-permute-start | bytes 49160 | tf_op jit(solution)/shard_map/ppermute | solution.py:277
  84.1 9.8 %collective-permute-start.2 = (f32[32,128]{1,0:T(8,128)S(1)}, f32[32,128]{1,0:T(8,128)S(1)}, u32[]{:S(2)}, u32[]{:S(2)}) collective-permute-start(f32[32,128]{1,0:T(8,128)S(1)} %get-tuple-element.23), channel_id=1, source_target_pairs={{0,1},{1,2},{2,3},{3,4},{4,5},{5,6},{6,7},{7,0},{8,9},{9,10},{10,1... | collective-permute-start | bytes 49160 | tf_op jit(solution)/shard_map/ppermute | solution.py:282
  84.2 9.7 %collective-permute-start.3 = (f32[32,128]{1,0:T(8,128)S(1)}, f32[32,128]{1,0:T(8,128)S(1)}, u32[]{:S(2)}, u32[]{:S(2)}) collective-permute-start(f32[32,128]{1,0:T(8,128)S(1)} %get-tuple-element.24), channel_id=1, source_target_pairs={{0,7},{1,0},{2,1},{3,2},{4,3},{5,4},{6,5},{7,6},{8,15},{9,8},{10,9... | collective-permute-start | bytes 49160 | tf_op jit(solution)/shard_map/ppermute | solution.py:283
  106.3 27.9 %copy-start.1 = (f32[2,128,8,128]{3,2,1,0:T(8,128)S(1)}, f32[2,128,8,128]{3,2,1,0:T(8,128)}, u32[]{:S(2)}) copy-start(f32[2,128,8,128]{3,2,1,0:T(8,128)} %get-tuple-element.37.dif_ref) | copy-start | bytes 3145732
  106.3 27.9 %copy-start.2 = (f32[2,128,8,128]{3,2,1,0:T(8,128)S(1)}, f32[2,128,8,128]{3,2,1,0:T(8,128)}, u32[]{:S(2)}) copy-start(f32[2,128,8,128]{3,2,1,0:T(8,128)} %get-tuple-element.49.vel_ref) | copy-start | bytes 3145732
  106.3 27.9 %collective-permute-start.7 = (f32[512,128]{1,0:T(8,128)S(1)}, f32[512,128]{1,0:T(8,128)S(1)}, u32[]{:S(2)}, u32[]{:S(2)}) collective-permute-start(f32[512,128]{1,0:T(8,128)S(1)} %get-tuple-element.26), channel_id=1, source_target_pairs={{0,8},{8,16},{16,24},{24,32},{32,40},{40,48},{48,56},{56,64},{64,7... | collective-permute-start | bytes 786440 | tf_op jit(solution)/shard_map/ppermute | solution.py:280
  108.4 25.8 %collective-permute-start.8 = (f32[512,128]{1,0:T(8,128)S(1)}, f32[512,128]{1,0:T(8,128)S(1)}, u32[]{:S(2)}, u32[]{:S(2)}) collective-permute-start(f32[512,128]{1,0:T(8,128)S(1)} %get-tuple-element.27), channel_id=1, source_target_pairs={{8,0},{16,8},{24,16},{32,24},{40,32},{48,40},{56,48},{64,56},{72,6... | collective-permute-start | bytes 786440 | tf_op jit(solution)/shard_map/ppermute | solution.py:281
  115.0 10.6 %collective-permute-start.11 = (f32[32,128]{1,0:T(8,128)S(1)}, f32[32,128]{1,0:T(8,128)S(1)}, u32[]{:S(2)}, u32[]{:S(2)}) collective-permute-start(f32[32,128]{1,0:T(8,128)S(1)} %slice_bitcast_fusion.7), channel_id=1, source_target_pairs={{0,128},{1,129},{2,130},{3,131},{4,132},{5,133},{6,134},{7,135},{8... | collective-permute-start | bytes 49160 | tf_op jit(solution)/shard_map/ppermute | solution.py:277
  116.3 9.6 %collective-permute-start.10 = (f32[32,128]{1,0:T(8,128)S(1)}, f32[32,128]{1,0:T(8,128)S(1)}, u32[]{:S(2)}, u32[]{:S(2)}) collective-permute-start(f32[32,128]{1,0:T(8,128)S(1)} %get-tuple-element.29), channel_id=1, source_target_pairs={{0,7},{1,0},{2,1},{3,2},{4,3},{5,4},{6,5},{7,6},{8,15},{9,8},{10,9... | collective-permute-start | bytes 49160 | tf_op jit(solution)/shard_map/ppermute | solution.py:283
  124.4 9.8 %collective-permute-start.9 = (f32[32,128]{1,0:T(8,128)S(1)}, f32[32,128]{1,0:T(8,128)S(1)}, u32[]{:S(2)}, u32[]{:S(2)}) collective-permute-start(f32[32,128]{1,0:T(8,128)S(1)} %get-tuple-element.28), channel_id=1, source_target_pairs={{0,1},{1,2},{2,3},{3,4},{4,5},{5,6},{6,7},{7,0},{8,9},{9,10},{10,1... | collective-permute-start | bytes 49160 | tf_op jit(solution)/shard_map/ppermute | solution.py:282
  134.2 32.0 %copy-start = (f32[2,128,8,128]{3,2,1,0:T(8,128)S(1)}, f32[2,128,8,128]{3,2,1,0:T(8,128)}, u32[]{:S(2)}) copy-start(f32[2,128,8,128]{3,2,1,0:T(8,128)} %get-tuple-element.51.vel_ref) | copy-start | bytes 3145732
  146.5 19.7 %collective-permute-start.12 = (f32[512,128]{1,0:T(8,128)S(1)}, f32[512,128]{1,0:T(8,128)S(1)}, u32[]{:S(2)}, u32[]{:S(2)}) collective-permute-start(f32[512,128]{1,0:T(8,128)S(1)} %get-tuple-element.31), channel_id=1, source_target_pairs={{0,8},{8,16},{16,24},{24,32},{32,40},{40,48},{48,56},{56,64},{64,7... | collective-permute-start | bytes 786440 | tf_op jit(solution)/shard_map/ppermute | solution.py:280
  148.4 17.8 %collective-permute-start.13 = (f32[512,128]{1,0:T(8,128)S(1)}, f32[512,128]{1,0:T(8,128)S(1)}, u32[]{:S(2)}, u32[]{:S(2)}) collective-permute-start(f32[512,128]{1,0:T(8,128)S(1)} %get-tuple-element.32), channel_id=1, source_target_pairs={{8,0},{16,8},{24,16},{32,24},{40,32},{48,40},{56,48},{64,56},{72,6... | collective-permute-start | bytes 786440 | tf_op jit(solution)/shard_map/ppermute | solution.py:281
  155.1 9.4 %collective-permute-start.16 = (f32[32,128]{1,0:T(8,128)S(1)}, f32[32,128]{1,0:T(8,128)S(1)}, u32[]{:S(2)}, u32[]{:S(2)}) collective-permute-start(f32[32,128]{1,0:T(8,128)S(1)} %slice_bitcast_fusion.6), channel_id=1, source_target_pairs={{0,128},{1,129},{2,130},{3,131},{4,132},{5,133},{6,134},{7,135},{8... | collective-permute-start | bytes 49160 | tf_op jit(solution)/shard_map/ppermute | solution.py:277
  156.4 9.8 %collective-permute-start.14 = (f32[32,128]{1,0:T(8,128)S(1)}, f32[32,128]{1,0:T(8,128)S(1)}, u32[]{:S(2)}, u32[]{:S(2)}) collective-permute-start(f32[32,128]{1,0:T(8,128)S(1)} %get-tuple-element.33), channel_id=1, source_target_pairs={{0,1},{1,2},{2,3},{3,4},{4,5},{5,6},{6,7},{7,0},{8,9},{9,10},{10,1... | collective-permute-start | bytes 49160 | tf_op jit(solution)/shard_map/ppermute | solution.py:282
  156.5 9.7 %collective-permute-start.15 = (f32[32,128]{1,0:T(8,128)S(1)}, f32[32,128]{1,0:T(8,128)S(1)}, u32[]{:S(2)}, u32[]{:S(2)}) collective-permute-start(f32[32,128]{1,0:T(8,128)S(1)} %get-tuple-element.34), channel_id=1, source_target_pairs={{0,7},{1,0},{2,1},{3,2},{4,3},{5,4},{6,5},{7,6},{8,15},{9,8},{10,9... | collective-permute-start | bytes 49160 | tf_op jit(solution)/shard_map/ppermute | solution.py:283
where the time goes:
time: 174 us; the launch traced here: 173 us
  starting transfers between devices  74.5 us (43%)
  Pallas kernels  43.2 us (25%)
  waiting for transfers between devices  42 us (24%)
  local copies, waits for them, and re-layouts  11.7 us (7%)
    pallas_call x3, Pallas kernels, shards(): pl.pallas_call(functools.partial(step_kernel, last, fields, levels), out_...  31.5 us
    ppermute x1, waiting for transfers between devices, shards(): lax.ppermute(jnp.swapaxes(last_col, 1, 2).reshape(steps * lat_rows, level...  31.1 us
    ppermute x3, starting transfers between devices, shards(): from_east = lax.ppermute(west, 'lon', ring('lon', -1, True))  24.2 us
    ppermute x3, starting transfers between devices, shards(): from_north = lax.ppermute(south, 'lat', ring('lat', -1, False))  19.9 us
    all_to_all x1, starting transfers between devices, shards(): lax.all_to_all(sent.reshape(owners, 1, stride * LANES), ('lat', 'lon'), s...  15.4 us
    ppermute x3, waiting for transfers between devices, shards(): from_west = lax.ppermute(east, 'lon', ring('lon', 1, True))  10.6 us
    pallas_call x1, Pallas kernels, shards(): pl.pallas_call(functools.partial(first_kernel, steps - 1, slots, fields,...  7.16 us
    ppermute x3, starting transfers between devices, shards(): from_south = lax.ppermute(north, 'lat', ring('lat', 1, False))  6.02 us
  transfers between devices with their start and end apart: 18, of which 5 were waited for; matrix products, arithmetic and copies ran while one was open for 6% of the time, Pallas kernels for 1%

commit v1 on v0

v1 whole, which is shorter than its diff:
```python
import functools

import jax
import jax.numpy as jnp
from jax import lax
from jax.experimental import pallas as pl
from jax.experimental.pallas import tpu as pltpu
from jax.sharding import PartitionSpec as P

LANES = 128
SUBS = 8
VMEM_LIMIT = 40 * 1024 * 1024


def split3(x):
    hi = x.astype(jnp.bfloat16)
    rest = x - hi.astype(jnp.float32)
    mid = rest.astype(jnp.bfloat16)
    low = (rest - mid.astype(jnp.float32)).astype(jnp.bfloat16)
    return [hi, mid, low]


def pack_kernel(slots, rows_ref, owner_ref, cell_ref, out_ref):
    steps, count, width = rows_ref.shape
    owners = count
    parts = width // LANES
    stride = out_ref.shape[0] // owners
    dest = lax.broadcasted_iota(jnp.int32, (owners, count), 0)
    lane = lax.broadcasted_iota(jnp.int32, (owners, count), 1)
    before = (dest < lane).astype(jnp.bfloat16)
    cells = jnp.zeros((owners, LANES), jnp.float32)
    for step in range(steps):
        hits = owner_ref[step : step + 1, :] == dest
        hits_f = hits.astype(jnp.float32)
        prior = jnp.dot(hits_f.astype(jnp.bfloat16), before, preferred_element_type=jnp.float32)
        terms = jnp.concatenate(split3(rows_ref[step]), axis=0)
        marks = (cell_ref[step : step + 1, :] + 1).astype(jnp.float32)
        for k in range(slots):
            slot = step * slots + k
            pick = jnp.where(prior == float(k), hits_f, 0.0)
            pick_b = pick.astype(jnp.bfloat16)
            out = jnp.dot(
                jnp.concatenate([pick_b] * 3, axis=1), terms, preferred_element_type=jnp.float32
            )
            for part in range(parts):
                out_ref[pl.ds(slot * parts + part, owners, stride=stride), :] = out[
                    :, part * LANES : (part + 1) * LANES
                ]
            mark = jnp.sum(pick * marks, axis=1, keepdims=True)
            cells = jnp.where(lane == slot, mark, cells)
    out_ref[pl.ds(stride - 1, owners, stride=stride), :] = cells


def spread_rows(step, slots, got_ref, width):
    parts = width // LANES
    stride = parts * slots * 3 + 1
    sources = got_ref.shape[0] // stride
    marks = got_ref[pl.ds(stride - 1, sources, stride=stride), :]
    where_to = lax.broadcasted_iota(jnp.int32, (sources, SUBS * LANES), 1)
    terms, onehots = [], []
    for k in range(slots):
        slot = step * slots + k
        cols = []
        for part in range(parts):
            block = got_ref[pl.ds(slot * parts + part, sources, stride=stride), :]
            cols.append(block.T)
        turned = jnp.concatenate(cols, axis=0)
        terms += split3(turned)
        cell = marks[:, slot : slot + 1].astype(jnp.int32) - 1
        onehot = (cell == where_to).astype(jnp.float32).astype(jnp.bfloat16)
        onehots += [onehot] * 3
    return jnp.dot(
        jnp.concatenate(terms, axis=1),
        jnp.concatenate(onehots, axis=0),
        preferred_element_type=jnp.float32,
    )


def columns_start(fields):
    zero = jnp.zeros((SUBS, LANES), jnp.float32)
    return [zero] * (2 * fields)


def columns_insert(cols, f, y, plane):
    lane = lax.broadcasted_iota(jnp.int32, (SUBS, LANES), 1)
    turned = plane if y == 0 else pltpu.roll(plane, y, 1)
    here = (lane == y) | (lane == (y - 1) % LANES)
    at = 2 * f + y % 2
    cols[at] = jnp.where(here, turned, cols[at])


def columns_turn(cols):
    return [pltpu.roll(c, LANES - SUBS, 1) for c in cols]


def columns_store(cols, west_ref, east_ref, fields):
    even = lax.broadcasted_iota(jnp.int32, (SUBS, LANES), 1) % 2 == 0
    for f in range(fields):
        a, b = cols[2 * f], cols[2 * f + 1]
        west_ref[f * SUBS : (f + 1) * SUBS, :] = jnp.where(even, a, b)
        east_ref[f * SUBS : (f + 1) * SUBS, :] = jnp.where(even, b, a)


def columns_load(from_west_ref, from_east_ref, fields):
    even = lax.broadcasted_iota(jnp.int32, (SUBS, LANES), 1) % 2 == 0
    cols = []
    for f in range(fields):
        west = pltpu.roll(from_west_ref[f * SUBS : (f + 1) * SUBS, :], 1, 1)
        east = pltpu.roll(from_east_ref[f * SUBS : (f + 1) * SUBS, :], LANES - 1, 1)
        cols += [jnp.where(even, west, east), jnp.where(even, east, west)]
    return cols


def columns_take(cols, f, y):
    col = cols[2 * f + y % 2]
    return col if y == 0 else pltpu.roll(col, LANES - y, 1)


def rows_of(base, group):
    if isinstance(group, int):
        return pl.ds(base + group * SUBS, SUBS)
    return pl.ds(pl.multiple_of(base + group * SUBS, SUBS), SUBS)


def first_kernel(
    step, slots, fields, levels, got_ref, mask_ref, m_ref, south_ref, north_ref, west_ref, east_ref, low_ref
):
    width = fields * levels
    out = spread_rows(step, slots, got_ref, width)
    for y in range(SUBS):
        m_ref[y * width : (y + 1) * width, :] = out[:, y * LANES : (y + 1) * LANES] * mask_ref[y : y + 1, :]
    south_ref[...] = m_ref[:width, :]
    north_ref[...] = m_ref[(SUBS - 1) * width :, :]

    def body(group, cols):
        cols = list(cols)
        for f in range(fields):
            for y in range(SUBS):
                columns_insert(cols, f, y, m_ref[rows_of(y * width + f * levels, group), :])
        return tuple(columns_turn(cols))

    cols = lax.fori_loop(0, levels // SUBS, body, tuple(columns_start(fields)))
    columns_store(cols, west_ref, east_ref, fields)
    for f in range(fields):
        low_ref[f * SUBS : (f + 1) * SUBS, :] = m_ref[pl.ds(f * levels + levels - 1, SUBS, stride=width), :]


def forcing_kernel(step, slots, width, got_ref, f_ref):
    out = spread_rows(step, slots, got_ref, width)
    for y in range(SUBS):
        f_ref[y * width : (y + 1) * width, :] = out[:, y * LANES : (y + 1) * LANES]


def rim_kernel(vel_ref, dif_ref, rim_ref, vel_row, dif_row, sems):
    copies = [
        pltpu.make_async_copy(src.at[:, 1, :, SUBS - 1, :], dst, sems.at[i])
        for i, (src, dst) in enumerate(((vel_ref, vel_row), (dif_ref, dif_row)))
    ]
    for copy in copies:
        copy.start()
    for copy in copies:
        copy.wait()
    steps, levels, lanes = vel_row.shape
    rim_ref[...] = (jnp.minimum(vel_row[...], 0.0) - dif_row[...]).reshape(steps * levels, lanes)


def coefficient_kernel(steps, levels, vel_ref, dif_ref, open_ref, *outs):
    tables, rim_ref = outs[:-1], outs[-1]
    lane = lax.broadcasted_iota(jnp.int32, (SUBS, LANES), 1)
    for step in range(steps):
        up_e_ref, down_e_ref, up_n_ref, down_n_ref = tables[4 * step : 4 * step + 4]
        east, north = 2 * step * levels * SUBS, (2 * step + 1) * levels * SUBS
        for y in range(SUBS):
            rows = slice(y * levels, (y + 1) * levels)
            w = vel_ref[pl.ds(east + y, levels, stride=SUBS), :]
            k = dif_ref[pl.ds(east + y, levels, stride=SUBS), :]
            up_e_ref[rows, :] = jnp.maximum(w, 0.0) + k
            down_e_ref[rows, :] = jnp.minimum(w, 0.0) - k
            w = vel_ref[pl.ds(north + y, levels, stride=SUBS), :]
            k = dif_ref[pl.ds(north + y, levels, stride=SUBS), :]
            up = jnp.maximum(w, 0.0) + k
            up_n_ref[rows, :] = up * open_ref[...] if y == SUBS - 1 else up
            down_n_ref[rows, :] = jnp.minimum(w, 0.0) - k

        def body(group, rim, down_e_ref=down_e_ref):
            for y in range(SUBS):
                plane = down_e_ref[rows_of(y * levels, group), :]
                rim = jnp.where(lane == y, pltpu.roll(plane, y + 1, 1), rim)
            return pltpu.roll(rim, LANES - SUBS, 1)

        rim_ref[step * SUBS : (step + 1) * SUBS, :] = lax.fori_loop(
            0, levels // SUBS, body, jnp.zeros((SUBS, LANES), jnp.float32)
        )


def shift_kernel(steps, levels, rim_ref, *refs):
    lane = lax.broadcasted_iota(jnp.int32, (SUBS, LANES), 1)
    for step in range(steps):
        down_e_ref, down_w_ref = refs[step], refs[steps + step]

        def body(group, rim, down_e_ref=down_e_ref, down_w_ref=down_w_ref):
            for y in range(SUBS):
                plane = down_e_ref[rows_of(y * levels, group), :]
                col = rim if y == 0 else pltpu.roll(rim, LANES - y, 1)
                down_w_ref[rows_of(y * levels, group), :] = jnp.where(lane == 0, col, pltpu.roll(plane, 1, 1))
            return pltpu.roll(rim, LANES - SUBS, 1)

        lax.fori_loop(0, levels // SUBS, body, rim_ref[step * SUBS : (step + 1) * SUBS, :])


def step_kernel(
    last,
    fields,
    levels,
    mix_ref,
    air_ref,
    m_ref,
    up_e_ref,
    down_w_ref,
    up_n_ref,
    down_n_ref,
    north_rim_ref,
    sea_ref,
    mask_ref,
    from_south_ref,
    from_north_ref,
    from_west_ref,
    from_east_ref,
    from_low_ref,
    *rest,
):
    if last:
        (out_ref,) = rest
    else:
        f_ref, out_ref, south_ref, north_ref, west_ref, east_ref, low_ref = rest
    width = fields * levels
    lane = lax.broadcasted_iota(jnp.int32, (SUBS, LANES), 1)
    sub = lax.broadcasted_iota(jnp.int32, (SUBS, LANES), 0)
    at_west, at_east = lane == 0, lane == LANES - 1
    mix = [[mix_ref[f, g] for g in range(fields)] for f in range(fields)]
    sea = sea_ref[...]
    coupled = []
    for g in range(fields):
        total = jnp.zeros((SUBS, LANES), jnp.float32)
        for f in range(fields):
            total = total + air_ref[f, g] * from_low_ref[f * SUBS : (f + 1) * SUBS, :]
        coupled.append(sea * total)

    def group_step(group, halos, cols):
        cols = list(cols)
        for y in range(SUBS):
            up_e = up_e_ref[rows_of(y * levels, group), :]
            down_w = down_w_ref[rows_of(y * levels, group), :]
            up_n = up_n_ref[rows_of(y * levels, group), :]
            if y == 0:
                down_s = north_rim_ref[rows_of(0, group), :]
            else:
                down_s = down_n_ref[rows_of((y - 1) * levels, group), :]
            planes = [m_ref[rows_of(y * width + f * levels, group), :] for f in range(fields)]
            for g in range(fields):
                m = planes[g]
                if y == SUBS - 1:
                    north = from_north_ref[rows_of(g * levels, group), :]
                else:
                    north = m_ref[rows_of((y + 1) * width + g * levels, group), :]
                if y == 0:
                    south = from_south_ref[rows_of(g * levels, group), :]
                else:
                    south = m_ref[rows_of((y - 1) * width + g * levels, group), :]
                halo = columns_take(halos, g, y)
                east = jnp.where(at_east, halo, pltpu.roll(m, LANES - 1, 1))
                west = jnp.where(at_west, halo, pltpu.roll(m, 1, 1))
                result = m
                for f in range(fields):
                    result = result + mix[f][g] * planes[f]
                result = result + (up_e * (east - m) + down_w * (m - west))
                result = result + (up_n * (north - m) + down_s * (m - south))
                if isinstance(group, int):
                    result = result + jnp.where(sub == 0, coupled[g][y : y + 1, :], 0.0)
                if last:
                    at = g * levels * SUBS + y
                    if isinstance(group, int):
                        out_ref[pl.ds(at + group * SUBS * SUBS, SUBS, stride=SUBS), :] = result
                    else:
                        out_ref[pl.ds(at + group * (SUBS * SUBS), SUBS, stride=SUBS), :] = result
                    continue
                rows = rows_of(y * width + g * levels, group)
                result = (result + f_ref[rows, :]) * mask_ref[y : y + 1, :]
                out_ref[rows, :] = result
                if y == 0:
                    south_ref[rows_of(g * levels, group), :] = result
                if y == SUBS - 1:
                    north_ref[rows_of(g * levels, group), :] = result
                columns_insert(cols, g, y, result)
        if not last:
            cols = columns_turn(cols)
        return columns_turn(halos), cols

    halos, cols = group_step(0, columns_load(from_west_ref, from_east_ref, fields), [] if last else columns_start(fields))

    def body(group, carry):
        halos, cols = group_step(group, list(carry[0]), list(carry[1]))
        return tuple(halos), tuple(cols)

    halos, cols = lax.fori_loop(1, levels // SUBS, body, (tuple(halos), tuple(cols)))
    if not last:
        columns_store(cols, west_ref, east_ref, fields)
        for f in range(fields):
            low_ref[f * SUBS : (f + 1) * SUBS, :] = out_ref[pl.ds(f * levels + levels - 1, SUBS, stride=width), :]


def params():
    return pltpu.CompilerParams(vmem_limit_bytes=VMEM_LIMIT)


def ring(axis, by, closed):
    count = lax.axis_size(axis)
    return [(i, (i + by) % count) for i in range(count) if closed or 0 <= i + by < count]


def shards(innovations, obs_owner, obs_cell, velocity, diffusion, mixing, air_sea, sea_mask):
    lat_count = lax.axis_size("lat")
    lon_count = lax.axis_size("lon")
    owners = lat_count * lon_count
    steps, levels, lat_rows, lon_cols = (velocity.shape[i] for i in (1, 3, 4, 5))
    fields = mixing.shape[1]
    width = fields * levels
    count = innovations.shape[2]
    slots = 2
    assert (lat_rows, lon_cols, levels, count, owners, steps) == (SUBS, LANES, LANES, LANES, LANES, 3)
    f32 = functools.partial(jax.ShapeDtypeStruct, dtype=jnp.float32)
    stride = steps * slots * width // LANES + 1

    is_ocean = lax.axis_index("comp") == 1
    sea_float = sea_mask.astype(jnp.float32)
    mask = jnp.where(is_ocean, sea_float, jnp.ones_like(sea_float))
    opened = jnp.full((1, lon_cols), lax.axis_index("lat") < lat_count - 1, jnp.float32)
    smem = pl.BlockSpec(memory_space=pltpu.SMEM)
    vmem = pl.BlockSpec(memory_space=pltpu.VMEM)
    anywhere = pl.BlockSpec(memory_space=pl.ANY)
    speeds, diffuse = velocity[0], diffusion[0]

    north_rims = pl.pallas_call(
        rim_kernel,
        out_shape=f32((steps * levels, LANES)),
        in_specs=[anywhere] * 2,
        scratch_shapes=[pltpu.VMEM((steps, levels, LANES), jnp.float32)] * 2 + [pltpu.SemaphoreType.DMA((2,))],
        compiler_params=params(),
        name="rim",
    )(speeds, diffuse)
    north_rims = lax.ppermute(north_rims, "lat", ring("lat", 1, False)).reshape(steps, levels, LANES)

    sent = pl.pallas_call(
        functools.partial(pack_kernel, slots),
        out_shape=f32((owners * stride, LANES)),
        compiler_params=params(),
        name="pack",
    )(innovations[0], obs_owner[0, :, :, 0], obs_cell[0])
    got = lax.all_to_all(
        sent.reshape(owners, 1, stride * LANES), ("lat", "lon"), split_axis=0, concat_axis=0, tiled=True
    ).reshape(owners * stride, LANES)

    table = f32((levels * SUBS, LANES))
    *tables, east_rims = pl.pallas_call(
        functools.partial(coefficient_kernel, steps, levels),
        out_shape=[table] * (4 * steps) + [f32((steps * SUBS, LANES))],
        compiler_params=params(),
        cost_estimate=pl.CostEstimate(flops=1 << 22, bytes_accessed=1 << 23, transcendentals=0),
        name="coefficients",
    )(
        speeds.reshape(steps * 2 * levels * SUBS, LANES),
        diffuse.reshape(steps * 2 * levels * SUBS, LANES),
        opened,
    )
    east_rims = lax.ppermute(east_rims, "lon", ring("lon", 1, True))
    downs_w = pl.pallas_call(
        functools.partial(shift_kernel, steps, levels),
        out_shape=[table] * steps,
        compiler_params=params(),
        name="shift",
    )(east_rims, *tables[1::4])

    edge_shapes = [
        f32((width * SUBS, LANES)),
        f32((width, LANES)),
        f32((width, LANES)),
        f32((fields * SUBS, LANES)),
        f32((fields * SUBS, LANES)),
        f32((fields * SUBS, LANES)),
    ]
    m, south, north, west, east, low = pl.pallas_call(
        functools.partial(first_kernel, steps - 1, slots, fields, levels),
        out_shape=edge_shapes,
        compiler_params=params(),
        name="first",
    )(got, mask)
    for step in reversed(range(steps)):
        from_south = lax.ppermute(north, "lat", ring("lat", 1, False))
        from_north = lax.ppermute(south, "lat", ring("lat", -1, False))
        from_west = lax.ppermute(east, "lon", ring("lon", 1, True))
        from_east = lax.ppermute(west, "lon", ring("lon", -1, True))
        from_low = lax.ppermute(low, "comp", [(0, 1)])
        last = step == 0
        operands = [
            mixing[0],
            air_sea,
            m,
            tables[4 * step],
            downs_w[step],
            tables[4 * step + 2],
            tables[4 * step + 3],
            north_rims[step],
            sea_float,
            mask,
            from_south,
            from_north,
            from_west,
            from_east,
            from_low,
        ]
        if not last:
            operands.append(
                pl.pallas_call(
                    functools.partial(forcing_kernel, step - 1, slots, width),
                    out_shape=f32((width * SUBS, LANES)),
                    compiler_params=params(),
                    cost_estimate=pl.CostEstimate(
                        flops=2 * 3 * width * 2 * LANES * SUBS * LANES,
                        bytes_accessed=4 * (owners * stride * LANES + width * SUBS * LANES),
                        transcendentals=0,
                    ),
                    name="forcing",
                )(got)
            )
        result = pl.pallas_call(
            functools.partial(step_kernel, last, fields, levels),
            out_shape=edge_shapes[:1] if last else edge_shapes,
            in_specs=[smem, smem] + [vmem] * (len(operands) - 2),
            compiler_params=params(),
            name="step",
        )(*operands)
        if last:
            m = result[0]
        else:
            m, south, north, west, east, low = result
    return m.reshape(1, fields, levels, lat_rows, lon_cols)


def solution(mesh):
    return jax.shard_map(
        shards,
        mesh=mesh,
        in_specs=(
            P("comp", None, ("lat", "lon"), None),
            P("comp", None, ("lat", "lon"), None),
            P("comp", None, ("lat", "lon")),
            P("comp", None, None, None, "lat", "lon"),
            P("comp", None, None, None, "lat", "lon"),
            P("comp", None, None),
            P(),
            P("lat", "lon"),
        ),
        out_specs=P("comp", None, None, "lat", "lon"),
        check_vma=False,
    )
```

time: 174 us -> 162 us (0.931)
  waiting for transfers between devices: 42 us -> 34.8 us
  Pallas kernels: 43.2 us -> 37.7 us
  local copies, waits for them, and re-layouts: 11.7 us -> 13.6 us
    pallas_call x3, Pallas kernels: 31.5 us -> 17 us  [shards(): pl.pallas_call(functools.partial(step_kernel, last, fields, levels), out_...]
    pallas_call x0 -> x3, Pallas kernels: none -> 12.6 us  [the longest x1 8.28 us: shards(): pl.pallas_call(functools.partial(coefficient_kernel, steps, levels), out_...]
    unnamed x20 -> x62, local copies, waits for them, and re-layouts: 2.53 us -> 12.7 us
    squeeze x2 -> x0, local copies, waits for them, and re-layouts: 9.12 us -> none  [the longest x1 5.18 us: shards(): diffuse[step]]
    ppermute x5, waiting for transfers between devices: 31.2 us -> 25.7 us  [the longest x1 25.3 us: shards(): east_rims = lax.ppermute(east_rims, 'lon', ring('lon', 1, True))]
    pallas_call x1, Pallas kernels: 7.16 us -> 3.79 us  [shards(): pl.pallas_call(functools.partial(first_kernel, steps - 1, slots, fields,...]
  transfers between devices with their start and end apart: 18 -> 18, of which waited for: 5 -> 4; matrix products, arithmetic and copies ran while one was open for 6% -> 1% of each run, Pallas kernels for 1% -> 12%
where the time goes in v1:
time: 162 us; the launch traced here: 161 us
  starting transfers between devices  74 us (46%)
  Pallas kernels  37.7 us (23%)
  waiting for transfers between devices  34.8 us (21%)
  local copies, waits for them, and re-layouts  13.6 us (8%)
    ppermute x1, waiting for transfers between devices, shards(): east_rims = lax.ppermute(east_rims, 'lon', ring('lon', 1, True))  25.3 us
    ppermute x3, starting transfers between devices, shards(): from_east = lax.ppermute(west, 'lon', ring('lon', -1, True))  23.5 us
    ppermute x3, starting transfers between devices, shards(): from_north = lax.ppermute(south, 'lat', ring('lat', -1, False))  18.7 us
    pallas_call x3, Pallas kernels, shards(): pl.pallas_call(functools.partial(step_kernel, last, fields, levels), out_...  17 us
    all_to_all x1, starting transfers between devices, shards(): lax.all_to_all(sent.reshape(owners, 1, stride * LANES), ('lat', 'lon'), s...  15.4 us
    unnamed x62, local copies, waits for them, and re-layouts  12.7 us
    ppermute x3, waiting for transfers between devices, shards(): from_west = lax.ppermute(east, 'lon', ring('lon', 1, True))  9.05 us
    pallas_call x1, Pallas kernels, shards(): pl.pallas_call(functools.partial(coefficient_kernel, steps, levels), out_...  8.28 us
  transfers between devices with their start and end apart: 18, of which 4 were waited for; matrix products, arithmetic and copies ran while one was open for 1% of the time, Pallas kernels for 12%

profile of v1, /device:TPU:8, one launch (start us, length us, event | category | flops | bytes accessed | tf_op | source)
XLA Modules:
  0.0 160.6 jit_solution(2712693656822359984)
XLA Ops:
  1.4 1.1 copy-done.2
  2.5 2.1 %pack.1 = f32[3200,128]{1,0:T(8,128)} custom-call(f32[3,128,512]{2,1,0:T(8,128)S(1)} %bitcast.22, s32[3,128]{1,0:T(4,128)S(1)} %bitcast.27, s32[3,128]{1,0:T(4,128)S(1)} %bitcast.26), custom_call_target="tpu_custom_call" | custom-call | tf_op jit(solution)/shard_map/pack/pallas_call | solution.py:353
  4.6 15.4 %all-to-all-start = ((f32[128,1,3200]{2,1,0:T(1,128)}), f32[128,1,3200]{2,1,0:T(1,128)S(1)}, u32[]{:S(2)}, u32[]{:S(2)}) async-start(f32[128,1,3200]{2,1,0:T(1,128)} %bitcast.2), calls=%async_computation | async-start | bytes 3276800 | tf_op jit(solution)/shard_map/all_to_all | solution.py:359
  20.1 1.9 %copy-done = f32[1,3,2,128,8,128]{5,4,3,2,1,0:T(8,128)S(1)} copy-done((f32[1,3,2,128,8,128]{5,4,3,2,1,0:T(8,128)S(1)}, f32[1,3,2,128,8,128]{5,4,3,2,1,0:T(8,128)}, u32[]{:S(2)}) %copy-start) | copy-done | bytes 3145752
  22.0 1.9 %copy-done.1 = f32[1,3,2,128,8,128]{5,4,3,2,1,0:T(8,128)S(1)} copy-done((f32[1,3,2,128,8,128]{5,4,3,2,1,0:T(8,128)S(1)}, f32[1,3,2,128,8,128]{5,4,3,2,1,0:T(8,128)}, u32[]{:S(2)}) %copy-start.1) | copy-done | bytes 3145752
  23.9 8.3 %coefficients.1 = (f32[1024,128]{1,0:T(8,128)S(1)}, f32[1024,128]{1,0:T(8,128)S(1)}, f32[1024,128]{1,0:T(8,128)S(1)}, f32[1024,128]{1,0:T(8,128)S(1)}, f32[1024,...) custom-call(f32[6144,128]{1,0:T(8,128)S(1)} %bitcast.18, ...), custom_call_target="tpu_custom_call" | custom-call | flops 4194304 | bytes 8388608 | tf_op jit(solution)/shard_map/coefficients/pallas_call | solution.py:364
  33.1 1.5 collective-permute-start
  35.0 3.4 %collective-permute-start.1 = (f32[384,128]{1,0:T(8,128)S(1)}, f32[384,128]{1,0:T(8,128)}, u32[]{:S(2)}, u32[]{:S(2)}) collective-permute-start(f32[384,128]{1,0:T(8,128)S(1)} %rim.1), channel_id=1, source_target_pairs={{0,8},{8,16},{16,24},{24,32},{32,40},{40,48},{48,56},{56,64},{64,7... | collective-permute-start | bytes 589832 | tf_op jit(solution)/shard_map/ppermute | solution.py:351
  38.5 25.3 %collective-permute-done.rim_ref = f32[24,128]{1,0:T(8,128)S(1)} collective-permute-done((f32[24,128]{1,0:T(8,128)S(1)}, f32[24,128]{1,0:T(8,128)S(1)}, u32[]{:S(2)}, u32[]{:S(2)}) %collective-permute-start) | collective-permute-done | bytes 12320 | tf_op jit(solution)/shard_map/ppermute | solution.py:375
  63.8 1.0 copy-done.22
  64.8 1.0 copy-done.24
  65.8 1.0 copy-done.26
  66.9 4.0 %shift.1 = (f32[1024,128]{1,0:T(8,128)S(1)}, f32[1024,128]{1,0:T(8,128)S(1)}, f32[1024,128]{1,0:T(8,128)S(1)}) custom-call(f32[24,128]{1,0:T(8,128)S(1)} %collective-permute-done.rim_ref, f32[1024,128]{1,0:T(8,128)S(1)} %copy-done.22, f32[1024,128]{1,0:T(8,128)S(1)} %copy-done.24, f32[1024,128]{1,0:T(8,128)S(1)} %copy-done.26), custom_call_target="tpu_custom_call" | custom-call | tf_op jit(solution)/shard_map/shift/pallas_call | solution.py:376
  73.3 3.8 %first.1 = (f32[4096,128]{1,0:T(8,128)S(1)}, f32[512,128]{1,0:T(8,128)S(1)}, f32[512,128]{1,0:T(8,128)S(1)}, f32[32,128]{1,0:T(8,128)S(1)}, f32[32,128]{1,0:T(8,128)S(1)}, /*index=5*/f32[32,128]{1,0:T(8,128)S(1)}) custom-call(f32[3200,128]{1,0:T(8,128)S(1)} %bitcast.15, f32[8,128]{1,0:T(8,128)S(1)} %broadcast_select_fusion.mask_ref), custom_call_target="tpu_custom_call" | custom-call | tf_op jit(solution)/shard_map/first/pallas_call | solution.py:391
  77.1 3.2 %collective-permute-start.2 = (f32[512,128]{1,0:T(8,128)S(1)}, f32[512,128]{1,0:T(8,128)S(1)}, u32[]{:S(2)}, u32[]{:S(2)}) collective-permute-start(f32[512,128]{1,0:T(8,128)S(1)} %get-tuple-element.48), channel_id=1, source_target_pairs={{0,8},{8,16},{16,24},{24,32},{32,40},{40,48},{48,56},{56,64},{64,7... | collective-permute-start | bytes 786440 | tf_op jit(solution)/shard_map/ppermute | solution.py:398
  80.3 5.5 %collective-permute-start.3 = (f32[512,128]{1,0:T(8,128)S(1)}, f32[512,128]{1,0:T(8,128)S(1)}, u32[]{:S(2)}, u32[]{:S(2)}) collective-permute-start(f32[512,128]{1,0:T(8,128)S(1)} %get-tuple-element.49), channel_id=1, source_target_pairs={{8,0},{16,8},{24,16},{32,24},{40,32},{48,40},{56,48},{64,56},{72,6... | collective-permute-start | bytes 786440 | tf_op jit(solution)/shard_map/ppermute | solution.py:399
  86.8 8.0 %collective-permute-start.5 = (f32[32,128]{1,0:T(8,128)S(1)}, f32[32,128]{1,0:T(8,128)S(1)}, u32[]{:S(2)}, u32[]{:S(2)}) collective-permute-start(f32[32,128]{1,0:T(8,128)S(1)} %get-tuple-element.51), channel_id=1, source_target_pairs={{0,7},{1,0},{2,1},{3,2},{4,3},{5,4},{6,5},{7,6},{8,15},{9,8},{10,9... | collective-permute-start | bytes 49160 | tf_op jit(solution)/shard_map/ppermute | solution.py:401
  94.9 1.3 collective-permute-start.6
  96.2 1.1 forcing.2.rest_0_
  97.4 6.1 %step.3 = (f32[4096,128]{1,0:T(8,128)S(1)}, f32[512,128]{1,0:T(8,128)S(1)}, f32[512,128]{1,0:T(8,128)S(1)}, f32[32,128]{1,0:T(8,128)S(1)}, f32[32,128]{1,0:T(8,128)S(1)}, /*index=5*/f32[32,128]{1,0:T(8,128)S(1)}) custom-call(f32[4,4]{1,0:T(4,128)S(1)} %bitcast.23, f32[4,4]{1,0:T(4,128)S(1)} %copy-done.28, f32[4096,128]{1,0:T(8,128)S(1)} %get-tuple-element.39.m_ref, ...), custom_call_target="tpu_custom_call" | custom-call | tf_op jit(solution)/shard_map/step/pallas_call | solution.py:435
  103.5 2.1 %collective-permute-start.7 = (f32[512,128]{1,0:T(8,128)S(1)}, f32[512,128]{1,0:T(8,128)S(1)}, u32[]{:S(2)}, u32[]{:S(2)}) collective-permute-start(f32[512,128]{1,0:T(8,128)S(1)} %get-tuple-element.58), channel_id=1, source_target_pairs={{0,8},{8,16},{16,24},{24,32},{32,40},{40,48},{48,56},{56,64},{64,7... | collective-permute-start | bytes 786440 | tf_op jit(solution)/shard_map/ppermute | solution.py:398
  105.6 6.6 %collective-permute-start.8 = (f32[512,128]{1,0:T(8,128)S(1)}, f32[512,128]{1,0:T(8,128)S(1)}, u32[]{:S(2)}, u32[]{:S(2)}) collective-permute-start(f32[512,128]{1,0:T(8,128)S(1)} %get-tuple-element.59), channel_id=1, source_target_pairs={{8,0},{16,8},{24,16},{32,24},{40,32},{48,40},{56,48},{64,56},{72,6... | collective-permute-start | bytes 786440 | tf_op jit(solution)/shard_map/ppermute | solution.py:399
  112.2 7.4 %collective-permute-start.10 = (f32[32,128]{1,0:T(8,128)S(1)}, f32[32,128]{1,0:T(8,128)S(1)}, u32[]{:S(2)}, u32[]{:S(2)}) collective-permute-start(f32[32,128]{1,0:T(8,128)S(1)} %get-tuple-element.61), channel_id=1, source_target_pairs={{0,7},{1,0},{2,1},{3,2},{4,3},{5,4},{6,5},{7,6},{8,15},{9,8},{10,9... | collective-permute-start | bytes 49160 | tf_op jit(solution)/shard_map/ppermute | solution.py:401
  119.6 1.3 collective-permute-start.11
  121.2 1.1 forcing.3.rest_0_
  122.3 8.6 %collective-permute-done.9.from_west_ref = f32[32,128]{1,0:T(8,128)S(1)} collective-permute-done((f32[32,128]{1,0:T(8,128)S(1)}, f32[32,128]{1,0:T(8,128)S(1)}, u32[]{:S(2)}, u32[]{:S(2)}) %collective-permute-start.9) | collective-permute-done | bytes 16416 | tf_op jit(solution)/shard_map/ppermute | solution.py:400
  131.0 6.1 %step.4 = (f32[4096,128]{1,0:T(8,128)S(1)}, f32[512,128]{1,0:T(8,128)S(1)}, f32[512,128]{1,0:T(8,128)S(1)}, f32[32,128]{1,0:T(8,128)S(1)}, f32[32,128]{1,0:T(8,128)S(1)}, /*index=5*/f32[32,128]{1,0:T(8,128)S(1)}) custom-call(f32[4,4]{1,0:T(4,128)S(1)} %bitcast.24, f32[4,4]{1,0:T(4,128)S(1)} %copy-done.28, f32[4096,128]{1,0:T(8,128)S(1)} %get-tuple-element.53.m_ref, ...), custom_call_target="tpu_custom_call" | custom-call | tf_op jit(solution)/shard_map/step/pallas_call | solution.py:435
  137.1 1.9 %collective-permute-start.12 = (f32[512,128]{1,0:T(8,128)S(1)}, f32[512,128]{1,0:T(8,128)S(1)}, u32[]{:S(2)}, u32[]{:S(2)}) collective-permute-start(f32[512,128]{1,0:T(8,128)S(1)} %get-tuple-element.68), channel_id=1, source_target_pairs={{0,8},{8,16},{16,24},{24,32},{32,40},{40,48},{48,56},{56,64},{64,7... | collective-permute-start | bytes 786440 | tf_op jit(solution)/shard_map/ppermute | solution.py:398
  139.0 6.6 %collective-permute-start.13 = (f32[512,128]{1,0:T(8,128)S(1)}, f32[512,128]{1,0:T(8,128)S(1)}, u32[]{:S(2)}, u32[]{:S(2)}) collective-permute-start(f32[512,128]{1,0:T(8,128)S(1)} %get-tuple-element.69), channel_id=1, source_target_pairs={{8,0},{16,8},{24,16},{32,24},{40,32},{48,40},{56,48},{64,56},{72,6... | collective-permute-start | bytes 786440 | tf_op jit(solution)/shard_map/ppermute | solution.py:399
  145.8 8.0 %collective-permute-start.15 = (f32[32,128]{1,0:T(8,128)S(1)}, f32[32,128]{1,0:T(8,128)S(1)}, u32[]{:S(2)}, u32[]{:S(2)}) collective-permute-start(f32[32,128]{1,0:T(8,128)S(1)} %get-tuple-element.71), channel_id=1, source_target_pairs={{0,7},{1,0},{2,1},{3,2},{4,3},{5,4},{6,5},{7,6},{8,15},{9,8},{10,9... | collective-permute-start | bytes 49160 | tf_op jit(solution)/shard_map/ppermute | solution.py:401
  153.8 1.3 collective-permute-start.16
  155.9 4.7 %step.5 = f32[4096,128]{1,0:T(8,128)} custom-call(f32[4,4]{1,0:T(4,128)S(1)} %bitcast.25, f32[4,4]{1,0:T(4,128)S(1)} %copy-done.28, f32[4096,128]{1,0:T(8,128)S(1)} %get-tuple-element.63.m_ref, f32[1024,128]{1,0:T(8,128)S(1)} %get-tuple-element.64.up_e_ref, f32[1024,128]{1,0:T(8,128)S(1)} %copy-done.4, f32[1024,128]{1,0:T(8,128)S(1)} %get-tuple-element.66.up_n_ref, ...), custom_call_target="tpu_custom_call" | custom-call | tf_op jit(solution)/shard_map/step/pallas_call | solution.py:435
  (80 shorter events, 7.2 us)
Async XLA Ops:
  4.6 68.6 %all-to-all-start = ((f32[128,1,3200]{2,1,0:T(1,128)}), f32[128,1,3200]{2,1,0:T(1,128)S(1)}, u32[]{:S(2)}, u32[]{:S(2)}) async-start(f32[128,1,3200]{2,1,0:T(1,128)} %bitcast.2), calls=%async_computation | async-start | bytes 3276800 | tf_op jit(solution)/shard_map/all_to_all | solution.py:359
  33.0 2.0 %copy-start.17 = (f32[1024,128]{1,0:T(8,128)}, f32[1024,128]{1,0:T(8,128)S(1)}, u32[]{:S(2)}) copy-start(f32[1024,128]{1,0:T(8,128)S(1)} %get-tuple-element.47.down_n_ref) | copy-start | bytes 1572868
  33.0 2.0 %copy-start.25 = (f32[1024,128]{1,0:T(8,128)}, f32[1024,128]{1,0:T(8,128)S(1)}, u32[]{:S(2)}) copy-start(f32[1024,128]{1,0:T(8,128)S(1)} %get-tuple-element.44.refs_2_) | copy-start | bytes 1572868
  33.1 30.7 %collective-permute-start = (f32[24,128]{1,0:T(8,128)S(1)}, f32[24,128]{1,0:T(8,128)S(1)}, u32[]{:S(2)}, u32[]{:S(2)}) collective-permute-start(f32[24,128]{1,0:T(8,128)S(1)} %get-tuple-element.41), channel_id=1, source_target_pairs={{0,1},{1,2},{2,3},{3,4},{4,5},{5,6},{6,7},{7,0},{8,9},{9,10},{10,1... | collective-permute-start | bytes 36872 | tf_op jit(solution)/shard_map/ppermute | solution.py:375
  34.6 3.8 %copy-start.29 = (s32[8,128]{1,0:T(8,128)S(1)}, s32[8,128]{1,0:T(8,128)}, u32[]{:S(2)}) copy-start(s32[8,128]{1,0:T(8,128)} %param.15) | copy-start | bytes 12292
  35.0 50.8 %collective-permute-start.1 = (f32[384,128]{1,0:T(8,128)S(1)}, f32[384,128]{1,0:T(8,128)}, u32[]{:S(2)}, u32[]{:S(2)}) collective-permute-start(f32[384,128]{1,0:T(8,128)S(1)} %rim.1), channel_id=1, source_target_pairs={{0,8},{8,16},{16,24},{24,32},{32,40},{40,48},{48,56},{56,64},{64,7... | collective-permute-start | bytes 589832 | tf_op jit(solution)/shard_map/ppermute | solution.py:351
  77.1 20.2 %copy-start.14 = (f32[1024,128]{1,0:T(8,128)S(1)}, f32[1024,128]{1,0:T(8,128)}, u32[]{:S(2)}) copy-start(f32[1024,128]{1,0:T(8,128)} %copy-done.13) | copy-start | bytes 1572868
  77.1 20.2 %copy-start.16 = (f32[1024,128]{1,0:T(8,128)S(1)}, f32[1024,128]{1,0:T(8,128)}, u32[]{:S(2)}) copy-start(f32[1024,128]{1,0:T(8,128)} %copy-done.15) | copy-start | bytes 1572868
  77.1 20.2 %copy-start.18 = (f32[1024,128]{1,0:T(8,128)S(1)}, f32[1024,128]{1,0:T(8,128)}, u32[]{:S(2)}) copy-start(f32[1024,128]{1,0:T(8,128)} %copy-done.17) | copy-start | bytes 1572868
  77.1 20.2 %copy-start.20 = (f32[1024,128]{1,0:T(8,128)S(1)}, f32[1024,128]{1,0:T(8,128)}, u32[]{:S(2)}) copy-start(f32[1024,128]{1,0:T(8,128)} %copy-done.19) | copy-start | bytes 1572868
  77.1 20.2 %copy-start.27 = (f32[1,4,4]{2,1,0:T(4,128)S(1)}, f32[1,4,4]{2,1,0:T(4,128)}, u32[]{:S(2)}) copy-start(f32[1,4,4]{2,1,0:T(4,128)} %param.13) | copy-start | bytes 196
  77.1 20.2 %copy-start.28 = (f32[4,4]{1,0:T(4,128)S(1)}, f32[4,4]{1,0:T(4,128)}, u32[]{:S(2)}) copy-start(f32[4,4]{1,0:T(4,128)} %air_ref.5) | copy-start | bytes 196
  77.1 20.2 %collective-permute-start.2 = (f32[512,128]{1,0:T(8,128)S(1)}, f32[512,128]{1,0:T(8,128)S(1)}, u32[]{:S(2)}, u32[]{:S(2)}) collective-permute-start(f32[512,128]{1,0:T(8,128)S(1)} %get-tuple-element.48), channel_id=1, source_target_pairs={{0,8},{8,16},{16,24},{24,32},{32,40},{40,48},{48,56},{56,64},{64,7... | collective-permute-start | bytes 786440 | tf_op jit(solution)/shard_map/ppermute | solution.py:398
  80.3 17.0 %collective-permute-start.3 = (f32[512,128]{1,0:T(8,128)S(1)}, f32[512,128]{1,0:T(8,128)S(1)}, u32[]{:S(2)}, u32[]{:S(2)}) collective-permute-start(f32[512,128]{1,0:T(8,128)S(1)} %get-tuple-element.49), channel_id=1, source_target_pairs={{8,0},{16,8},{24,16},{32,24},{40,32},{48,40},{56,48},{64,56},{72,6... | collective-permute-start | bytes 786440 | tf_op jit(solution)/shard_map/ppermute | solution.py:399
  86.8 10.5 %collective-permute-start.4 = (f32[32,128]{1,0:T(8,128)S(1)}, f32[32,128]{1,0:T(8,128)S(1)}, u32[]{:S(2)}, u32[]{:S(2)}) collective-permute-start(f32[32,128]{1,0:T(8,128)S(1)} %get-tuple-element.50), channel_id=1, source_target_pairs={{0,1},{1,2},{2,3},{3,4},{4,5},{5,6},{6,7},{7,0},{8,9},{9,10},{10,1... | collective-permute-start | bytes 49160 | tf_op jit(solution)/shard_map/ppermute | solution.py:400
  86.8 10.4 %collective-permute-start.5 = (f32[32,128]{1,0:T(8,128)S(1)}, f32[32,128]{1,0:T(8,128)S(1)}, u32[]{:S(2)}, u32[]{:S(2)}) collective-permute-start(f32[32,128]{1,0:T(8,128)S(1)} %get-tuple-element.51), channel_id=1, source_target_pairs={{0,7},{1,0},{2,1},{3,2},{4,3},{5,4},{6,5},{7,6},{8,15},{9,8},{10,9... | collective-permute-start | bytes 49160 | tf_op jit(solution)/shard_map/ppermute | solution.py:401
  94.9 2.4 %collective-permute-start.6 = (f32[32,128]{1,0:T(8,128)S(1)}, f32[32,128]{1,0:T(8,128)S(1)}, u32[]{:S(2)}, u32[]{:S(2)}) collective-permute-start(f32[32,128]{1,0:T(8,128)S(1)} %get-tuple-element.52), channel_id=1, source_target_pairs={{0,128},{1,129},{2,130},{3,131},{4,132},{5,133},{6,134},{7,135},{8... | collective-permute-start | bytes 49160 | tf_op jit(solution)/shard_map/ppermute | solution.py:402
  103.5 27.4 %copy-start.6 = (f32[1024,128]{1,0:T(8,128)S(1)}, f32[1024,128]{1,0:T(8,128)}, u32[]{:S(2)}) copy-start(f32[1024,128]{1,0:T(8,128)} %copy-done.5) | copy-start | bytes 1572868
  103.5 27.4 %copy-start.8 = (f32[1024,128]{1,0:T(8,128)S(1)}, f32[1024,128]{1,0:T(8,128)}, u32[]{:S(2)}) copy-start(f32[1024,128]{1,0:T(8,128)} %copy-done.7) | copy-start | bytes 1572868
  103.5 27.4 %copy-start.10 = (f32[1024,128]{1,0:T(8,128)S(1)}, f32[1024,128]{1,0:T(8,128)}, u32[]{:S(2)}) copy-start(f32[1024,128]{1,0:T(8,128)} %copy-done.9) | copy-start | bytes 1572868
  103.5 27.4 %copy-start.12 = (f32[1024,128]{1,0:T(8,128)S(1)}, f32[1024,128]{1,0:T(8,128)}, u32[]{:S(2)}) copy-start(f32[1024,128]{1,0:T(8,128)} %copy-done.11) | copy-start | bytes 1572868
  103.5 27.4 %collective-permute-start.7 = (f32[512,128]{1,0:T(8,128)S(1)}, f32[512,128]{1,0:T(8,128)S(1)}, u32[]{:S(2)}, u32[]{:S(2)}) collective-permute-start(f32[512,128]{1,0:T(8,128)S(1)} %get-tuple-element.58), channel_id=1, source_target_pairs={{0,8},{8,16},{16,24},{24,32},{32,40},{40,48},{48,56},{56,64},{64,7... | collective-permute-start | bytes 786440 | tf_op jit(solution)/shard_map/ppermute | solution.py:398
  105.6 25.3 %collective-permute-start.8 = (f32[512,128]{1,0:T(8,128)S(1)}, f32[512,128]{1,0:T(8,128)S(1)}, u32[]{:S(2)}, u32[]{:S(2)}) collective-permute-start(f32[512,128]{1,0:T(8,128)S(1)} %get-tuple-element.59), channel_id=1, source_target_pairs={{8,0},{16,8},{24,16},{32,24},{40,32},{48,40},{56,48},{64,56},{72,6... | collective-permute-start | bytes 786440 | tf_op jit(solution)/shard_map/ppermute | solution.py:399
  112.2 10.1 %collective-permute-start.10 = (f32[32,128]{1,0:T(8,128)S(1)}, f32[32,128]{1,0:T(8,128)S(1)}, u32[]{:S(2)}, u32[]{:S(2)}) collective-permute-start(f32[32,128]{1,0:T(8,128)S(1)} %get-tuple-element.61), channel_id=1, source_target_pairs={{0,7},{1,0},{2,1},{3,2},{4,3},{5,4},{6,5},{7,6},{8,15},{9,8},{10,9... | collective-permute-start | bytes 49160 | tf_op jit(solution)/shard_map/ppermute | solution.py:401
  119.6 2.7 %collective-permute-start.11 = (f32[32,128]{1,0:T(8,128)S(1)}, f32[32,128]{1,0:T(8,128)S(1)}, u32[]{:S(2)}, u32[]{:S(2)}) collective-permute-start(f32[32,128]{1,0:T(8,128)S(1)} %get-tuple-element.62), channel_id=1, source_target_pairs={{0,128},{1,129},{2,130},{3,131},{4,132},{5,133},{6,134},{7,135},{8... | collective-permute-start | bytes 49160 | tf_op jit(solution)/shard_map/ppermute | solution.py:402
  120.9 10.0 %collective-permute-start.9 = (f32[32,128]{1,0:T(8,128)S(1)}, f32[32,128]{1,0:T(8,128)S(1)}, u32[]{:S(2)}, u32[]{:S(2)}) collective-permute-start(f32[32,128]{1,0:T(8,128)S(1)} %get-tuple-element.60), channel_id=1, source_target_pairs={{0,1},{1,2},{2,3},{3,4},{4,5},{5,6},{6,7},{7,0},{8,9},{9,10},{10,1... | collective-permute-start | bytes 49160 | tf_op jit(solution)/shard_map/ppermute | solution.py:400
  131.0 24.9 %copy-start.4 = (f32[1024,128]{1,0:T(8,128)S(1)}, f32[1024,128]{1,0:T(8,128)}, u32[]{:S(2)}) copy-start(f32[1024,128]{1,0:T(8,128)} %copy-done.3) | copy-start | bytes 1572868
  137.1 18.8 %collective-permute-start.12 = (f32[512,128]{1,0:T(8,128)S(1)}, f32[512,128]{1,0:T(8,128)S(1)}, u32[]{:S(2)}, u32[]{:S(2)}) collective-permute-start(f32[512,128]{1,0:T(8,128)S(1)} %get-tuple-element.68), channel_id=1, source_target_pairs={{0,8},{8,16},{16,24},{24,32},{32,40},{40,48},{48,56},{56,64},{64,7... | collective-permute-start | bytes 786440 | tf_op jit(solution)/shard_map/ppermute | solution.py:398
  139.0 16.9 %collective-permute-start.13 = (f32[512,128]{1,0:T(8,128)S(1)}, f32[512,128]{1,0:T(8,128)S(1)}, u32[]{:S(2)}, u32[]{:S(2)}) collective-permute-start(f32[512,128]{1,0:T(8,128)S(1)} %get-tuple-element.69), channel_id=1, source_target_pairs={{8,0},{16,8},{24,16},{32,24},{40,32},{48,40},{56,48},{64,56},{72,6... | collective-permute-start | bytes 786440 | tf_op jit(solution)/shard_map/ppermute | solution.py:399
  145.7 9.8 %collective-permute-start.14 = (f32[32,128]{1,0:T(8,128)S(1)}, f32[32,128]{1,0:T(8,128)S(1)}, u32[]{:S(2)}, u32[]{:S(2)}) collective-permute-start(f32[32,128]{1,0:T(8,128)S(1)} %get-tuple-element.70), channel_id=1, source_target_pairs={{0,1},{1,2},{2,3},{3,4},{4,5},{5,6},{6,7},{7,0},{8,9},{9,10},{10,1... | collective-permute-start | bytes 49160 | tf_op jit(solution)/shard_map/ppermute | solution.py:400
  145.8 9.7 %collective-permute-start.15 = (f32[32,128]{1,0:T(8,128)S(1)}, f32[32,128]{1,0:T(8,128)S(1)}, u32[]{:S(2)}, u32[]{:S(2)}) collective-permute-start(f32[32,128]{1,0:T(8,128)S(1)} %get-tuple-element.71), channel_id=1, source_target_pairs={{0,7},{1,0},{2,1},{3,2},{4,3},{5,4},{6,5},{7,6},{8,15},{9,8},{10,9... | collective-permute-start | bytes 49160 | tf_op jit(solution)/shard_map/ppermute | solution.py:401
  153.8 2.1 %collective-permute-start.16 = (f32[32,128]{1,0:T(8,128)S(1)}, f32[32,128]{1,0:T(8,128)S(1)}, u32[]{:S(2)}, u32[]{:S(2)}) collective-permute-start(f32[32,128]{1,0:T(8,128)S(1)} %get-tuple-element.72), channel_id=1, source_target_pairs={{0,128},{1,129},{2,130},{3,131},{4,132},{5,133},{6,134},{7,135},{8... | collective-permute-start | bytes 49160 | tf_op jit(solution)/shard_map/ppermute | solution.py:402
  (16 other events, 22.9 us)

commit v2 on v1

v2 whole, which is shorter than its diff:
```python
import functools

import jax
import jax.numpy as jnp
from jax import lax
from jax.experimental import pallas as pl
from jax.experimental.pallas import tpu as pltpu
from jax.sharding import PartitionSpec as P

LANES = 128
SUBS = 8
VMEM_LIMIT = 20 * 1024 * 1024


def split3(x):
    hi = x.astype(jnp.bfloat16)
    rest = x - hi.astype(jnp.float32)
    mid = rest.astype(jnp.bfloat16)
    low = (rest - mid.astype(jnp.float32)).astype(jnp.bfloat16)
    return [hi, mid, low]


def pack_kernel(slots, rows_hbm, owner_hbm, cell_hbm, out_ref, rows_ref, owner_ref, cell_ref, sems):
    steps, count, width = rows_ref.shape
    owners = count
    parts = width // LANES
    stride = out_ref.shape[0] // owners
    small = [
        pltpu.make_async_copy(owner_hbm, owner_ref, sems.at[steps]),
        pltpu.make_async_copy(cell_hbm, cell_ref, sems.at[steps + 1]),
    ]
    large = [
        pltpu.make_async_copy(rows_hbm.at[step], rows_ref.at[step], sems.at[step]) for step in range(steps)
    ]
    for copy in small + large:
        copy.start()
    dest = lax.broadcasted_iota(jnp.int32, (owners, count), 0)
    lane = lax.broadcasted_iota(jnp.int32, (owners, count), 1)
    before = (dest < lane).astype(jnp.bfloat16)
    cells = jnp.zeros((owners, LANES), jnp.float32)
    for copy in small:
        copy.wait()
    for step in range(steps):
        hits = owner_ref[step : step + 1, :] == dest
        hits_f = hits.astype(jnp.float32)
        prior = jnp.dot(hits_f.astype(jnp.bfloat16), before, preferred_element_type=jnp.float32)
        large[step].wait()
        terms = jnp.concatenate(split3(rows_ref[step]), axis=0)
        marks = (cell_ref[step : step + 1, :] + 1).astype(jnp.float32)
        for k in range(slots):
            slot = step * slots + k
            pick = jnp.where(prior == float(k), hits_f, 0.0)
            pick_b = pick.astype(jnp.bfloat16)
            out = jnp.dot(
                jnp.concatenate([pick_b] * 3, axis=1), terms, preferred_element_type=jnp.float32
            )
            for part in range(parts):
                out_ref[pl.ds(slot * parts + part, owners, stride=stride), :] = out[
                    :, part * LANES : (part + 1) * LANES
                ]
            mark = jnp.sum(pick * marks, axis=1, keepdims=True)
            cells = jnp.where(lane == slot, mark, cells)
    out_ref[pl.ds(stride - 1, owners, stride=stride), :] = cells


def spread_rows(step, slots, got_ref, width):
    parts = width // LANES
    stride = parts * slots * 3 + 1
    sources = got_ref.shape[0] // stride
    marks = got_ref[pl.ds(stride - 1, sources, stride=stride), :]
    where_to = lax.broadcasted_iota(jnp.int32, (sources, SUBS * LANES), 1)
    terms, onehots = [], []
    for k in range(slots):
        slot = step * slots + k
        cols = []
        for part in range(parts):
            block = got_ref[pl.ds(slot * parts + part, sources, stride=stride), :]
            cols.append(block.T)
        turned = jnp.concatenate(cols, axis=0)
        terms += split3(turned)
        cell = marks[:, slot : slot + 1].astype(jnp.int32) - 1
        onehot = (cell == where_to).astype(jnp.float32).astype(jnp.bfloat16)
        onehots += [onehot] * 3
    return jnp.dot(
        jnp.concatenate(terms, axis=1),
        jnp.concatenate(onehots, axis=0),
        preferred_element_type=jnp.float32,
    )


def columns_start(fields):
    zero = jnp.zeros((SUBS, LANES), jnp.float32)
    return [zero] * (2 * fields)


def columns_insert(cols, f, at, plane):
    lane = lax.broadcasted_iota(jnp.int32, (SUBS, LANES), 1)
    turned = plane if at == 0 else pltpu.roll(plane, at, 1)
    here = (lane == at) | (lane == (at - 1) % LANES)
    half = 2 * f + at % 2
    cols[half] = jnp.where(here, turned, cols[half])


def columns_turn(cols, groups):
    return [pltpu.roll(c, LANES - groups * SUBS, 1) for c in cols]


def columns_store(cols, rim, column_ref, fields):
    even = lax.broadcasted_iota(jnp.int32, (SUBS, LANES), 1) % 2 == 0
    for f in range(fields):
        a, b = cols[2 * f], cols[2 * f + 1]
        column_ref[f * SUBS : (f + 1) * SUBS, :] = jnp.where(even, a, b)
        column_ref[(fields + f) * SUBS : (fields + f + 1) * SUBS, :] = jnp.where(even, b, a)
    column_ref[2 * fields * SUBS :, :] = rim


def columns_load(lon_even, first_ref, second_ref, fields):
    even = lax.broadcasted_iota(jnp.int32, (SUBS, LANES), 1) % 2 == 0

    def rows(i):
        one, two = first_ref[i * SUBS : (i + 1) * SUBS, :], second_ref[i * SUBS : (i + 1) * SUBS, :]
        return jnp.where(lon_even, one, two), jnp.where(lon_even, two, one)

    cols = []
    for f in range(fields):
        west = pltpu.roll(rows(fields + f)[0], 1, 1)
        east = pltpu.roll(rows(f)[1], LANES - 1, 1)
        cols += [jnp.where(even, west, east), jnp.where(even, east, west)]
    return cols + [pltpu.roll(rows(2 * fields)[0], 1, 1)]


def turn_to_first(col, at):
    return col if at == 0 else pltpu.roll(col, LANES - at, 1)


def rows_of(base, group):
    if isinstance(group, int):
        return pl.ds(base + group * SUBS, SUBS)
    return pl.ds(pl.multiple_of(base + group * SUBS, SUBS), SUBS)


def slabs_store(lat_even, m_ref, first_ref, second_ref, width):
    for i in range(width // SUBS):
        rows = slice(i * SUBS, (i + 1) * SUBS)
        south = m_ref[rows, :]
        north = m_ref[(SUBS - 1) * width + i * SUBS : (SUBS - 1) * width + (i + 1) * SUBS, :]
        first_ref[rows, :] = jnp.where(lat_even, north, south)
        second_ref[rows, :] = jnp.where(lat_even, south, north)


def parity(ref, i):
    return jnp.full((SUBS, LANES), ref[i], jnp.int32) == 0


def low_store(m_ref, low_ref, fields, levels):
    for f in range(fields):
        low_ref[f * SUBS : (f + 1) * SUBS, :] = m_ref[
            pl.ds(f * levels + levels - 1, SUBS, stride=fields * levels), :
        ]


def first_kernel(
    step, slots, fields, levels, odd_ref, got_ref, mask_ref, rim_ref, m_ref, slab1_ref, slab2_ref, column_ref, low_ref
):
    width = fields * levels
    out = spread_rows(step, slots, got_ref, width)
    for y in range(SUBS):
        m_ref[y * width : (y + 1) * width, :] = out[:, y * LANES : (y + 1) * LANES] * mask_ref[y : y + 1, :]
    slabs_store(parity(odd_ref, 0), m_ref, slab1_ref, slab2_ref, width)
    cols = columns_start(fields)
    for group in range(levels // SUBS):
        for f in range(fields):
            for y in range(SUBS):
                columns_insert(cols, f, group * SUBS + y, m_ref[rows_of(y * width + f * levels, group), :])
    columns_store(cols, rim_ref[step * SUBS : (step + 1) * SUBS, :], column_ref, fields)
    low_store(m_ref, low_ref, fields, levels)


def forcing_kernel(step, slots, width, got_ref, f_ref):
    out = spread_rows(step, slots, got_ref, width)
    for y in range(SUBS):
        f_ref[y * width : (y + 1) * width, :] = out[:, y * LANES : (y + 1) * LANES]


def rim_kernel(vel_ref, dif_ref, rim_ref, vel_row, dif_row, sems):
    copies = [
        pltpu.make_async_copy(src.at[:, 1, :, SUBS - 1, :], dst, sems.at[i])
        for i, (src, dst) in enumerate(((vel_ref, vel_row), (dif_ref, dif_row)))
    ]
    for copy in copies:
        copy.start()
    for copy in copies:
        copy.wait()
    steps, levels, lanes = vel_row.shape
    rim_ref[...] = (jnp.minimum(vel_row[...], 0.0) - dif_row[...]).reshape(steps * levels, lanes)


def coefficient_kernel(steps, levels, vel_ref, dif_ref, open_ref, *outs):
    tables, rim_ref = outs[:-1], outs[-1]
    lane = lax.broadcasted_iota(jnp.int32, (SUBS, LANES), 1)
    for step in range(steps):
        up_e_ref, down_w_ref, up_n_ref, down_n_ref = tables[4 * step : 4 * step + 4]
        east, north = 2 * step * levels * SUBS, (2 * step + 1) * levels * SUBS
        for y in range(SUBS):
            rows = slice(y * levels, (y + 1) * levels)
            w = vel_ref[pl.ds(east + y, levels, stride=SUBS), :]
            k = dif_ref[pl.ds(east + y, levels, stride=SUBS), :]
            up_e_ref[rows, :] = jnp.maximum(w, 0.0) + k
            down_w_ref[rows, :] = pltpu.roll(jnp.minimum(w, 0.0) - k, 1, 1)
            w = vel_ref[pl.ds(north + y, levels, stride=SUBS), :]
            k = dif_ref[pl.ds(north + y, levels, stride=SUBS), :]
            up = jnp.maximum(w, 0.0) + k
            up_n_ref[rows, :] = up * open_ref[...] if y == SUBS - 1 else up
            down_n_ref[rows, :] = jnp.minimum(w, 0.0) - k
        rim = jnp.zeros((SUBS, LANES), jnp.float32)
        for group in range(levels // SUBS):
            for y in range(SUBS):
                at = group * SUBS + y
                plane = down_w_ref[rows_of(y * levels, group), :]
                to = (at - 1) % LANES
                rim = jnp.where(lane == to, plane if to == 0 else pltpu.roll(plane, to, 1), rim)
        rim_ref[step * SUBS : (step + 1) * SUBS, :] = rim


def step_kernel(
    last,
    step,
    fields,
    levels,
    mix_ref,
    air_ref,
    odd_ref,
    m_ref,
    up_e_ref,
    down_w_ref,
    up_n_ref,
    down_n_ref,
    north_rim_ref,
    sea_ref,
    mask_ref,
    from_slab1_ref,
    from_slab2_ref,
    from_column1_ref,
    from_column2_ref,
    from_low_ref,
    *rest,
):
    if last:
        (out_ref,) = rest
    else:
        f_ref, rim_ref, out_ref, slab1_ref, slab2_ref, column_ref, low_ref = rest
    width = fields * levels
    batch = 4
    lane = lax.broadcasted_iota(jnp.int32, (SUBS, LANES), 1)
    sub = lax.broadcasted_iota(jnp.int32, (SUBS, LANES), 0)
    at_west, at_east = lane == 0, lane == LANES - 1
    mix = [[mix_ref[f, g] for g in range(fields)] for f in range(fields)]
    lat_even, lon_even = parity(odd_ref, 0), parity(odd_ref, 1)
    sea = sea_ref[...]
    coupled = []
    for g in range(fields):
        total = jnp.zeros((SUBS, LANES), jnp.float32)
        for f in range(fields):
            total = total + air_ref[f, g] * from_low_ref[f * SUBS : (f + 1) * SUBS, :]
        coupled.append(sea * total)

    def batch_step(group0, halos, cols):
        cols = list(cols)
        for u in range(batch):
            group = group0 + u
            for y in range(SUBS):
                at = u * SUBS + y
                up_e = up_e_ref[rows_of(y * levels, group), :]
                down_w = jnp.where(
                    at_west, turn_to_first(halos[2 * fields], at), down_w_ref[rows_of(y * levels, group), :]
                )
                up_n = up_n_ref[rows_of(y * levels, group), :]
                if y == 0:
                    down_s = north_rim_ref[rows_of(0, group), :]
                else:
                    down_s = down_n_ref[rows_of((y - 1) * levels, group), :]
                planes = [m_ref[rows_of(y * width + f * levels, group), :] for f in range(fields)]
                for g in range(fields):
                    m = planes[g]
                    if y == 0 or y == SUBS - 1:
                        one = from_slab1_ref[rows_of(g * levels, group), :]
                        two = from_slab2_ref[rows_of(g * levels, group), :]
                    if y == SUBS - 1:
                        north = jnp.where(lat_even, one, two)
                    else:
                        north = m_ref[rows_of((y + 1) * width + g * levels, group), :]
                    if y == 0:
                        south = jnp.where(lat_even, two, one)
                    else:
                        south = m_ref[rows_of((y - 1) * width + g * levels, group), :]
                    halo = turn_to_first(halos[2 * g + at % 2], at)
                    east = jnp.where(at_east, halo, pltpu.roll(m, LANES - 1, 1))
                    west = jnp.where(at_west, halo, pltpu.roll(m, 1, 1))
                    result = m
                    for f in range(fields):
                        result = result + mix[f][g] * planes[f]
                    result = result + (up_e * (east - m) + down_w * (m - west))
                    result = result + (up_n * (north - m) + down_s * (m - south))
                    if isinstance(group, int) and group == 0:
                        result = result + jnp.where(sub == 0, coupled[g][y : y + 1, :], 0.0)
                    if last:
                        out_ref[pl.ds(g * levels * SUBS + y + group * (SUBS * SUBS), SUBS, stride=SUBS), :] = result
                        continue
                    rows = rows_of(y * width + g * levels, group)
                    result = (result + f_ref[rows, :]) * mask_ref[y : y + 1, :]
                    out_ref[rows, :] = result
                    columns_insert(cols, g, at, result)
        return columns_turn(halos, batch), columns_turn(cols, batch)

    halos = columns_load(lon_even, from_column1_ref, from_column2_ref, fields)
    halos, cols = batch_step(0, halos, [] if last else columns_start(fields))

    def body(i, carry):
        halos, cols = batch_step(i * batch, list(carry[0]), list(carry[1]))
        return tuple(halos), tuple(cols)

    halos, cols = lax.fori_loop(1, levels // (SUBS * batch), body, (tuple(halos), tuple(cols)))
    if not last:
        columns_store(cols, rim_ref[(step - 1) * SUBS : step * SUBS, :], column_ref, fields)
        slabs_store(lat_even, out_ref, slab1_ref, slab2_ref, width)
        low_store(out_ref, low_ref, fields, levels)


def params():
    return pltpu.CompilerParams(vmem_limit_bytes=VMEM_LIMIT)


def swaps(axis, start, closed):
    count = lax.axis_size(axis)
    pairs = []
    for i in range(start, count if closed else count - 1, 2):
        j = (i + 1) % count
        pairs += [(i, j), (j, i)]
    return pairs


def shards(innovations, obs_owner, obs_cell, velocity, diffusion, mixing, air_sea, sea_mask):
    lat_count = lax.axis_size("lat")
    lon_count = lax.axis_size("lon")
    owners = lat_count * lon_count
    steps, levels, lat_rows, lon_cols = (velocity.shape[i] for i in (1, 3, 4, 5))
    fields = mixing.shape[1]
    width = fields * levels
    count = innovations.shape[2]
    slots = 2
    assert (lat_rows, lon_cols, levels, count, owners, steps) == (SUBS, LANES, LANES, LANES, LANES, 3)
    f32 = functools.partial(jax.ShapeDtypeStruct, dtype=jnp.float32)
    stride = steps * slots * width // LANES + 1

    is_ocean = lax.axis_index("comp") == 1
    sea_float = sea_mask.astype(jnp.float32)
    mask = jnp.where(is_ocean, sea_float, jnp.ones_like(sea_float))
    opened = jnp.full((1, lon_cols), lax.axis_index("lat") < lat_count - 1, jnp.float32)
    smem = pl.BlockSpec(memory_space=pltpu.SMEM)
    vmem = pl.BlockSpec(memory_space=pltpu.VMEM)
    anywhere = pl.BlockSpec(memory_space=pltpu.HBM)
    speeds, diffuse = velocity[0], diffusion[0]

    north_rims = pl.pallas_call(
        rim_kernel,
        out_shape=f32((steps * levels, LANES)),
        in_specs=[anywhere] * 2,
        scratch_shapes=[pltpu.VMEM((steps, levels, LANES), jnp.float32)] * 2 + [pltpu.SemaphoreType.DMA((2,))],
        compiler_params=params(),
        name="rim",
    )(speeds, diffuse)
    north_rims = lax.ppermute(
        north_rims, "lat", [(i, i + 1) for i in range(lat_count - 1)]
    ).reshape(steps, levels, LANES)

    sent = pl.pallas_call(
        functools.partial(pack_kernel, slots),
        out_shape=f32((owners * stride, LANES)),
        in_specs=[anywhere] * 3,
        scratch_shapes=[
            pltpu.VMEM((steps, count, width), jnp.float32),
            pltpu.VMEM((steps, count), jnp.int32),
            pltpu.VMEM((steps, count), jnp.int32),
            pltpu.SemaphoreType.DMA((steps + 2,)),
        ],
        compiler_params=params(),
        name="pack",
    )(innovations[0], obs_owner[0, :, :, 0], obs_cell[0])
    got = lax.all_to_all(
        sent.reshape(owners, 1, stride * LANES), ("lat", "lon"), split_axis=0, concat_axis=0, tiled=True
    ).reshape(owners * stride, LANES)

    table = f32((levels * SUBS, LANES))
    *tables, east_rims = pl.pallas_call(
        functools.partial(coefficient_kernel, steps, levels),
        out_shape=[table] * (4 * steps) + [f32((steps * SUBS, LANES))],
        compiler_params=params(),
        cost_estimate=pl.CostEstimate(flops=1 << 22, bytes_accessed=1 << 23, transcendentals=0),
        name="coefficients",
    )(
        speeds.reshape(steps * 2 * levels * SUBS, LANES),
        diffuse.reshape(steps * 2 * levels * SUBS, LANES),
        opened,
    )
    odd = jnp.stack([lax.axis_index("lat") % 2, lax.axis_index("lon") % 2]).astype(jnp.int32)
    edge_shapes = [
        f32((width * SUBS, LANES)),
        f32((width, LANES)),
        f32((width, LANES)),
        f32(((2 * fields + 1) * SUBS, LANES)),
        f32((fields * SUBS, LANES)),
    ]
    m, slab1, slab2, columns, low = pl.pallas_call(
        functools.partial(first_kernel, steps - 1, slots, fields, levels),
        out_shape=edge_shapes,
        in_specs=[smem] + [vmem] * 3,
        compiler_params=params(),
        name="first",
    )(odd, got, mask, east_rims)
    for step in reversed(range(steps)):
        last = step == 0
        operands = [
            mixing[0],
            air_sea,
            odd,
            m,
            *tables[4 * step : 4 * step + 4],
            north_rims[step],
            sea_float,
            mask,
            lax.ppermute(slab1, "lat", swaps("lat", 0, False)),
            lax.ppermute(slab2, "lat", swaps("lat", 1, False)),
            lax.ppermute(columns, "lon", swaps("lon", 1, True)),
            lax.ppermute(columns, "lon", swaps("lon", 0, True)),
            lax.ppermute(low, "comp", [(0, 1)]),
        ]
        if not last:
            operands.append(
                pl.pallas_call(
                    functools.partial(forcing_kernel, step - 1, slots, width),
                    out_shape=f32((width * SUBS, LANES)),
                    compiler_params=params(),
                    cost_estimate=pl.CostEstimate(
                        flops=2 * 3 * width * 2 * LANES * SUBS * LANES,
                        bytes_accessed=4 * (owners * stride * LANES + width * SUBS * LANES),
                        transcendentals=0,
                    ),
                    name="forcing",
                )(got)
            )
            operands.append(east_rims)
        result = pl.pallas_call(
            functools.partial(step_kernel, last, step, fields, levels),
            out_shape=edge_shapes[:1] if last else edge_shapes,
            in_specs=[smem] * 3 + [vmem] * (len(operands) - 3),
            compiler_params=params(),
            name="step",
        )(*operands)
        if last:
            m = result[0]
        else:
            m, slab1, slab2, columns, low = result
    return m.reshape(1, fields, levels, lat_rows, lon_cols)


def solution(mesh):
    return jax.shard_map(
        shards,
        mesh=mesh,
        in_specs=(
            P("comp", None, ("lat", "lon"), None),
            P("comp", None, ("lat", "lon"), None),
            P("comp", None, ("lat", "lon")),
            P("comp", None, None, None, "lat", "lon"),
            P("comp", None, None, None, "lat", "lon"),
            P("comp", None, None),
            P(),
            P("lat", "lon"),
        ),
        out_specs=P("comp", None, None, "lat", "lon"),
        check_vma=False,
    )
```

time: 162 us -> 178 us (1.099)
  Pallas kernels: 37.7 us -> 70 us
  starting transfers between devices: 74 us -> 48 us
  waiting for transfers between devices: 34.8 us -> 40 us
  local copies, waits for them, and re-layouts: 13.6 us -> 18.3 us
    pallas_call x4 -> x3, Pallas kernels: 20.9 us -> 61.3 us  [shards(): pl.pallas_call(functools.partial(step_kernel, last, step, fields, levels)...]
    ppermute x17 -> x16, starting transfers between devices: 58.6 us -> 32.6 us  [the longest x3 11.8 us: shards(): lax.ppermute(columns, 'lon', swaps('lon', 1, True))]
    all_to_all x1, waiting for transfers between devices: 0.01 us -> 22.7 us  [shards(): lax.all_to_all(sent.reshape(owners, 1, stride * LANES), ('lat', 'lon'), s...]
    ppermute x17 -> x16, waiting for transfers between devices: 34.8 us -> 17.3 us  [the longest x3 16.4 us: shards(): lax.ppermute(columns, 'lon', swaps('lon', 1, True))]
    pallas_call x1, Pallas kernels: 8.28 us -> 1.85 us  [shards(): pl.pallas_call(functools.partial(coefficient_kernel, steps, levels), out_...]
    unnamed x62 -> x54, local copies, waits for them, and re-layouts: 12.7 us -> 17.4 us
    pallas_call x1, Pallas kernels: 3.79 us -> 1.92 us  [shards(): pl.pallas_call(functools.partial(first_kernel, steps - 1, slots, fields,...]
  transfers between devices with their start and end apart: 18 -> 17, of which waited for: 4 -> 5; matrix products, arithmetic and copies ran while one was open for 1% -> 1% of each run, Pallas kernels for 12% -> 4%
where the time goes in v2:
time: 178 us; the launch traced here: 177 us
  Pallas kernels  70 us (39%)
  starting transfers between devices  48 us (27%)
  waiting for transfers between devices  40 us (22%)
  local copies, waits for them, and re-layouts  18.3 us (10%)
    pallas_call x3, Pallas kernels, shards(): pl.pallas_call(functools.partial(step_kernel, last, step, fields, levels)...  61.3 us
    all_to_all x1, waiting for transfers between devices, shards(): lax.all_to_all(sent.reshape(owners, 1, stride * LANES), ('lat', 'lon'), s...  22.7 us
    unnamed x54, local copies, waits for them, and re-layouts  17.4 us
    ppermute x3, waiting for transfers between devices, shards(): lax.ppermute(columns, 'lon', swaps('lon', 1, True))  16.4 us
    all_to_all x1, starting transfers between devices, shards(): lax.all_to_all(sent.reshape(owners, 1, stride * LANES), ('lat', 'lon'), s...  15.5 us
    ppermute x3, starting transfers between devices, shards(): lax.ppermute(columns, 'lon', swaps('lon', 1, True))  11.8 us
    ppermute x3, starting transfers between devices, shards(): lax.ppermute(slab2, 'lat', swaps('lat', 1, False))  11.5 us
    ppermute x3, starting transfers between devices, shards(): lax.ppermute(low, 'comp', [(0, 1)])  3.84 us
  transfers between devices with their start and end apart: 17, of which 5 were waited for; matrix products, arithmetic and copies ran while one was open for 1% of the time, Pallas kernels for 4%

profile of v2, /device:TPU:8, one launch (start us, length us, event | category | flops | bytes accessed | tf_op | source)
XLA Modules:
  0.0 176.8 jit_solution(2839395516919537710)
XLA Ops:
  1.4 1.1 copy-done.4
  2.5 2.4 %pack.1 = f32[3200,128]{1,0:T(8,128)} custom-call(f32[3,128,512]{2,1,0:T(8,128)S(1)} %bitcast.24, s32[3,128]{1,0:T(4,128)S(1)} %bitcast.29, s32[3,128]{1,0:T(4,128)S(1)} %bitcast.28), custom_call_target="tpu_custom_call" | custom-call | tf_op jit(solution)/shard_map/pack/pallas_call | solution.py:376
  4.9 15.5 %all-to-all-start = ((f32[128,1,3200]{2,1,0:T(1,128)}), f32[128,1,3200]{2,1,0:T(1,128)S(1)}, u32[]{:S(2)}, u32[]{:S(2)}) async-start(f32[128,1,3200]{2,1,0:T(1,128)} %bitcast.4), calls=%async_computation | async-start | bytes 3276800 | tf_op jit(solution)/shard_map/all_to_all | solution.py:389
  20.4 1.9 %copy-done = f32[1,3,2,128,8,128]{5,4,3,2,1,0:T(8,128)S(1)} copy-done((f32[1,3,2,128,8,128]{5,4,3,2,1,0:T(8,128)S(1)}, f32[1,3,2,128,8,128]{5,4,3,2,1,0:T(8,128)}, u32[]{:S(2)}) %copy-start) | copy-done | bytes 3145752
  22.3 1.9 %copy-done.2 = f32[1,3,2,128,8,128]{5,4,3,2,1,0:T(8,128)S(1)} copy-done((f32[1,3,2,128,8,128]{5,4,3,2,1,0:T(8,128)S(1)}, f32[1,3,2,128,8,128]{5,4,3,2,1,0:T(8,128)}, u32[]{:S(2)}) %copy-start.2) | copy-done | bytes 3145752
  24.5 3.4 %collective-permute-start = (f32[384,128]{1,0:T(8,128)S(1)}, f32[384,128]{1,0:T(8,128)}, u32[]{:S(2)}, u32[]{:S(2)}) collective-permute-start(f32[384,128]{1,0:T(8,128)S(1)} %rim.1), channel_id=1, source_target_pairs={{0,8},{8,16},{16,24},{24,32},{32,40},{40,48},{48,56},{56,64},{64,7... | collective-permute-start | bytes 589832 | tf_op jit(solution)/shard_map/ppermute | solution.py:372
  28.0 1.9 %copy-done.1 = f32[1,3,2,128,8,128]{5,4,3,2,1,0:T(8,128)S(1)} copy-done((f32[1,3,2,128,8,128]{5,4,3,2,1,0:T(8,128)S(1)}, f32[1,3,2,128,8,128]{5,4,3,2,1,0:T(8,128)}, u32[]{:S(2)}) %copy-start.1) | copy-done | bytes 3145752
  29.9 1.9 %copy-done.3 = f32[1,3,2,128,8,128]{5,4,3,2,1,0:T(8,128)S(1)} copy-done((f32[1,3,2,128,8,128]{5,4,3,2,1,0:T(8,128)S(1)}, f32[1,3,2,128,8,128]{5,4,3,2,1,0:T(8,128)}, u32[]{:S(2)}) %copy-start.3) | copy-done | bytes 3145752
  31.8 1.9 %coefficients.1 = (f32[1024,128]{1,0:T(8,128)S(1)}, f32[1024,128]{1,0:T(8,128)S(1)}, f32[1024,128]{1,0:T(8,128)S(1)}, f32[1024,128]{1,0:T(8,128)S(1)}, f32[1024,...) custom-call(f32[6144,128]{1,0:T(8,128)S(1)} %bitcast.21, ...), custom_call_target="tpu_custom_call" | custom-call | flops 4194304 | bytes 8388608 | tf_op jit(solution)/shard_map/coefficients/pallas_call | solution.py:394
  34.4 0.8 copy-done.7
  35.2 0.8 copy-done.9
  41.0 22.7 %all-to-all-done = f32[128,1,3200]{2,1,0:T(1,128)S(1)} async-done(((f32[128,1,3200]{2,1,0:T(1,128)}), f32[128,1,3200]{2,1,0:T(1,128)S(1)}, u32[]{:S(2)}, u32[]{:S(2)}) %all-to-all-start) | async-done | bytes 1638432 | tf_op jit(solution)/shard_map/all_to_all | solution.py:389
  63.7 1.9 %first.1 = (f32[4096,128]{1,0:T(8,128)S(1)}, f32[512,128]{1,0:T(8,128)S(1)}, f32[512,128]{1,0:T(8,128)S(1)}, f32[72,128]{1,0:T(8,128)S(1)}, f32[32,128]{1,0:T(8,128)S(1)}) custom-call(s32[2]{0:T(128)S(1)} %pad_add_fusion.odd_ref, f32[3200,128]{1,0:T(8,128)S(1)} %bitcast.17, f32[8,128]{1,0:T(8,128)S(1)} %broadcast_select_fusion.mask_ref, ...), custom_call_target="tpu_custom_call" | custom-call | tf_op jit(solution)/shard_map/first/pallas_call | solution.py:413
  65.8 4.7 %collective-permute-start.2 = (f32[512,128]{1,0:T(8,128)S(1)}, f32[512,128]{1,0:T(8,128)S(1)}, u32[]{:S(2)}, u32[]{:S(2)}) collective-permute-start(f32[512,128]{1,0:T(8,128)S(1)} %get-tuple-element.40), channel_id=1, source_target_pairs={{8,16},{16,8},{24,32},{32,24},{40,48},{48,40},{56,64},{64,56},{72,... | collective-permute-start | bytes 786440 | tf_op jit(solution)/shard_map/ppermute | solution.py:432
  70.5 0.9 fusion
  71.4 4.1 %collective-permute-start.3 = (f32[72,128]{1,0:T(8,128)S(1)}, f32[72,128]{1,0:T(8,128)S(1)}, u32[]{:S(2)}, u32[]{:S(2)}) collective-permute-start(f32[72,128]{1,0:T(8,128)S(1)} %get-tuple-element.41), channel_id=1, source_target_pairs={{1,2},{2,1},{3,4},{4,3},{5,6},{6,5},{7,0},{0,7},{9,10},{10,9},{11,... | collective-permute-start | bytes 110600 | tf_op jit(solution)/shard_map/ppermute | solution.py:433
  75.5 1.3 collective-permute-start.5
  76.8 1.1 forcing.2.rest_0_
  77.9 3.7 %collective-permute-done.3.from_column1_ref = f32[72,128]{1,0:T(8,128)S(1)} collective-permute-done((f32[72,128]{1,0:T(8,128)S(1)}, f32[72,128]{1,0:T(8,128)S(1)}, u32[]{:S(2)}, u32[]{:S(2)}) %collective-permute-start.3) | collective-permute-done | bytes 36896 | tf_op jit(solution)/shard_map/ppermute | solution.py:433
  81.7 28.6 %step.3 = (f32[4096,128]{1,0:T(8,128)S(1)}, f32[512,128]{1,0:T(8,128)S(1)}, f32[512,128]{1,0:T(8,128)S(1)}, f32[72,128]{1,0:T(8,128)S(1)}, f32[32,128]{1,0:T(8,128)S(1)}) custom-call(f32[4,4]{1,0:T(4,128)S(1)} %bitcast.25, f32[4,4]{1,0:T(4,128)S(1)} %copy-done.24, s32[2]{0:T(128)S(1)} %pad_add_fusion.odd_ref, f32[4096,128]{1,0:T(8,128)S(1)} %get-tuple-element.34.m_ref, ...), custom_call_target="tpu_custom_call" | custom-call | tf_op jit(solution)/shard_map/step/pallas_call | solution.py:452
  110.4 1.9 %collective-permute-start.6 = (f32[512,128]{1,0:T(8,128)S(1)}, f32[512,128]{1,0:T(8,128)S(1)}, u32[]{:S(2)}, u32[]{:S(2)}) collective-permute-start(f32[512,128]{1,0:T(8,128)S(1)} %get-tuple-element.48), channel_id=1, source_target_pairs={{0,8},{8,0},{16,24},{24,16},{32,40},{40,32},{48,56},{56,48},{64,72... | collective-permute-start | bytes 786440 | tf_op jit(solution)/shard_map/ppermute | solution.py:431
  112.2 3.1 %collective-permute-start.7 = (f32[512,128]{1,0:T(8,128)S(1)}, f32[512,128]{1,0:T(8,128)S(1)}, u32[]{:S(2)}, u32[]{:S(2)}) collective-permute-start(f32[512,128]{1,0:T(8,128)S(1)} %get-tuple-element.49), channel_id=1, source_target_pairs={{8,16},{16,8},{24,32},{32,24},{40,48},{48,40},{56,64},{64,56},{72,... | collective-permute-start | bytes 786440 | tf_op jit(solution)/shard_map/ppermute | solution.py:432
  115.3 3.7 %collective-permute-start.8 = (f32[72,128]{1,0:T(8,128)S(1)}, f32[72,128]{1,0:T(8,128)S(1)}, u32[]{:S(2)}, u32[]{:S(2)}) collective-permute-start(f32[72,128]{1,0:T(8,128)S(1)} %get-tuple-element.50), channel_id=1, source_target_pairs={{1,2},{2,1},{3,4},{4,3},{5,6},{6,5},{7,0},{0,7},{9,10},{10,9},{11,... | collective-permute-start | bytes 110600 | tf_op jit(solution)/shard_map/ppermute | solution.py:433
  119.1 1.3 collective-permute-start.10
  120.4 1.1 forcing.3.rest_0_
  121.5 5.8 %collective-permute-done.8.from_column1_ref = f32[72,128]{1,0:T(8,128)S(1)} collective-permute-done((f32[72,128]{1,0:T(8,128)S(1)}, f32[72,128]{1,0:T(8,128)S(1)}, u32[]{:S(2)}, u32[]{:S(2)}) %collective-permute-start.8) | collective-permute-done | bytes 36896 | tf_op jit(solution)/shard_map/ppermute | solution.py:433
  127.4 28.6 %step.4 = (f32[4096,128]{1,0:T(8,128)S(1)}, f32[512,128]{1,0:T(8,128)S(1)}, f32[512,128]{1,0:T(8,128)S(1)}, f32[72,128]{1,0:T(8,128)S(1)}, f32[32,128]{1,0:T(8,128)S(1)}) custom-call(f32[4,4]{1,0:T(4,128)S(1)} %bitcast.26, f32[4,4]{1,0:T(4,128)S(1)} %copy-done.24, s32[2]{0:T(128)S(1)} %pad_add_fusion.odd_ref, f32[4096,128]{1,0:T(8,128)S(1)} %get-tuple-element.43.m_ref, ...), custom_call_target="tpu_custom_call" | custom-call | tf_op jit(solution)/shard_map/step/pallas_call | solution.py:452
  156.1 3.6 %collective-permute-start.12 = (f32[512,128]{1,0:T(8,128)S(1)}, f32[512,128]{1,0:T(8,128)S(1)}, u32[]{:S(2)}, u32[]{:S(2)}) collective-permute-start(f32[512,128]{1,0:T(8,128)S(1)} %get-tuple-element.58), channel_id=1, source_target_pairs={{8,16},{16,8},{24,32},{32,24},{40,48},{48,40},{56,64},{64,56},{72,... | collective-permute-start | bytes 786440 | tf_op jit(solution)/shard_map/ppermute | solution.py:432
  159.7 4.0 %collective-permute-start.13 = (f32[72,128]{1,0:T(8,128)S(1)}, f32[72,128]{1,0:T(8,128)S(1)}, u32[]{:S(2)}, u32[]{:S(2)}) collective-permute-start(f32[72,128]{1,0:T(8,128)S(1)} %get-tuple-element.59), channel_id=1, source_target_pairs={{1,2},{2,1},{3,4},{4,3},{5,6},{6,5},{7,0},{0,7},{9,10},{10,9},{11,... | collective-permute-start | bytes 110600 | tf_op jit(solution)/shard_map/ppermute | solution.py:433
  163.7 1.3 collective-permute-start.15
  165.8 6.9 %collective-permute-done.13.from_column1_ref = f32[72,128]{1,0:T(8,128)S(1)} collective-permute-done((f32[72,128]{1,0:T(8,128)S(1)}, f32[72,128]{1,0:T(8,128)S(1)}, u32[]{:S(2)}, u32[]{:S(2)}) %collective-permute-start.13) | collective-permute-done | bytes 36896 | tf_op jit(solution)/shard_map/ppermute | solution.py:433
  172.8 4.0 %step.5 = f32[4096,128]{1,0:T(8,128)} custom-call(f32[4,4]{1,0:T(4,128)S(1)} %bitcast.27, f32[4,4]{1,0:T(4,128)S(1)} %copy-done.24, s32[2]{0:T(128)S(1)} %pad_add_fusion.odd_ref, f32[4096,128]{1,0:T(8,128)S(1)} %get-tuple-element.52.m_ref, f32[1024,128]{1,0:T(8,128)S(1)} %get-tuple-element.53.up_e_ref, f32[1024,128]{1,0:T(8,128)S(1)} %get-tuple-element.54.down_w_ref, ...), custom_call_target="tpu_custom_call" | custom-call | tf_op jit(solution)/shard_map/step/pallas_call | solution.py:452
  (70 shorter events, 8.5 us)
Async XLA Ops:
  4.9 58.8 %all-to-all-start = ((f32[128,1,3200]{2,1,0:T(1,128)}), f32[128,1,3200]{2,1,0:T(1,128)S(1)}, u32[]{:S(2)}, u32[]{:S(2)}) async-start(f32[128,1,3200]{2,1,0:T(1,128)} %bitcast.4), calls=%async_computation | async-start | bytes 3276800 | tf_op jit(solution)/shard_map/all_to_all | solution.py:389
  20.4 1.9 %copy-start = (f32[1,3,2,128,8,128]{5,4,3,2,1,0:T(8,128)S(1)}, f32[1,3,2,128,8,128]{5,4,3,2,1,0:T(8,128)}, u32[]{:S(2)}) copy-start(f32[1,3,2,128,8,128]{5,4,3,2,1,0:T(8,128)} %param.11) | copy-start | bytes 9437188
  22.3 1.9 %copy-start.2 = (f32[1,3,2,128,8,128]{5,4,3,2,1,0:T(8,128)S(1)}, f32[1,3,2,128,8,128]{5,4,3,2,1,0:T(8,128)}, u32[]{:S(2)}) copy-start(f32[1,3,2,128,8,128]{5,4,3,2,1,0:T(8,128)} %param.12) | copy-start | bytes 9437188
  24.2 3.8 %copy-start.25 = (s32[8,128]{1,0:T(8,128)S(1)}, s32[8,128]{1,0:T(8,128)}, u32[]{:S(2)}) copy-start(s32[8,128]{1,0:T(8,128)} %param.15) | copy-start | bytes 12292
  24.5 46.0 %collective-permute-start = (f32[384,128]{1,0:T(8,128)S(1)}, f32[384,128]{1,0:T(8,128)}, u32[]{:S(2)}, u32[]{:S(2)}) collective-permute-start(f32[384,128]{1,0:T(8,128)S(1)} %rim.1), channel_id=1, source_target_pairs={{0,8},{8,16},{16,24},{24,32},{32,40},{40,48},{48,56},{56,64},{64,7... | collective-permute-start | bytes 589832 | tf_op jit(solution)/shard_map/ppermute | solution.py:372
  28.0 1.9 %copy-start.1 = (f32[1,3,2,128,8,128]{5,4,3,2,1,0:T(8,128)S(1)}, f32[1,3,2,128,8,128]{5,4,3,2,1,0:T(8,128)}, u32[]{:S(2)}) copy-start(f32[1,3,2,128,8,128]{5,4,3,2,1,0:T(8,128)} %param.11) | copy-start | bytes 9437188
  65.6 16.0 %copy-start.16 = (f32[1024,128]{1,0:T(8,128)S(1)}, f32[1024,128]{1,0:T(8,128)}, u32[]{:S(2)}) copy-start(f32[1024,128]{1,0:T(8,128)} %copy-done.15) | copy-start | bytes 1572868
  65.6 16.0 %copy-start.18 = (f32[1024,128]{1,0:T(8,128)S(1)}, f32[1024,128]{1,0:T(8,128)}, u32[]{:S(2)}) copy-start(f32[1024,128]{1,0:T(8,128)} %copy-done.17) | copy-start | bytes 1572868
  65.6 16.0 %copy-start.20 = (f32[1024,128]{1,0:T(8,128)S(1)}, f32[1024,128]{1,0:T(8,128)}, u32[]{:S(2)}) copy-start(f32[1024,128]{1,0:T(8,128)} %copy-done.19) | copy-start | bytes 1572868
  65.6 16.0 %copy-start.22 = (f32[1024,128]{1,0:T(8,128)S(1)}, f32[1024,128]{1,0:T(8,128)}, u32[]{:S(2)}) copy-start(f32[1024,128]{1,0:T(8,128)} %copy-done.21) | copy-start | bytes 1572868
  65.6 16.0 %copy-start.23 = (f32[1,4,4]{2,1,0:T(4,128)S(1)}, f32[1,4,4]{2,1,0:T(4,128)}, u32[]{:S(2)}) copy-start(f32[1,4,4]{2,1,0:T(4,128)} %param.13) | copy-start | bytes 196
  65.6 16.0 %copy-start.24 = (f32[4,4]{1,0:T(4,128)S(1)}, f32[4,4]{1,0:T(4,128)}, u32[]{:S(2)}) copy-start(f32[4,4]{1,0:T(4,128)} %air_ref.5) | copy-start | bytes 196
  65.7 15.9 %collective-permute-start.1 = (f32[512,128]{1,0:T(8,128)S(1)}, f32[512,128]{1,0:T(8,128)S(1)}, u32[]{:S(2)}, u32[]{:S(2)}) collective-permute-start(f32[512,128]{1,0:T(8,128)S(1)} %get-tuple-element.39), channel_id=1, source_target_pairs={{0,8},{8,0},{16,24},{24,16},{32,40},{40,32},{48,56},{56,48},{64,72... | collective-permute-start | bytes 786440 | tf_op jit(solution)/shard_map/ppermute | solution.py:431
  65.8 15.8 %collective-permute-start.2 = (f32[512,128]{1,0:T(8,128)S(1)}, f32[512,128]{1,0:T(8,128)S(1)}, u32[]{:S(2)}, u32[]{:S(2)}) collective-permute-start(f32[512,128]{1,0:T(8,128)S(1)} %get-tuple-element.40), channel_id=1, source_target_pairs={{8,16},{16,8},{24,32},{32,24},{40,48},{48,40},{56,64},{64,56},{72,... | collective-permute-start | bytes 786440 | tf_op jit(solution)/shard_map/ppermute | solution.py:432
  71.4 10.2 %collective-permute-start.3 = (f32[72,128]{1,0:T(8,128)S(1)}, f32[72,128]{1,0:T(8,128)S(1)}, u32[]{:S(2)}, u32[]{:S(2)}) collective-permute-start(f32[72,128]{1,0:T(8,128)S(1)} %get-tuple-element.41), channel_id=1, source_target_pairs={{1,2},{2,1},{3,4},{4,3},{5,6},{6,5},{7,0},{0,7},{9,10},{10,9},{11,... | collective-permute-start | bytes 110600 | tf_op jit(solution)/shard_map/ppermute | solution.py:433
  75.5 6.1 %collective-permute-start.4 = (f32[72,128]{1,0:T(8,128)S(1)}, f32[72,128]{1,0:T(8,128)S(1)}, u32[]{:S(2)}, u32[]{:S(2)}) collective-permute-start(f32[72,128]{1,0:T(8,128)S(1)} %get-tuple-element.41), channel_id=1, source_target_pairs={{0,1},{1,0},{2,3},{3,2},{4,5},{5,4},{6,7},{7,6},{8,9},{9,8},{10,11... | collective-permute-start | bytes 110600 | tf_op jit(solution)/shard_map/ppermute | solution.py:434
  75.5 2.4 %collective-permute-start.5 = (f32[32,128]{1,0:T(8,128)S(1)}, f32[32,128]{1,0:T(8,128)S(1)}, u32[]{:S(2)}, u32[]{:S(2)}) collective-permute-start(f32[32,128]{1,0:T(8,128)S(1)} %get-tuple-element.42), channel_id=1, source_target_pairs={{0,128},{1,129},{2,130},{3,131},{4,132},{5,133},{6,134},{7,135},{8... | collective-permute-start | bytes 49160 | tf_op jit(solution)/shard_map/ppermute | solution.py:435
  110.3 17.0 %copy-start.8 = (f32[1024,128]{1,0:T(8,128)S(1)}, f32[1024,128]{1,0:T(8,128)}, u32[]{:S(2)}) copy-start(f32[1024,128]{1,0:T(8,128)} %copy-done.7) | copy-start | bytes 1572868
  110.3 17.0 %copy-start.10 = (f32[1024,128]{1,0:T(8,128)S(1)}, f32[1024,128]{1,0:T(8,128)}, u32[]{:S(2)}) copy-start(f32[1024,128]{1,0:T(8,128)} %copy-done.9) | copy-start | bytes 1572868
  110.3 17.0 %copy-start.12 = (f32[1024,128]{1,0:T(8,128)S(1)}, f32[1024,128]{1,0:T(8,128)}, u32[]{:S(2)}) copy-start(f32[1024,128]{1,0:T(8,128)} %copy-done.11) | copy-start | bytes 1572868
  110.4 17.0 %copy-start.14 = (f32[1024,128]{1,0:T(8,128)S(1)}, f32[1024,128]{1,0:T(8,128)}, u32[]{:S(2)}) copy-start(f32[1024,128]{1,0:T(8,128)} %copy-done.13) | copy-start | bytes 1572868
  110.4 16.9 %collective-permute-start.6 = (f32[512,128]{1,0:T(8,128)S(1)}, f32[512,128]{1,0:T(8,128)S(1)}, u32[]{:S(2)}, u32[]{:S(2)}) collective-permute-start(f32[512,128]{1,0:T(8,128)S(1)} %get-tuple-element.48), channel_id=1, source_target_pairs={{0,8},{8,0},{16,24},{24,16},{32,40},{40,32},{48,56},{56,48},{64,72... | collective-permute-start | bytes 786440 | tf_op jit(solution)/shard_map/ppermute | solution.py:431
  112.2 15.1 %collective-permute-start.7 = (f32[512,128]{1,0:T(8,128)S(1)}, f32[512,128]{1,0:T(8,128)S(1)}, u32[]{:S(2)}, u32[]{:S(2)}) collective-permute-start(f32[512,128]{1,0:T(8,128)S(1)} %get-tuple-element.49), channel_id=1, source_target_pairs={{8,16},{16,8},{24,32},{32,24},{40,48},{48,40},{56,64},{64,56},{72,... | collective-permute-start | bytes 786440 | tf_op jit(solution)/shard_map/ppermute | solution.py:432
  115.3 11.9 %collective-permute-start.8 = (f32[72,128]{1,0:T(8,128)S(1)}, f32[72,128]{1,0:T(8,128)S(1)}, u32[]{:S(2)}, u32[]{:S(2)}) collective-permute-start(f32[72,128]{1,0:T(8,128)S(1)} %get-tuple-element.50), channel_id=1, source_target_pairs={{1,2},{2,1},{3,4},{4,3},{5,6},{6,5},{7,0},{0,7},{9,10},{10,9},{11,... | collective-permute-start | bytes 110600 | tf_op jit(solution)/shard_map/ppermute | solution.py:433
  119.1 8.2 %collective-permute-start.9 = (f32[72,128]{1,0:T(8,128)S(1)}, f32[72,128]{1,0:T(8,128)S(1)}, u32[]{:S(2)}, u32[]{:S(2)}) collective-permute-start(f32[72,128]{1,0:T(8,128)S(1)} %get-tuple-element.50), channel_id=1, source_target_pairs={{0,1},{1,0},{2,3},{3,2},{4,5},{5,4},{6,7},{7,6},{8,9},{9,8},{10,11... | collective-permute-start | bytes 110600 | tf_op jit(solution)/shard_map/ppermute | solution.py:434
  119.1 2.4 %collective-permute-start.10 = (f32[32,128]{1,0:T(8,128)S(1)}, f32[32,128]{1,0:T(8,128)S(1)}, u32[]{:S(2)}, u32[]{:S(2)}) collective-permute-start(f32[32,128]{1,0:T(8,128)S(1)} %get-tuple-element.51), channel_id=1, source_target_pairs={{0,128},{1,129},{2,130},{3,131},{4,132},{5,133},{6,134},{7,135},{8... | collective-permute-start | bytes 49160 | tf_op jit(solution)/shard_map/ppermute | solution.py:435
  127.4 45.4 %copy-start.6 = (f32[1024,128]{1,0:T(8,128)S(1)}, f32[1024,128]{1,0:T(8,128)}, u32[]{:S(2)}) copy-start(f32[1024,128]{1,0:T(8,128)} %copy-done.5) | copy-start | bytes 1572868
  156.0 16.8 %collective-permute-start.11 = (f32[512,128]{1,0:T(8,128)S(1)}, f32[512,128]{1,0:T(8,128)S(1)}, u32[]{:S(2)}, u32[]{:S(2)}) collective-permute-start(f32[512,128]{1,0:T(8,128)S(1)} %get-tuple-element.57), channel_id=1, source_target_pairs={{0,8},{8,0},{16,24},{24,16},{32,40},{40,32},{48,56},{56,48},{64,72... | collective-permute-start | bytes 786440 | tf_op jit(solution)/shard_map/ppermute | solution.py:431
  156.1 16.7 %collective-permute-start.12 = (f32[512,128]{1,0:T(8,128)S(1)}, f32[512,128]{1,0:T(8,128)S(1)}, u32[]{:S(2)}, u32[]{:S(2)}) collective-permute-start(f32[512,128]{1,0:T(8,128)S(1)} %get-tuple-element.58), channel_id=1, source_target_pairs={{8,16},{16,8},{24,32},{32,24},{40,48},{48,40},{56,64},{64,56},{72,... | collective-permute-start | bytes 786440 | tf_op jit(solution)/shard_map/ppermute | solution.py:432
  159.7 13.0 %collective-permute-start.13 = (f32[72,128]{1,0:T(8,128)S(1)}, f32[72,128]{1,0:T(8,128)S(1)}, u32[]{:S(2)}, u32[]{:S(2)}) collective-permute-start(f32[72,128]{1,0:T(8,128)S(1)} %get-tuple-element.59), channel_id=1, source_target_pairs={{1,2},{2,1},{3,4},{4,3},{5,6},{6,5},{7,0},{0,7},{9,10},{10,9},{11,... | collective-permute-start | bytes 110600 | tf_op jit(solution)/shard_map/ppermute | solution.py:433
  163.7 9.0 %collective-permute-start.14 = (f32[72,128]{1,0:T(8,128)S(1)}, f32[72,128]{1,0:T(8,128)S(1)}, u32[]{:S(2)}, u32[]{:S(2)}) collective-permute-start(f32[72,128]{1,0:T(8,128)S(1)} %get-tuple-element.59), channel_id=1, source_target_pairs={{0,1},{1,0},{2,3},{3,2},{4,5},{5,4},{6,7},{7,6},{8,9},{9,8},{10,11... | collective-permute-start | bytes 110600 | tf_op jit(solution)/shard_map/ppermute | solution.py:434
  163.7 2.1 %collective-permute-start.15 = (f32[32,128]{1,0:T(8,128)S(1)}, f32[32,128]{1,0:T(8,128)S(1)}, u32[]{:S(2)}, u32[]{:S(2)}) collective-permute-start(f32[32,128]{1,0:T(8,128)S(1)} %get-tuple-element.60), channel_id=1, source_target_pairs={{0,128},{1,129},{2,130},{3,131},{4,132},{5,133},{6,134},{7,135},{8... | collective-permute-start | bytes 49160 | tf_op jit(solution)/shard_map/ppermute | solution.py:435
  (11 other events, 10.3 us)

commit v3 on v2

--- a/solution.py
+++ b/solution.py
@@ -88,30 +88,25 @@
     )
 
 
-def columns_start(fields):
-    zero = jnp.zeros((SUBS, LANES), jnp.float32)
-    return [zero] * (2 * fields)
-
-
-def columns_insert(cols, f, at, plane):
+def columns_store(m_ref, rim, column_ref, fields, levels):
     lane = lax.broadcasted_iota(jnp.int32, (SUBS, LANES), 1)
-    turned = plane if at == 0 else pltpu.roll(plane, at, 1)
-    here = (lane == at) | (lane == (at - 1) % LANES)
-    half = 2 * f + at % 2
-    cols[half] = jnp.where(here, turned, cols[half])
+    even = lane % 2 == 0
+    for f in range(fields):
+        halves = [jnp.zeros((SUBS, LANES), jnp.float32)] * 2
+        for group in range(levels // SUBS):
+            for y in range(SUBS):
+                at = group * SUBS + y
+                plane = m_ref[rows_of((y * fields + f) * levels, group), :]
+                turned = plane if at == 0 else pltpu.roll(plane, at, 1)
+                here = (lane == at) | (lane == (at - 1) % LANES)
+                halves[at % 2] = jnp.where(here, turned, halves[at % 2])
+        column_ref[f * SUBS : (f + 1) * SUBS, :] = jnp.where(even, halves[0], halves[1])
+        column_ref[(fields + f) * SUBS : (fields + f + 1) * SUBS, :] = jnp.where(even, halves[1], halves[0])
+    column_ref[2 * fields * SUBS :, :] = rim
 
 
 def columns_turn(cols, groups):
     return [pltpu.roll(c, LANES - groups * SUBS, 1) for c in cols]
-
-
-def columns_store(cols, rim, column_ref, fields):
-    even = lax.broadcasted_iota(jnp.int32, (SUBS, LANES), 1) % 2 == 0
-    for f in range(fields):
-        a, b = cols[2 * f], cols[2 * f + 1]
-        column_ref[f * SUBS : (f + 1) * SUBS, :] = jnp.where(even, a, b)
-        column_ref[(fields + f) * SUBS : (fields + f + 1) * SUBS, :] = jnp.where(even, b, a)
-    column_ref[2 * fields * SUBS :, :] = rim
 
 
 def columns_load(lon_even, first_ref, second_ref, fields):
@@ -167,12 +162,7 @@
     for y in range(SUBS):
         m_ref[y * width : (y + 1) * width, :] = out[:, y * LANES : (y + 1) * LANES] * mask_ref[y : y + 1, :]
     slabs_store(parity(odd_ref, 0), m_ref, slab1_ref, slab2_ref, width)
-    cols = columns_start(fields)
-    for group in range(levels // SUBS):
-        for f in range(fields):
-            for y in range(SUBS):
-                columns_insert(cols, f, group * SUBS + y, m_ref[rows_of(y * width + f * levels, group), :])
-    columns_store(cols, rim_ref[step * SUBS : (step + 1) * SUBS, :], column_ref, fields)
+    columns_store(m_ref, rim_ref[step * SUBS : (step + 1) * SUBS, :], column_ref, fields, levels)
     low_store(m_ref, low_ref, fields, levels)
 
 
@@ -264,8 +254,7 @@
             total = total + air_ref[f, g] * from_low_ref[f * SUBS : (f + 1) * SUBS, :]
         coupled.append(sea * total)
 
-    def batch_step(group0, halos, cols):
-        cols = list(cols)
+    def batch_step(group0, halos):
         for u in range(batch):
             group = group0 + u
             for y in range(SUBS):
@@ -309,19 +298,17 @@
                     rows = rows_of(y * width + g * levels, group)
                     result = (result + f_ref[rows, :]) * mask_ref[y : y + 1, :]
                     out_ref[rows, :] = result
-                    columns_insert(cols, g, at, result)
-        return columns_turn(halos, batch), columns_turn(cols, batch)
+        return columns_turn(halos, batch)
 
     halos = columns_load(lon_even, from_column1_ref, from_column2_ref, fields)
-    halos, cols = batch_step(0, halos, [] if last else columns_start(fields))
-
-    def body(i, carry):
-        halos, cols = batch_step(i * batch, list(carry[0]), list(carry[1]))
-        return tuple(halos), tuple(cols)
-
-    halos, cols = lax.fori_loop(1, levels // (SUBS * batch), body, (tuple(halos), tuple(cols)))
+    halos = batch_step(0, halos)
+
+    def body(i, halos):
+        return tuple(batch_step(i * batch, list(halos)))
+
+    lax.fori_loop(1, levels // (SUBS * batch), body, tuple(halos))
     if not last:
-        columns_store(cols, rim_ref[(step - 1) * SUBS : step * SUBS, :], column_ref, fields)
+        columns_store(out_ref, rim_ref[(step - 1) * SUBS : step * SUBS, :], column_ref, fields, levels)
         slabs_store(lat_even, out_ref, slab1_ref, slab2_ref, width)
         low_store(out_ref, low_ref, fields, levels)
 

time: 178 us -> 127 us (0.71)
  Pallas kernels: 70 us -> 19.7 us
    pallas_call x3, Pallas kernels: 61.3 us -> 11 us  [shards(): pl.pallas_call(functools.partial(step_kernel, last, step, fields, levels)...]
  transfers between devices with their start and end apart: 17 -> 17, of which waited for: 5 -> 5; matrix products, arithmetic and copies ran while one was open for 1% -> 1% of each run, Pallas kernels for 4% -> 5%
where the time goes in v3:
time: 127 us; the launch traced here: 126 us
  starting transfers between devices  47.9 us (38%)
  waiting for transfers between devices  40 us (31%)
  Pallas kernels  19.7 us (16%)
  local copies, waits for them, and re-layouts  18.3 us (14%)
    all_to_all x1, waiting for transfers between devices, shards(): lax.all_to_all(sent.reshape(owners, 1, stride * LANES), ('lat', 'lon'), s...  22.7 us
    unnamed x54, local copies, waits for them, and re-layouts  17.4 us
    ppermute x3, waiting for transfers between devices, shards(): lax.ppermute(columns, 'lon', swaps('lon', 1, True))  16.4 us
    all_to_all x1, starting transfers between devices, shards(): lax.all_to_all(sent.reshape(owners, 1, stride * LANES), ('lat', 'lon'), s...  15.5 us
    ppermute x3, starting transfers between devices, shards(): lax.ppermute(columns, 'lon', swaps('lon', 1, True))  11.8 us
    ppermute x3, starting transfers between devices, shards(): lax.ppermute(slab2, 'lat', swaps('lat', 1, False))  11.5 us
    pallas_call x3, Pallas kernels, shards(): pl.pallas_call(functools.partial(step_kernel, last, step, fields, levels)...  11 us
    ppermute x3, starting transfers between devices, shards(): lax.ppermute(low, 'comp', [(0, 1)])  3.84 us
  transfers between devices with their start and end apart: 17, of which 5 were waited for; matrix products, arithmetic and copies ran while one was open for 1% of the time, Pallas kernels for 5%

profile of v3, /device:TPU:8, one launch (start us, length us, event | category | flops | bytes accessed | tf_op | source)
XLA Modules:
  0.0 126.4 jit_solution(14679094567421921782)
XLA Ops:
  1.4 1.1 copy-done.4
  2.5 2.4 %pack.1 = f32[3200,128]{1,0:T(8,128)} custom-call(f32[3,128,512]{2,1,0:T(8,128)S(1)} %bitcast.24, s32[3,128]{1,0:T(4,128)S(1)} %bitcast.29, s32[3,128]{1,0:T(4,128)S(1)} %bitcast.28), custom_call_target="tpu_custom_call" | custom-call | tf_op jit(solution)/shard_map/pack/pallas_call | solution.py:363
  4.9 15.5 %all-to-all-start = ((f32[128,1,3200]{2,1,0:T(1,128)}), f32[128,1,3200]{2,1,0:T(1,128)S(1)}, u32[]{:S(2)}, u32[]{:S(2)}) async-start(f32[128,1,3200]{2,1,0:T(1,128)} %bitcast.4), calls=%async_computation | async-start | bytes 3276800 | tf_op jit(solution)/shard_map/all_to_all | solution.py:376
  20.4 1.9 %copy-done = f32[1,3,2,128,8,128]{5,4,3,2,1,0:T(8,128)S(1)} copy-done((f32[1,3,2,128,8,128]{5,4,3,2,1,0:T(8,128)S(1)}, f32[1,3,2,128,8,128]{5,4,3,2,1,0:T(8,128)}, u32[]{:S(2)}) %copy-start) | copy-done | bytes 3145752
  22.3 1.9 %copy-done.2 = f32[1,3,2,128,8,128]{5,4,3,2,1,0:T(8,128)S(1)} copy-done((f32[1,3,2,128,8,128]{5,4,3,2,1,0:T(8,128)S(1)}, f32[1,3,2,128,8,128]{5,4,3,2,1,0:T(8,128)}, u32[]{:S(2)}) %copy-start.2) | copy-done | bytes 3145752
  24.5 3.4 %collective-permute-start = (f32[384,128]{1,0:T(8,128)S(1)}, f32[384,128]{1,0:T(8,128)}, u32[]{:S(2)}, u32[]{:S(2)}) collective-permute-start(f32[384,128]{1,0:T(8,128)S(1)} %rim.1), channel_id=1, source_target_pairs={{0,8},{8,16},{16,24},{24,32},{32,40},{40,48},{48,56},{56,64},{64,7... | collective-permute-start | bytes 589832 | tf_op jit(solution)/shard_map/ppermute | solution.py:359
  28.0 1.9 %copy-done.1 = f32[1,3,2,128,8,128]{5,4,3,2,1,0:T(8,128)S(1)} copy-done((f32[1,3,2,128,8,128]{5,4,3,2,1,0:T(8,128)S(1)}, f32[1,3,2,128,8,128]{5,4,3,2,1,0:T(8,128)}, u32[]{:S(2)}) %copy-start.1) | copy-done | bytes 3145752
  29.9 1.9 %copy-done.3 = f32[1,3,2,128,8,128]{5,4,3,2,1,0:T(8,128)S(1)} copy-done((f32[1,3,2,128,8,128]{5,4,3,2,1,0:T(8,128)S(1)}, f32[1,3,2,128,8,128]{5,4,3,2,1,0:T(8,128)}, u32[]{:S(2)}) %copy-start.3) | copy-done | bytes 3145752
  31.8 1.9 %coefficients.1 = (f32[1024,128]{1,0:T(8,128)S(1)}, f32[1024,128]{1,0:T(8,128)S(1)}, f32[1024,128]{1,0:T(8,128)S(1)}, f32[1024,128]{1,0:T(8,128)S(1)}, f32[1024,...) custom-call(f32[6144,128]{1,0:T(8,128)S(1)} %bitcast.21, ...), custom_call_target="tpu_custom_call" | custom-call | flops 4194304 | bytes 8388608 | tf_op jit(solution)/shard_map/coefficients/pallas_call | solution.py:381
  34.4 0.8 copy-done.7
  35.2 0.8 copy-done.9
  41.0 22.7 %all-to-all-done = f32[128,1,3200]{2,1,0:T(1,128)S(1)} async-done(((f32[128,1,3200]{2,1,0:T(1,128)}), f32[128,1,3200]{2,1,0:T(1,128)S(1)}, u32[]{:S(2)}, u32[]{:S(2)}) %all-to-all-start) | async-done | bytes 1638432 | tf_op jit(solution)/shard_map/all_to_all | solution.py:376
  63.7 1.9 %first.1 = (f32[4096,128]{1,0:T(8,128)S(1)}, f32[512,128]{1,0:T(8,128)S(1)}, f32[512,128]{1,0:T(8,128)S(1)}, f32[72,128]{1,0:T(8,128)S(1)}, f32[32,128]{1,0:T(8,128)S(1)}) custom-call(s32[2]{0:T(128)S(1)} %pad_add_fusion.odd_ref, f32[3200,128]{1,0:T(8,128)S(1)} %bitcast.17, f32[8,128]{1,0:T(8,128)S(1)} %broadcast_select_fusion.mask_ref, ...), custom_call_target="tpu_custom_call" | custom-call | tf_op jit(solution)/shard_map/first/pallas_call | solution.py:400
  65.8 4.7 %collective-permute-start.2 = (f32[512,128]{1,0:T(8,128)S(1)}, f32[512,128]{1,0:T(8,128)S(1)}, u32[]{:S(2)}, u32[]{:S(2)}) collective-permute-start(f32[512,128]{1,0:T(8,128)S(1)} %get-tuple-element.40), channel_id=1, source_target_pairs={{8,16},{16,8},{24,32},{32,24},{40,48},{48,40},{56,64},{64,56},{72,... | collective-permute-start | bytes 786440 | tf_op jit(solution)/shard_map/ppermute | solution.py:419
  70.5 0.9 fusion
  71.4 4.1 %collective-permute-start.3 = (f32[72,128]{1,0:T(8,128)S(1)}, f32[72,128]{1,0:T(8,128)S(1)}, u32[]{:S(2)}, u32[]{:S(2)}) collective-permute-start(f32[72,128]{1,0:T(8,128)S(1)} %get-tuple-element.41), channel_id=1, source_target_pairs={{1,2},{2,1},{3,4},{4,3},{5,6},{6,5},{7,0},{0,7},{9,10},{10,9},{11,... | collective-permute-start | bytes 110600 | tf_op jit(solution)/shard_map/ppermute | solution.py:420
  75.5 1.3 %collective-permute-start.5 = (f32[32,128]{1,0:T(8,128)S(1)}, f32[32,128]{1,0:T(8,128)S(1)}, u32[]{:S(2)}, u32[]{:S(2)}) collective-permute-start(f32[32,128]{1,0:T(8,128)S(1)} %get-tuple-element.42), channel_id=1, source_target_pairs={{0,128},{1,129},{2,130},{3,131},{4,132},{5,133},{6,134},{7,135},{8... | collective-permute-start | bytes 49160 | tf_op jit(solution)/shard_map/ppermute | solution.py:422
  76.8 1.1 forcing.2.rest_0_
  77.9 3.7 %collective-permute-done.3.from_column1_ref = f32[72,128]{1,0:T(8,128)S(1)} collective-permute-done((f32[72,128]{1,0:T(8,128)S(1)}, f32[72,128]{1,0:T(8,128)S(1)}, u32[]{:S(2)}, u32[]{:S(2)}) %collective-permute-start.3) | collective-permute-done | bytes 36896 | tf_op jit(solution)/shard_map/ppermute | solution.py:420
  81.7 3.5 %step.3 = (f32[4096,128]{1,0:T(8,128)S(1)}, f32[512,128]{1,0:T(8,128)S(1)}, f32[512,128]{1,0:T(8,128)S(1)}, f32[72,128]{1,0:T(8,128)S(1)}, f32[32,128]{1,0:T(8,128)S(1)}) custom-call(f32[4,4]{1,0:T(4,128)S(1)} %bitcast.25, f32[4,4]{1,0:T(4,128)S(1)} %copy-done.24, s32[2]{0:T(128)S(1)} %pad_add_fusion.odd_ref, f32[4096,128]{1,0:T(8,128)S(1)} %get-tuple-element.34.m_ref, ...), custom_call_target="tpu_custom_call" | custom-call | tf_op jit(solution)/shard_map/step/pallas_call | solution.py:439
  85.2 1.7 %collective-permute-start.6 = (f32[512,128]{1,0:T(8,128)S(1)}, f32[512,128]{1,0:T(8,128)S(1)}, u32[]{:S(2)}, u32[]{:S(2)}) collective-permute-start(f32[512,128]{1,0:T(8,128)S(1)} %get-tuple-element.48), channel_id=1, source_target_pairs={{0,8},{8,0},{16,24},{24,16},{32,40},{40,32},{48,56},{56,48},{64,72... | collective-permute-start | bytes 786440 | tf_op jit(solution)/shard_map/ppermute | solution.py:418
  86.9 3.1 %collective-permute-start.7 = (f32[512,128]{1,0:T(8,128)S(1)}, f32[512,128]{1,0:T(8,128)S(1)}, u32[]{:S(2)}, u32[]{:S(2)}) collective-permute-start(f32[512,128]{1,0:T(8,128)S(1)} %get-tuple-element.49), channel_id=1, source_target_pairs={{8,16},{16,8},{24,32},{32,24},{40,48},{48,40},{56,64},{64,56},{72,... | collective-permute-start | bytes 786440 | tf_op jit(solution)/shard_map/ppermute | solution.py:419
  90.0 3.7 %collective-permute-start.8 = (f32[72,128]{1,0:T(8,128)S(1)}, f32[72,128]{1,0:T(8,128)S(1)}, u32[]{:S(2)}, u32[]{:S(2)}) collective-permute-start(f32[72,128]{1,0:T(8,128)S(1)} %get-tuple-element.50), channel_id=1, source_target_pairs={{1,2},{2,1},{3,4},{4,3},{5,6},{6,5},{7,0},{0,7},{9,10},{10,9},{11,... | collective-permute-start | bytes 110600 | tf_op jit(solution)/shard_map/ppermute | solution.py:420
  93.7 1.3 %collective-permute-start.10 = (f32[32,128]{1,0:T(8,128)S(1)}, f32[32,128]{1,0:T(8,128)S(1)}, u32[]{:S(2)}, u32[]{:S(2)}) collective-permute-start(f32[32,128]{1,0:T(8,128)S(1)} %get-tuple-element.51), channel_id=1, source_target_pairs={{0,128},{1,129},{2,130},{3,131},{4,132},{5,133},{6,134},{7,135},{8... | collective-permute-start | bytes 49160 | tf_op jit(solution)/shard_map/ppermute | solution.py:422
  95.0 1.1 forcing.3.rest_0_
  96.1 5.8 %collective-permute-done.8.from_column1_ref = f32[72,128]{1,0:T(8,128)S(1)} collective-permute-done((f32[72,128]{1,0:T(8,128)S(1)}, f32[72,128]{1,0:T(8,128)S(1)}, u32[]{:S(2)}, u32[]{:S(2)}) %collective-permute-start.8) | collective-permute-done | bytes 36896 | tf_op jit(solution)/shard_map/ppermute | solution.py:420
  102.0 3.5 %step.4 = (f32[4096,128]{1,0:T(8,128)S(1)}, f32[512,128]{1,0:T(8,128)S(1)}, f32[512,128]{1,0:T(8,128)S(1)}, f32[72,128]{1,0:T(8,128)S(1)}, f32[32,128]{1,0:T(8,128)S(1)}) custom-call(f32[4,4]{1,0:T(4,128)S(1)} %bitcast.26, f32[4,4]{1,0:T(4,128)S(1)} %copy-done.24, s32[2]{0:T(128)S(1)} %pad_add_fusion.odd_ref, f32[4096,128]{1,0:T(8,128)S(1)} %get-tuple-element.43.m_ref, ...), custom_call_target="tpu_custom_call" | custom-call | tf_op jit(solution)/shard_map/step/pallas_call | solution.py:439
  105.6 3.6 %collective-permute-start.12 = (f32[512,128]{1,0:T(8,128)S(1)}, f32[512,128]{1,0:T(8,128)S(1)}, u32[]{:S(2)}, u32[]{:S(2)}) collective-permute-start(f32[512,128]{1,0:T(8,128)S(1)} %get-tuple-element.58), channel_id=1, source_target_pairs={{8,16},{16,8},{24,32},{32,24},{40,48},{48,40},{56,64},{64,56},{72,... | collective-permute-start | bytes 786440 | tf_op jit(solution)/shard_map/ppermute | solution.py:419
  109.3 4.0 %collective-permute-start.13 = (f32[72,128]{1,0:T(8,128)S(1)}, f32[72,128]{1,0:T(8,128)S(1)}, u32[]{:S(2)}, u32[]{:S(2)}) collective-permute-start(f32[72,128]{1,0:T(8,128)S(1)} %get-tuple-element.59), channel_id=1, source_target_pairs={{1,2},{2,1},{3,4},{4,3},{5,6},{6,5},{7,0},{0,7},{9,10},{10,9},{11,... | collective-permute-start | bytes 110600 | tf_op jit(solution)/shard_map/ppermute | solution.py:420
  113.3 1.3 %collective-permute-start.15 = (f32[32,128]{1,0:T(8,128)S(1)}, f32[32,128]{1,0:T(8,128)S(1)}, u32[]{:S(2)}, u32[]{:S(2)}) collective-permute-start(f32[32,128]{1,0:T(8,128)S(1)} %get-tuple-element.60), channel_id=1, source_target_pairs={{0,128},{1,129},{2,130},{3,131},{4,132},{5,133},{6,134},{7,135},{8... | collective-permute-start | bytes 49160 | tf_op jit(solution)/shard_map/ppermute | solution.py:422
  115.4 6.9 %collective-permute-done.13.from_column1_ref = f32[72,128]{1,0:T(8,128)S(1)} collective-permute-done((f32[72,128]{1,0:T(8,128)S(1)}, f32[72,128]{1,0:T(8,128)S(1)}, u32[]{:S(2)}, u32[]{:S(2)}) %collective-permute-start.13) | collective-permute-done | bytes 36896 | tf_op jit(solution)/shard_map/ppermute | solution.py:420
  122.3 4.0 %step.5 = f32[4096,128]{1,0:T(8,128)} custom-call(f32[4,4]{1,0:T(4,128)S(1)} %bitcast.27, f32[4,4]{1,0:T(4,128)S(1)} %copy-done.24, s32[2]{0:T(128)S(1)} %pad_add_fusion.odd_ref, f32[4096,128]{1,0:T(8,128)S(1)} %get-tuple-element.52.m_ref, f32[1024,128]{1,0:T(8,128)S(1)} %get-tuple-element.53.up_e_ref, f32[1024,128]{1,0:T(8,128)S(1)} %get-tuple-element.54.down_w_ref, ...), custom_call_target="tpu_custom_call" | custom-call | tf_op jit(solution)/shard_map/step/pallas_call | solution.py:439
  (70 shorter events, 8.5 us)
Async XLA Ops:
  4.9 58.8 %all-to-all-start = ((f32[128,1,3200]{2,1,0:T(1,128)}), f32[128,1,3200]{2,1,0:T(1,128)S(1)}, u32[]{:S(2)}, u32[]{:S(2)}) async-start(f32[128,1,3200]{2,1,0:T(1,128)} %bitcast.4), calls=%async_computation | async-start | bytes 3276800 | tf_op jit(solution)/shard_map/all_to_all | solution.py:376
  20.4 1.9 %copy-start = (f32[1,3,2,128,8,128]{5,4,3,2,1,0:T(8,128)S(1)}, f32[1,3,2,128,8,128]{5,4,3,2,1,0:T(8,128)}, u32[]{:S(2)}) copy-start(f32[1,3,2,128,8,128]{5,4,3,2,1,0:T(8,128)} %param.11) | copy-start | bytes 9437188
  22.3 1.9 %copy-start.2 = (f32[1,3,2,128,8,128]{5,4,3,2,1,0:T(8,128)S(1)}, f32[1,3,2,128,8,128]{5,4,3,2,1,0:T(8,128)}, u32[]{:S(2)}) copy-start(f32[1,3,2,128,8,128]{5,4,3,2,1,0:T(8,128)} %param.12) | copy-start | bytes 9437188
  24.2 3.8 %copy-start.25 = (s32[8,128]{1,0:T(8,128)S(1)}, s32[8,128]{1,0:T(8,128)}, u32[]{:S(2)}) copy-start(s32[8,128]{1,0:T(8,128)} %param.15) | copy-start | bytes 12292
  24.5 46.0 %collective-permute-start = (f32[384,128]{1,0:T(8,128)S(1)}, f32[384,128]{1,0:T(8,128)}, u32[]{:S(2)}, u32[]{:S(2)}) collective-permute-start(f32[384,128]{1,0:T(8,128)S(1)} %rim.1), channel_id=1, source_target_pairs={{0,8},{8,16},{16,24},{24,32},{32,40},{40,48},{48,56},{56,64},{64,7... | collective-permute-start | bytes 589832 | tf_op jit(solution)/shard_map/ppermute | solution.py:359
  28.0 1.9 %copy-start.1 = (f32[1,3,2,128,8,128]{5,4,3,2,1,0:T(8,128)S(1)}, f32[1,3,2,128,8,128]{5,4,3,2,1,0:T(8,128)}, u32[]{:S(2)}) copy-start(f32[1,3,2,128,8,128]{5,4,3,2,1,0:T(8,128)} %param.11) | copy-start | bytes 9437188
  65.6 16.0 %copy-start.16 = (f32[1024,128]{1,0:T(8,128)S(1)}, f32[1024,128]{1,0:T(8,128)}, u32[]{:S(2)}) copy-start(f32[1024,128]{1,0:T(8,128)} %copy-done.15) | copy-start | bytes 1572868
  65.6 16.0 %copy-start.18 = (f32[1024,128]{1,0:T(8,128)S(1)}, f32[1024,128]{1,0:T(8,128)}, u32[]{:S(2)}) copy-start(f32[1024,128]{1,0:T(8,128)} %copy-done.17) | copy-start | bytes 1572868
  65.6 16.0 %copy-start.20 = (f32[1024,128]{1,0:T(8,128)S(1)}, f32[1024,128]{1,0:T(8,128)}, u32[]{:S(2)}) copy-start(f32[1024,128]{1,0:T(8,128)} %copy-done.19) | copy-start | bytes 1572868
  65.6 16.0 %copy-start.22 = (f32[1024,128]{1,0:T(8,128)S(1)}, f32[1024,128]{1,0:T(8,128)}, u32[]{:S(2)}) copy-start(f32[1024,128]{1,0:T(8,128)} %copy-done.21) | copy-start | bytes 1572868
  65.6 16.0 %copy-start.23 = (f32[1,4,4]{2,1,0:T(4,128)S(1)}, f32[1,4,4]{2,1,0:T(4,128)}, u32[]{:S(2)}) copy-start(f32[1,4,4]{2,1,0:T(4,128)} %param.13) | copy-start | bytes 196
  65.7 16.0 %copy-start.24 = (f32[4,4]{1,0:T(4,128)S(1)}, f32[4,4]{1,0:T(4,128)}, u32[]{:S(2)}) copy-start(f32[4,4]{1,0:T(4,128)} %air_ref.5) | copy-start | bytes 196
  65.7 15.9 %collective-permute-start.1 = (f32[512,128]{1,0:T(8,128)S(1)}, f32[512,128]{1,0:T(8,128)S(1)}, u32[]{:S(2)}, u32[]{:S(2)}) collective-permute-start(f32[512,128]{1,0:T(8,128)S(1)} %get-tuple-element.39), channel_id=1, source_target_pairs={{0,8},{8,0},{16,24},{24,16},{32,40},{40,32},{48,56},{56,48},{64,72... | collective-permute-start | bytes 786440 | tf_op jit(solution)/shard_map/ppermute | solution.py:418
  65.8 15.8 %collective-permute-start.2 = (f32[512,128]{1,0:T(8,128)S(1)}, f32[512,128]{1,0:T(8,128)S(1)}, u32[]{:S(2)}, u32[]{:S(2)}) collective-permute-start(f32[512,128]{1,0:T(8,128)S(1)} %get-tuple-element.40), channel_id=1, source_target_pairs={{8,16},{16,8},{24,32},{32,24},{40,48},{48,40},{56,64},{64,56},{72,... | collective-permute-start | bytes 786440 | tf_op jit(solution)/shard_map/ppermute | solution.py:419
  71.4 10.2 %collective-permute-start.3 = (f32[72,128]{1,0:T(8,128)S(1)}, f32[72,128]{1,0:T(8,128)S(1)}, u32[]{:S(2)}, u32[]{:S(2)}) collective-permute-start(f32[72,128]{1,0:T(8,128)S(1)} %get-tuple-element.41), channel_id=1, source_target_pairs={{1,2},{2,1},{3,4},{4,3},{5,6},{6,5},{7,0},{0,7},{9,10},{10,9},{11,... | collective-permute-start | bytes 110600 | tf_op jit(solution)/shard_map/ppermute | solution.py:420
  75.5 6.1 %collective-permute-start.4 = (f32[72,128]{1,0:T(8,128)S(1)}, f32[72,128]{1,0:T(8,128)S(1)}, u32[]{:S(2)}, u32[]{:S(2)}) collective-permute-start(f32[72,128]{1,0:T(8,128)S(1)} %get-tuple-element.41), channel_id=1, source_target_pairs={{0,1},{1,0},{2,3},{3,2},{4,5},{5,4},{6,7},{7,6},{8,9},{9,8},{10,11... | collective-permute-start | bytes 110600 | tf_op jit(solution)/shard_map/ppermute | solution.py:421
  75.5 2.4 %collective-permute-start.5 = (f32[32,128]{1,0:T(8,128)S(1)}, f32[32,128]{1,0:T(8,128)S(1)}, u32[]{:S(2)}, u32[]{:S(2)}) collective-permute-start(f32[32,128]{1,0:T(8,128)S(1)} %get-tuple-element.42), channel_id=1, source_target_pairs={{0,128},{1,129},{2,130},{3,131},{4,132},{5,133},{6,134},{7,135},{8... | collective-permute-start | bytes 49160 | tf_op jit(solution)/shard_map/ppermute | solution.py:422
  85.2 16.8 %copy-start.8 = (f32[1024,128]{1,0:T(8,128)S(1)}, f32[1024,128]{1,0:T(8,128)}, u32[]{:S(2)}) copy-start(f32[1024,128]{1,0:T(8,128)} %copy-done.7) | copy-start | bytes 1572868
  85.2 16.8 %copy-start.10 = (f32[1024,128]{1,0:T(8,128)S(1)}, f32[1024,128]{1,0:T(8,128)}, u32[]{:S(2)}) copy-start(f32[1024,128]{1,0:T(8,128)} %copy-done.9) | copy-start | bytes 1572868
  85.2 16.8 %copy-start.12 = (f32[1024,128]{1,0:T(8,128)S(1)}, f32[1024,128]{1,0:T(8,128)}, u32[]{:S(2)}) copy-start(f32[1024,128]{1,0:T(8,128)} %copy-done.11) | copy-start | bytes 1572868
  85.2 16.8 %copy-start.14 = (f32[1024,128]{1,0:T(8,128)S(1)}, f32[1024,128]{1,0:T(8,128)}, u32[]{:S(2)}) copy-start(f32[1024,128]{1,0:T(8,128)} %copy-done.13) | copy-start | bytes 1572868
  85.2 16.8 %collective-permute-start.6 = (f32[512,128]{1,0:T(8,128)S(1)}, f32[512,128]{1,0:T(8,128)S(1)}, u32[]{:S(2)}, u32[]{:S(2)}) collective-permute-start(f32[512,128]{1,0:T(8,128)S(1)} %get-tuple-element.48), channel_id=1, source_target_pairs={{0,8},{8,0},{16,24},{24,16},{32,40},{40,32},{48,56},{56,48},{64,72... | collective-permute-start | bytes 786440 | tf_op jit(solution)/shard_map/ppermute | solution.py:418
  86.9 15.1 %collective-permute-start.7 = (f32[512,128]{1,0:T(8,128)S(1)}, f32[512,128]{1,0:T(8,128)S(1)}, u32[]{:S(2)}, u32[]{:S(2)}) collective-permute-start(f32[512,128]{1,0:T(8,128)S(1)} %get-tuple-element.49), channel_id=1, source_target_pairs={{8,16},{16,8},{24,32},{32,24},{40,48},{48,40},{56,64},{64,56},{72,... | collective-permute-start | bytes 786440 | tf_op jit(solution)/shard_map/ppermute | solution.py:419
  90.0 11.9 %collective-permute-start.8 = (f32[72,128]{1,0:T(8,128)S(1)}, f32[72,128]{1,0:T(8,128)S(1)}, u32[]{:S(2)}, u32[]{:S(2)}) collective-permute-start(f32[72,128]{1,0:T(8,128)S(1)} %get-tuple-element.50), channel_id=1, source_target_pairs={{1,2},{2,1},{3,4},{4,3},{5,6},{6,5},{7,0},{0,7},{9,10},{10,9},{11,... | collective-permute-start | bytes 110600 | tf_op jit(solution)/shard_map/ppermute | solution.py:420
  93.7 8.2 %collective-permute-start.9 = (f32[72,128]{1,0:T(8,128)S(1)}, f32[72,128]{1,0:T(8,128)S(1)}, u32[]{:S(2)}, u32[]{:S(2)}) collective-permute-start(f32[72,128]{1,0:T(8,128)S(1)} %get-tuple-element.50), channel_id=1, source_target_pairs={{0,1},{1,0},{2,3},{3,2},{4,5},{5,4},{6,7},{7,6},{8,9},{9,8},{10,11... | collective-permute-start | bytes 110600 | tf_op jit(solution)/shard_map/ppermute | solution.py:421
  93.7 2.4 %collective-permute-start.10 = (f32[32,128]{1,0:T(8,128)S(1)}, f32[32,128]{1,0:T(8,128)S(1)}, u32[]{:S(2)}, u32[]{:S(2)}) collective-permute-start(f32[32,128]{1,0:T(8,128)S(1)} %get-tuple-element.51), channel_id=1, source_target_pairs={{0,128},{1,129},{2,130},{3,131},{4,132},{5,133},{6,134},{7,135},{8... | collective-permute-start | bytes 49160 | tf_op jit(solution)/shard_map/ppermute | solution.py:422
  102.0 20.3 %copy-start.6 = (f32[1024,128]{1,0:T(8,128)S(1)}, f32[1024,128]{1,0:T(8,128)}, u32[]{:S(2)}) copy-start(f32[1024,128]{1,0:T(8,128)} %copy-done.5) | copy-start | bytes 1572868
  105.5 16.8 %collective-permute-start.11 = (f32[512,128]{1,0:T(8,128)S(1)}, f32[512,128]{1,0:T(8,128)S(1)}, u32[]{:S(2)}, u32[]{:S(2)}) collective-permute-start(f32[512,128]{1,0:T(8,128)S(1)} %get-tuple-element.57), channel_id=1, source_target_pairs={{0,8},{8,0},{16,24},{24,16},{32,40},{40,32},{48,56},{56,48},{64,72... | collective-permute-start | bytes 786440 | tf_op jit(solution)/shard_map/ppermute | solution.py:418
  105.6 16.7 %collective-permute-start.12 = (f32[512,128]{1,0:T(8,128)S(1)}, f32[512,128]{1,0:T(8,128)S(1)}, u32[]{:S(2)}, u32[]{:S(2)}) collective-permute-start(f32[512,128]{1,0:T(8,128)S(1)} %get-tuple-element.58), channel_id=1, source_target_pairs={{8,16},{16,8},{24,32},{32,24},{40,48},{48,40},{56,64},{64,56},{72,... | collective-permute-start | bytes 786440 | tf_op jit(solution)/shard_map/ppermute | solution.py:419
  109.3 13.0 %collective-permute-start.13 = (f32[72,128]{1,0:T(8,128)S(1)}, f32[72,128]{1,0:T(8,128)S(1)}, u32[]{:S(2)}, u32[]{:S(2)}) collective-permute-start(f32[72,128]{1,0:T(8,128)S(1)} %get-tuple-element.59), channel_id=1, source_target_pairs={{1,2},{2,1},{3,4},{4,3},{5,6},{6,5},{7,0},{0,7},{9,10},{10,9},{11,... | collective-permute-start | bytes 110600 | tf_op jit(solution)/shard_map/ppermute | solution.py:420
  113.3 9.0 %collective-permute-start.14 = (f32[72,128]{1,0:T(8,128)S(1)}, f32[72,128]{1,0:T(8,128)S(1)}, u32[]{:S(2)}, u32[]{:S(2)}) collective-permute-start(f32[72,128]{1,0:T(8,128)S(1)} %get-tuple-element.59), channel_id=1, source_target_pairs={{0,1},{1,0},{2,3},{3,2},{4,5},{5,4},{6,7},{7,6},{8,9},{9,8},{10,11... | collective-permute-start | bytes 110600 | tf_op jit(solution)/shard_map/ppermute | solution.py:421
  113.3 2.1 %collective-permute-start.15 = (f32[32,128]{1,0:T(8,128)S(1)}, f32[32,128]{1,0:T(8,128)S(1)}, u32[]{:S(2)}, u32[]{:S(2)}) collective-permute-start(f32[32,128]{1,0:T(8,128)S(1)} %get-tuple-element.60), channel_id=1, source_target_pairs={{0,128},{1,129},{2,130},{3,131},{4,132},{5,133},{6,134},{7,135},{8... | collective-permute-start | bytes 49160 | tf_op jit(solution)/shard_map/ppermute | solution.py:422
  (11 other events, 10.3 us)

commit v4 on v3

--- a/solution.py
+++ b/solution.py
@@ -9,7 +9,9 @@
 
 LANES = 128
 SUBS = 8
+BATCH = 4
 VMEM_LIMIT = 20 * 1024 * 1024
+VMEM_WHOLE = 58 * 1024 * 1024
 
 
 def split3(x):
@@ -41,12 +43,12 @@
     for copy in small:
         copy.wait()
     for step in range(steps):
-        hits = owner_ref[step : step + 1, :] == dest
+        hits = owner_ref[step] == dest
         hits_f = hits.astype(jnp.float32)
         prior = jnp.dot(hits_f.astype(jnp.bfloat16), before, preferred_element_type=jnp.float32)
         large[step].wait()
         terms = jnp.concatenate(split3(rows_ref[step]), axis=0)
-        marks = (cell_ref[step : step + 1, :] + 1).astype(jnp.float32)
+        marks = (cell_ref[step] + 1).astype(jnp.float32)
         for k in range(slots):
             slot = step * slots + k
             pick = jnp.where(prior == float(k), hits_f, 0.0)
@@ -236,11 +238,11 @@
     *rest,
 ):
     if last:
-        (out_ref,) = rest
+        sent_ref, out_ref, sems = rest
     else:
         f_ref, rim_ref, out_ref, slab1_ref, slab2_ref, column_ref, low_ref = rest
     width = fields * levels
-    batch = 4
+    batch = BATCH
     lane = lax.broadcasted_iota(jnp.int32, (SUBS, LANES), 1)
     sub = lax.broadcasted_iota(jnp.int32, (SUBS, LANES), 0)
     at_west, at_east = lane == 0, lane == LANES - 1
@@ -265,7 +267,7 @@
                 )
                 up_n = up_n_ref[rows_of(y * levels, group), :]
                 if y == 0:
-                    down_s = north_rim_ref[rows_of(0, group), :]
+                    down_s = north_rim_ref[rows_of(step * levels, group), :]
                 else:
                     down_s = down_n_ref[rows_of((y - 1) * levels, group), :]
                 planes = [m_ref[rows_of(y * width + f * levels, group), :] for f in range(fields)]
@@ -298,6 +300,12 @@
                     rows = rows_of(y * width + g * levels, group)
                     result = (result + f_ref[rows, :]) * mask_ref[y : y + 1, :]
                     out_ref[rows, :] = result
+        if last:
+            for f in range(fields):
+                rows = pl.ds((f * levels + group0 * SUBS) * SUBS, batch * SUBS * SUBS)
+                pltpu.make_async_copy(
+                    out_ref.at[rows], sent_ref.at[rows], sems.at[f * levels // (batch * SUBS) + group0 // batch]
+                ).start()
         return columns_turn(halos, batch)
 
     halos = columns_load(lon_even, from_column1_ref, from_column2_ref, fields)
@@ -307,14 +315,18 @@
         return tuple(batch_step(i * batch, list(halos)))
 
     lax.fori_loop(1, levels // (SUBS * batch), body, tuple(halos))
-    if not last:
+    if last:
+        for i in range(fields * levels // (batch * SUBS)):
+            rows = pl.ds(i * batch * SUBS * SUBS, batch * SUBS * SUBS)
+            pltpu.make_async_copy(out_ref.at[rows], sent_ref.at[rows], sems.at[i]).wait()
+    else:
         columns_store(out_ref, rim_ref[(step - 1) * SUBS : step * SUBS, :], column_ref, fields, levels)
         slabs_store(lat_even, out_ref, slab1_ref, slab2_ref, width)
         low_store(out_ref, low_ref, fields, levels)
 
 
-def params():
-    return pltpu.CompilerParams(vmem_limit_bytes=VMEM_LIMIT)
+def params(limit=VMEM_LIMIT):
+    return pltpu.CompilerParams(vmem_limit_bytes=limit)
 
 
 def swaps(axis, start, closed):
@@ -353,12 +365,12 @@
         out_shape=f32((steps * levels, LANES)),
         in_specs=[anywhere] * 2,
         scratch_shapes=[pltpu.VMEM((steps, levels, LANES), jnp.float32)] * 2 + [pltpu.SemaphoreType.DMA((2,))],
-        compiler_params=params(),
+        compiler_params=params(VMEM_WHOLE),
         name="rim",
     )(speeds, diffuse)
     north_rims = lax.ppermute(
         north_rims, "lat", [(i, i + 1) for i in range(lat_count - 1)]
-    ).reshape(steps, levels, LANES)
+    )
 
     sent = pl.pallas_call(
         functools.partial(pack_kernel, slots),
@@ -366,13 +378,17 @@
         in_specs=[anywhere] * 3,
         scratch_shapes=[
             pltpu.VMEM((steps, count, width), jnp.float32),
-            pltpu.VMEM((steps, count), jnp.int32),
-            pltpu.VMEM((steps, count), jnp.int32),
+            pltpu.VMEM((steps, 1, count), jnp.int32),
+            pltpu.VMEM((steps, 1, count), jnp.int32),
             pltpu.SemaphoreType.DMA((steps + 2,)),
         ],
-        compiler_params=params(),
+        compiler_params=params(VMEM_WHOLE),
         name="pack",
-    )(innovations[0], obs_owner[0, :, :, 0], obs_cell[0])
+    )(
+        innovations[0],
+        obs_owner.reshape(steps, 1, count),
+        obs_cell.reshape(steps, 1, count),
+    )
     got = lax.all_to_all(
         sent.reshape(owners, 1, stride * LANES), ("lat", "lon"), split_axis=0, concat_axis=0, tiled=True
     ).reshape(owners * stride, LANES)
@@ -412,7 +428,7 @@
             odd,
             m,
             *tables[4 * step : 4 * step + 4],
-            north_rims[step],
+            north_rims,
             sea_float,
             mask,
             lax.ppermute(slab1, "lat", swaps("lat", 0, False)),
@@ -440,6 +456,13 @@
             functools.partial(step_kernel, last, step, fields, levels),
             out_shape=edge_shapes[:1] if last else edge_shapes,
             in_specs=[smem] * 3 + [vmem] * (len(operands) - 3),
+            out_specs=[anywhere] if last else [vmem] * len(edge_shapes),
+            scratch_shapes=[
+                pltpu.VMEM((width * SUBS, LANES), jnp.float32),
+                pltpu.SemaphoreType.DMA((width // (BATCH * SUBS),)),
+            ]
+            if last
+            else [],
             compiler_params=params(),
             name="step",
         )(*operands)

time: 127 us -> 125 us (0.984)
  local copies, waits for them, and re-layouts: 18.3 us -> 11.1 us
  waiting for transfers between devices: 40 us -> 42.3 us
  Pallas kernels: 19.7 us -> 21.5 us
    unnamed x54 -> x46, local copies, waits for them, and re-layouts: 17.4 us -> 11.1 us
    all_to_all x1, waiting for transfers between devices: 22.7 us -> 25.1 us  [shards(): lax.all_to_all(sent.reshape(owners, 1, stride * LANES), ('lat', 'lon'), s...]
    ppermute x3, starting transfers between devices: 1.87 us -> 3.43 us  [shards(): lax.ppermute(slab1, 'lat', swaps('lat', 0, False))]
    pallas_call x1, Pallas kernels: 0.31 us -> 1.77 us  [shards(): pl.pallas_call(rim_kernel, out_shape=f32((steps * levels, LANES)), in_spe...]
    ppermute x3, starting transfers between devices: 11.5 us -> 10.1 us  [shards(): lax.ppermute(slab2, 'lat', swaps('lat', 1, False))]
  transfers between devices with their start and end apart: 17 -> 17, of which waited for: 5 -> 5; matrix products, arithmetic and copies ran while one was open for 1% -> 0% of each run, Pallas kernels for 5% -> 6%
where the time goes in v4:
time: 125 us; the launch traced here: 124 us
  starting transfers between devices  48.7 us (39%)
  waiting for transfers between devices  42.3 us (34%)
  Pallas kernels  21.5 us (17%)
  local copies, waits for them, and re-layouts  11.1 us (9%)
    all_to_all x1, waiting for transfers between devices, shards(): lax.all_to_all(sent.reshape(owners, 1, stride * LANES), ('lat', 'lon'), s...  25.1 us
    ppermute x3, waiting for transfers between devices, shards(): lax.ppermute(columns, 'lon', swaps('lon', 1, True))  16.4 us
    all_to_all x1, starting transfers between devices, shards(): lax.all_to_all(sent.reshape(owners, 1, stride * LANES), ('lat', 'lon'), s...  15.5 us
    ppermute x3, starting transfers between devices, shards(): lax.ppermute(columns, 'lon', swaps('lon', 1, True))  12.5 us
    unnamed x46, local copies, waits for them, and re-layouts  11.1 us
    pallas_call x3, Pallas kernels, shards(): pl.pallas_call(functools.partial(step_kernel, last, step, fields, levels)...  10.6 us
    ppermute x3, starting transfers between devices, shards(): lax.ppermute(slab2, 'lat', swaps('lat', 1, False))  10.1 us
    ppermute x3, starting transfers between devices, shards(): lax.ppermute(low, 'comp', [(0, 1)])  3.84 us
  transfers between devices with their start and end apart: 17, of which 5 were waited for; matrix products, arithmetic and copies ran while one was open for 0% of the time, Pallas kernels for 6%

profile of v4, /device:TPU:8, one launch (start us, length us, event | category | flops | bytes accessed | tf_op | source)
XLA Modules:
  0.0 124.3 jit_solution(9319682166197326990)
XLA Ops:
  0.0 3.2 %pack.1 = f32[3200,128]{1,0:T(8,128)} custom-call(f32[3,128,512]{2,1,0:T(8,128)} %bitcast.24, s32[3,1,128]{2,1,0:T(1,128)} %bitcast.25, s32[3,1,128]{2,1,0:T(1,128)} %bitcast.26), custom_call_target="tpu_custom_call" | custom-call | tf_op jit(solution)/shard_map/pack/pallas_call | solution.py:375
  3.2 15.5 %all-to-all-start = ((f32[128,1,3200]{2,1,0:T(1,128)}), f32[128,1,3200]{2,1,0:T(1,128)S(1)}, u32[]{:S(2)}, u32[]{:S(2)}) async-start(f32[128,1,3200]{2,1,0:T(1,128)} %bitcast.23), calls=%async_computation | async-start | bytes 3276800 | tf_op jit(solution)/shard_map/all_to_all | solution.py:392
  18.7 1.8 %rim.1 = f32[384,128]{1,0:T(8,128)} custom-call(f32[3,2,128,8,128]{4,3,2,1,0:T(8,128)} %bitcast.16, f32[3,2,128,8,128]{4,3,2,1,0:T(8,128)} %bitcast.18), custom_call_target="tpu_custom_call" | custom-call | tf_op jit(solution)/shard_map/rim/pallas_call | solution.py:363
  20.4 3.4 %collective-permute-start = (f32[384,128]{1,0:T(8,128)}, f32[384,128]{1,0:T(8,128)S(1)}, u32[]{:S(2)}, u32[]{:S(2)}) collective-permute-start(f32[384,128]{1,0:T(8,128)} %rim.1), channel_id=1, source_target_pairs={{0,8},{8,16},{16,24},{24,32},{32,40},{40,48},{48,56},{56,64},{64,7... | collective-permute-start | bytes 589832 | tf_op jit(solution)/shard_map/ppermute | solution.py:371
  24.0 1.9 %copy-done = f32[1,3,2,128,8,128]{5,4,3,2,1,0:T(8,128)S(1)} copy-done((f32[1,3,2,128,8,128]{5,4,3,2,1,0:T(8,128)S(1)}, f32[1,3,2,128,8,128]{5,4,3,2,1,0:T(8,128)}, u32[]{:S(2)}) %copy-start) | copy-done | bytes 3145752
  25.9 1.9 %copy-done.1 = f32[1,3,2,128,8,128]{5,4,3,2,1,0:T(8,128)S(1)} copy-done((f32[1,3,2,128,8,128]{5,4,3,2,1,0:T(8,128)S(1)}, f32[1,3,2,128,8,128]{5,4,3,2,1,0:T(8,128)}, u32[]{:S(2)}) %copy-start.1) | copy-done | bytes 3145752
  27.8 1.9 %coefficients.1 = (f32[1024,128]{1,0:T(8,128)S(1)}, f32[1024,128]{1,0:T(8,128)S(1)}, f32[1024,128]{1,0:T(8,128)S(1)}, f32[1024,128]{1,0:T(8,128)S(1)}, f32[1024,...) custom-call(f32[6144,128]{1,0:T(8,128)S(1)} %bitcast.17, ...), custom_call_target="tpu_custom_call" | custom-call | flops 4194304 | bytes 8388608 | tf_op jit(solution)/shard_map/coefficients/pallas_call | solution.py:397
  30.4 0.8 copy-done.4
  33.6 0.8 copy-done.12
  36.1 0.8 copy-done.18
  36.9 25.1 %all-to-all-done = f32[128,1,3200]{2,1,0:T(1,128)S(1)} async-done(((f32[128,1,3200]{2,1,0:T(1,128)}), f32[128,1,3200]{2,1,0:T(1,128)S(1)}, u32[]{:S(2)}, u32[]{:S(2)}) %all-to-all-start) | async-done | bytes 1638432 | tf_op jit(solution)/shard_map/all_to_all | solution.py:392
  61.9 1.9 %first.1 = (f32[4096,128]{1,0:T(8,128)S(1)}, f32[512,128]{1,0:T(8,128)S(1)}, f32[512,128]{1,0:T(8,128)S(1)}, f32[72,128]{1,0:T(8,128)S(1)}, f32[32,128]{1,0:T(8,128)S(1)}) custom-call(s32[2]{0:T(128)S(1)} %pad_add_fusion.odd_ref, f32[3200,128]{1,0:T(8,128)S(1)} %bitcast.13, f32[8,128]{1,0:T(8,128)S(1)} %broadcast_select_fusion.mask_ref, ...), custom_call_target="tpu_custom_call" | custom-call | tf_op jit(solution)/shard_map/first/pallas_call | solution.py:416
  64.0 4.7 %collective-permute-start.2 = (f32[512,128]{1,0:T(8,128)S(1)}, f32[512,128]{1,0:T(8,128)S(1)}, u32[]{:S(2)}, u32[]{:S(2)}) collective-permute-start(f32[512,128]{1,0:T(8,128)S(1)} %get-tuple-element.40), channel_id=1, source_target_pairs={{8,16},{16,8},{24,32},{32,24},{40,48},{48,40},{56,64},{64,56},{72,... | collective-permute-start | bytes 786440 | tf_op jit(solution)/shard_map/ppermute | solution.py:435
  68.8 4.1 %collective-permute-start.3 = (f32[72,128]{1,0:T(8,128)S(1)}, f32[72,128]{1,0:T(8,128)S(1)}, u32[]{:S(2)}, u32[]{:S(2)}) collective-permute-start(f32[72,128]{1,0:T(8,128)S(1)} %get-tuple-element.41), channel_id=1, source_target_pairs={{1,2},{2,1},{3,4},{4,3},{5,6},{6,5},{7,0},{0,7},{9,10},{10,9},{11,... | collective-permute-start | bytes 110600 | tf_op jit(solution)/shard_map/ppermute | solution.py:436
  72.9 1.3 %collective-permute-start.5 = (f32[32,128]{1,0:T(8,128)S(1)}, f32[32,128]{1,0:T(8,128)S(1)}, u32[]{:S(2)}, u32[]{:S(2)}) collective-permute-start(f32[32,128]{1,0:T(8,128)S(1)} %get-tuple-element.42), channel_id=1, source_target_pairs={{0,128},{1,129},{2,130},{3,131},{4,132},{5,133},{6,134},{7,135},{8... | collective-permute-start | bytes 49160 | tf_op jit(solution)/shard_map/ppermute | solution.py:438
  74.2 1.1 forcing.2.rest_0_
  75.3 3.8 %collective-permute-done.3.from_column1_ref = f32[72,128]{1,0:T(8,128)S(1)} collective-permute-done((f32[72,128]{1,0:T(8,128)S(1)}, f32[72,128]{1,0:T(8,128)S(1)}, u32[]{:S(2)}, u32[]{:S(2)}) %collective-permute-start.3) | collective-permute-done | bytes 36896 | tf_op jit(solution)/shard_map/ppermute | solution.py:436
  79.1 3.5 %step.3 = (f32[4096,128]{1,0:T(8,128)S(1)}, f32[512,128]{1,0:T(8,128)S(1)}, f32[512,128]{1,0:T(8,128)S(1)}, f32[72,128]{1,0:T(8,128)S(1)}, f32[32,128]{1,0:T(8,128)S(1)}) custom-call(f32[4,4]{1,0:T(4,128)S(1)} %bitcast.20, f32[4,4]{1,0:T(4,128)S(1)} %copy-done.21, s32[2]{0:T(128)S(1)} %pad_add_fusion.odd_ref, f32[4096,128]{1,0:T(8,128)S(1)} %get-tuple-element.34.m_ref, ...), custom_call_target="tpu_custom_call" | custom-call | tf_op jit(solution)/shard_map/step/pallas_call | solution.py:455
  82.6 2.4 %collective-permute-start.6 = (f32[512,128]{1,0:T(8,128)S(1)}, f32[512,128]{1,0:T(8,128)S(1)}, u32[]{:S(2)}, u32[]{:S(2)}) collective-permute-start(f32[512,128]{1,0:T(8,128)S(1)} %get-tuple-element.48), channel_id=1, source_target_pairs={{0,8},{8,0},{16,24},{24,16},{32,40},{40,32},{48,56},{56,48},{64,72... | collective-permute-start | bytes 786440 | tf_op jit(solution)/shard_map/ppermute | solution.py:434
  85.0 2.8 %collective-permute-start.7 = (f32[512,128]{1,0:T(8,128)S(1)}, f32[512,128]{1,0:T(8,128)S(1)}, u32[]{:S(2)}, u32[]{:S(2)}) collective-permute-start(f32[512,128]{1,0:T(8,128)S(1)} %get-tuple-element.49), channel_id=1, source_target_pairs={{8,16},{16,8},{24,32},{32,24},{40,48},{48,40},{56,64},{64,56},{72,... | collective-permute-start | bytes 786440 | tf_op jit(solution)/shard_map/ppermute | solution.py:435
  87.8 4.2 %collective-permute-start.8 = (f32[72,128]{1,0:T(8,128)S(1)}, f32[72,128]{1,0:T(8,128)S(1)}, u32[]{:S(2)}, u32[]{:S(2)}) collective-permute-start(f32[72,128]{1,0:T(8,128)S(1)} %get-tuple-element.50), channel_id=1, source_target_pairs={{1,2},{2,1},{3,4},{4,3},{5,6},{6,5},{7,0},{0,7},{9,10},{10,9},{11,... | collective-permute-start | bytes 110600 | tf_op jit(solution)/shard_map/ppermute | solution.py:436
  92.0 1.3 %collective-permute-start.10 = (f32[32,128]{1,0:T(8,128)S(1)}, f32[32,128]{1,0:T(8,128)S(1)}, u32[]{:S(2)}, u32[]{:S(2)}) collective-permute-start(f32[32,128]{1,0:T(8,128)S(1)} %get-tuple-element.51), channel_id=1, source_target_pairs={{0,128},{1,129},{2,130},{3,131},{4,132},{5,133},{6,134},{7,135},{8... | collective-permute-start | bytes 49160 | tf_op jit(solution)/shard_map/ppermute | solution.py:438
  93.2 1.1 forcing.3.rest_0_
  94.4 5.9 %collective-permute-done.8.from_column1_ref = f32[72,128]{1,0:T(8,128)S(1)} collective-permute-done((f32[72,128]{1,0:T(8,128)S(1)}, f32[72,128]{1,0:T(8,128)S(1)}, u32[]{:S(2)}, u32[]{:S(2)}) %collective-permute-start.8) | collective-permute-done | bytes 36896 | tf_op jit(solution)/shard_map/ppermute | solution.py:436
  100.3 3.5 %step.4 = (f32[4096,128]{1,0:T(8,128)S(1)}, f32[512,128]{1,0:T(8,128)S(1)}, f32[512,128]{1,0:T(8,128)S(1)}, f32[72,128]{1,0:T(8,128)S(1)}, f32[32,128]{1,0:T(8,128)S(1)}) custom-call(f32[4,4]{1,0:T(4,128)S(1)} %bitcast.21, f32[4,4]{1,0:T(4,128)S(1)} %copy-done.21, s32[2]{0:T(128)S(1)} %pad_add_fusion.odd_ref, f32[4096,128]{1,0:T(8,128)S(1)} %get-tuple-element.43.m_ref, ...), custom_call_target="tpu_custom_call" | custom-call | tf_op jit(solution)/shard_map/step/pallas_call | solution.py:455
  103.8 0.9 collective-permute-start.11
  104.7 2.6 %collective-permute-start.12 = (f32[512,128]{1,0:T(8,128)S(1)}, f32[512,128]{1,0:T(8,128)S(1)}, u32[]{:S(2)}, u32[]{:S(2)}) collective-permute-start(f32[512,128]{1,0:T(8,128)S(1)} %get-tuple-element.58), channel_id=1, source_target_pairs={{8,16},{16,8},{24,32},{32,24},{40,48},{48,40},{56,64},{64,56},{72,... | collective-permute-start | bytes 786440 | tf_op jit(solution)/shard_map/ppermute | solution.py:435
  107.3 4.2 %collective-permute-start.13 = (f32[72,128]{1,0:T(8,128)S(1)}, f32[72,128]{1,0:T(8,128)S(1)}, u32[]{:S(2)}, u32[]{:S(2)}) collective-permute-start(f32[72,128]{1,0:T(8,128)S(1)} %get-tuple-element.59), channel_id=1, source_target_pairs={{1,2},{2,1},{3,4},{4,3},{5,6},{6,5},{7,0},{0,7},{9,10},{10,9},{11,... | collective-permute-start | bytes 110600 | tf_op jit(solution)/shard_map/ppermute | solution.py:436
  111.5 1.3 %collective-permute-start.15 = (f32[32,128]{1,0:T(8,128)S(1)}, f32[32,128]{1,0:T(8,128)S(1)}, u32[]{:S(2)}, u32[]{:S(2)}) collective-permute-start(f32[32,128]{1,0:T(8,128)S(1)} %get-tuple-element.60), channel_id=1, source_target_pairs={{0,128},{1,129},{2,130},{3,131},{4,132},{5,133},{6,134},{7,135},{8... | collective-permute-start | bytes 49160 | tf_op jit(solution)/shard_map/ppermute | solution.py:438
  112.8 0.8 collective-permute-done.15.from_low_ref
  113.6 6.8 %collective-permute-done.13.from_column1_ref = f32[72,128]{1,0:T(8,128)S(1)} collective-permute-done((f32[72,128]{1,0:T(8,128)S(1)}, f32[72,128]{1,0:T(8,128)S(1)}, u32[]{:S(2)}, u32[]{:S(2)}) %collective-permute-start.13) | collective-permute-done | bytes 36896 | tf_op jit(solution)/shard_map/ppermute | solution.py:436
  120.5 3.6 %step.5 = f32[4096,128]{1,0:T(8,128)} custom-call(f32[4,4]{1,0:T(4,128)S(1)} %bitcast.22, f32[4,4]{1,0:T(4,128)S(1)} %copy-done.21, s32[2]{0:T(128)S(1)} %pad_add_fusion.odd_ref, f32[4096,128]{1,0:T(8,128)S(1)} %get-tuple-element.52.m_ref, f32[1024,128]{1,0:T(8,128)S(1)} %copy-done.13, f32[1024,128]{1,0:T(8,128)S(1)} %copy-done.15, ...), custom_call_target="tpu_custom_call" | custom-call | tf_op jit(solution)/shard_map/step/pallas_call | solution.py:455
  (61 shorter events, 5.1 us)
Async XLA Ops:
  3.2 58.8 %all-to-all-start = ((f32[128,1,3200]{2,1,0:T(1,128)}), f32[128,1,3200]{2,1,0:T(1,128)S(1)}, u32[]{:S(2)}, u32[]{:S(2)}) async-start(f32[128,1,3200]{2,1,0:T(1,128)} %bitcast.23), calls=%async_computation | async-start | bytes 3276800 | tf_op jit(solution)/shard_map/all_to_all | solution.py:392
  18.6 5.2 %copy-start.22 = (s32[8,128]{1,0:T(8,128)S(1)}, s32[8,128]{1,0:T(8,128)}, u32[]{:S(2)}) copy-start(s32[8,128]{1,0:T(8,128)} %param.15) | copy-start | bytes 12292
  20.4 52.5 %collective-permute-start = (f32[384,128]{1,0:T(8,128)}, f32[384,128]{1,0:T(8,128)S(1)}, u32[]{:S(2)}, u32[]{:S(2)}) collective-permute-start(f32[384,128]{1,0:T(8,128)} %rim.1), channel_id=1, source_target_pairs={{0,8},{8,16},{16,24},{24,32},{32,40},{40,48},{48,56},{56,64},{64,7... | collective-permute-start | bytes 589832 | tf_op jit(solution)/shard_map/ppermute | solution.py:371
  24.0 1.9 %copy-start = (f32[1,3,2,128,8,128]{5,4,3,2,1,0:T(8,128)S(1)}, f32[1,3,2,128,8,128]{5,4,3,2,1,0:T(8,128)}, u32[]{:S(2)}) copy-start(f32[1,3,2,128,8,128]{5,4,3,2,1,0:T(8,128)} %param.11) | copy-start | bytes 9437188
  25.9 1.9 %copy-start.1 = (f32[1,3,2,128,8,128]{5,4,3,2,1,0:T(8,128)S(1)}, f32[1,3,2,128,8,128]{5,4,3,2,1,0:T(8,128)}, u32[]{:S(2)}) copy-start(f32[1,3,2,128,8,128]{5,4,3,2,1,0:T(8,128)} %param.12) | copy-start | bytes 9437188
  30.4 0.8 copy-start.4
  63.9 15.2 %copy-start.5 = (f32[1024,128]{1,0:T(8,128)S(1)}, f32[1024,128]{1,0:T(8,128)}, u32[]{:S(2)}) copy-start(f32[1024,128]{1,0:T(8,128)} %copy-done.4) | copy-start | bytes 1572868
  63.9 15.2 %copy-start.7 = (f32[1024,128]{1,0:T(8,128)S(1)}, f32[1024,128]{1,0:T(8,128)}, u32[]{:S(2)}) copy-start(f32[1024,128]{1,0:T(8,128)} %copy-done.6) | copy-start | bytes 1572868
  63.9 15.2 %copy-start.9 = (f32[1024,128]{1,0:T(8,128)S(1)}, f32[1024,128]{1,0:T(8,128)}, u32[]{:S(2)}) copy-start(f32[1024,128]{1,0:T(8,128)} %copy-done.8) | copy-start | bytes 1572868
  63.9 15.2 %copy-start.11 = (f32[1024,128]{1,0:T(8,128)S(1)}, f32[1024,128]{1,0:T(8,128)}, u32[]{:S(2)}) copy-start(f32[1024,128]{1,0:T(8,128)} %copy-done.10) | copy-start | bytes 1572868
  63.9 15.2 %copy-start.20 = (f32[1,4,4]{2,1,0:T(4,128)S(1)}, f32[1,4,4]{2,1,0:T(4,128)}, u32[]{:S(2)}) copy-start(f32[1,4,4]{2,1,0:T(4,128)} %param.13) | copy-start | bytes 196
  63.9 15.2 %copy-start.21 = (f32[4,4]{1,0:T(4,128)S(1)}, f32[4,4]{1,0:T(4,128)}, u32[]{:S(2)}) copy-start(f32[4,4]{1,0:T(4,128)} %air_ref.5) | copy-start | bytes 196
  63.9 15.1 %collective-permute-start.1 = (f32[512,128]{1,0:T(8,128)S(1)}, f32[512,128]{1,0:T(8,128)S(1)}, u32[]{:S(2)}, u32[]{:S(2)}) collective-permute-start(f32[512,128]{1,0:T(8,128)S(1)} %get-tuple-element.39), channel_id=1, source_target_pairs={{0,8},{8,0},{16,24},{24,16},{32,40},{40,32},{48,56},{56,48},{64,72... | collective-permute-start | bytes 786440 | tf_op jit(solution)/shard_map/ppermute | solution.py:434
  64.0 15.0 %collective-permute-start.2 = (f32[512,128]{1,0:T(8,128)S(1)}, f32[512,128]{1,0:T(8,128)S(1)}, u32[]{:S(2)}, u32[]{:S(2)}) collective-permute-start(f32[512,128]{1,0:T(8,128)S(1)} %get-tuple-element.40), channel_id=1, source_target_pairs={{8,16},{16,8},{24,32},{32,24},{40,48},{48,40},{56,64},{64,56},{72,... | collective-permute-start | bytes 786440 | tf_op jit(solution)/shard_map/ppermute | solution.py:435
  68.8 10.3 %collective-permute-start.3 = (f32[72,128]{1,0:T(8,128)S(1)}, f32[72,128]{1,0:T(8,128)S(1)}, u32[]{:S(2)}, u32[]{:S(2)}) collective-permute-start(f32[72,128]{1,0:T(8,128)S(1)} %get-tuple-element.41), channel_id=1, source_target_pairs={{1,2},{2,1},{3,4},{4,3},{5,6},{6,5},{7,0},{0,7},{9,10},{10,9},{11,... | collective-permute-start | bytes 110600 | tf_op jit(solution)/shard_map/ppermute | solution.py:436
  72.9 6.2 %collective-permute-start.4 = (f32[72,128]{1,0:T(8,128)S(1)}, f32[72,128]{1,0:T(8,128)S(1)}, u32[]{:S(2)}, u32[]{:S(2)}) collective-permute-start(f32[72,128]{1,0:T(8,128)S(1)} %get-tuple-element.41), channel_id=1, source_target_pairs={{0,1},{1,0},{2,3},{3,2},{4,5},{5,4},{6,7},{7,6},{8,9},{9,8},{10,11... | collective-permute-start | bytes 110600 | tf_op jit(solution)/shard_map/ppermute | solution.py:437
  72.9 2.4 %collective-permute-start.5 = (f32[32,128]{1,0:T(8,128)S(1)}, f32[32,128]{1,0:T(8,128)S(1)}, u32[]{:S(2)}, u32[]{:S(2)}) collective-permute-start(f32[32,128]{1,0:T(8,128)S(1)} %get-tuple-element.42), channel_id=1, source_target_pairs={{0,128},{1,129},{2,130},{3,131},{4,132},{5,133},{6,134},{7,135},{8... | collective-permute-start | bytes 49160 | tf_op jit(solution)/shard_map/ppermute | solution.py:438
  82.6 17.6 %copy-start.3 = (f32[1024,128]{1,0:T(8,128)S(1)}, f32[1024,128]{1,0:T(8,128)}, u32[]{:S(2)}) copy-start(f32[1024,128]{1,0:T(8,128)} %copy-done.2) | copy-start | bytes 1572868
  82.6 17.6 %collective-permute-start.6 = (f32[512,128]{1,0:T(8,128)S(1)}, f32[512,128]{1,0:T(8,128)S(1)}, u32[]{:S(2)}, u32[]{:S(2)}) collective-permute-start(f32[512,128]{1,0:T(8,128)S(1)} %get-tuple-element.48), channel_id=1, source_target_pairs={{0,8},{8,0},{16,24},{24,16},{32,40},{40,32},{48,56},{56,48},{64,72... | collective-permute-start | bytes 786440 | tf_op jit(solution)/shard_map/ppermute | solution.py:434
  85.0 15.2 %collective-permute-start.7 = (f32[512,128]{1,0:T(8,128)S(1)}, f32[512,128]{1,0:T(8,128)S(1)}, u32[]{:S(2)}, u32[]{:S(2)}) collective-permute-start(f32[512,128]{1,0:T(8,128)S(1)} %get-tuple-element.49), channel_id=1, source_target_pairs={{8,16},{16,8},{24,32},{32,24},{40,48},{48,40},{56,64},{64,56},{72,... | collective-permute-start | bytes 786440 | tf_op jit(solution)/shard_map/ppermute | solution.py:435
  87.8 12.4 %collective-permute-start.8 = (f32[72,128]{1,0:T(8,128)S(1)}, f32[72,128]{1,0:T(8,128)S(1)}, u32[]{:S(2)}, u32[]{:S(2)}) collective-permute-start(f32[72,128]{1,0:T(8,128)S(1)} %get-tuple-element.50), channel_id=1, source_target_pairs={{1,2},{2,1},{3,4},{4,3},{5,6},{6,5},{7,0},{0,7},{9,10},{10,9},{11,... | collective-permute-start | bytes 110600 | tf_op jit(solution)/shard_map/ppermute | solution.py:436
  92.0 8.3 %collective-permute-start.9 = (f32[72,128]{1,0:T(8,128)S(1)}, f32[72,128]{1,0:T(8,128)S(1)}, u32[]{:S(2)}, u32[]{:S(2)}) collective-permute-start(f32[72,128]{1,0:T(8,128)S(1)} %get-tuple-element.50), channel_id=1, source_target_pairs={{0,1},{1,0},{2,3},{3,2},{4,5},{5,4},{6,7},{7,6},{8,9},{9,8},{10,11... | collective-permute-start | bytes 110600 | tf_op jit(solution)/shard_map/ppermute | solution.py:437
  92.0 2.4 %collective-permute-start.10 = (f32[32,128]{1,0:T(8,128)S(1)}, f32[32,128]{1,0:T(8,128)S(1)}, u32[]{:S(2)}, u32[]{:S(2)}) collective-permute-start(f32[32,128]{1,0:T(8,128)S(1)} %get-tuple-element.51), channel_id=1, source_target_pairs={{0,128},{1,129},{2,130},{3,131},{4,132},{5,133},{6,134},{7,135},{8... | collective-permute-start | bytes 49160 | tf_op jit(solution)/shard_map/ppermute | solution.py:438
  100.2 20.2 %copy-start.13 = (f32[1024,128]{1,0:T(8,128)S(1)}, f32[1024,128]{1,0:T(8,128)}, u32[]{:S(2)}) copy-start(f32[1024,128]{1,0:T(8,128)} %copy-done.12) | copy-start | bytes 1572868
  100.3 20.2 %copy-start.15 = (f32[1024,128]{1,0:T(8,128)S(1)}, f32[1024,128]{1,0:T(8,128)}, u32[]{:S(2)}) copy-start(f32[1024,128]{1,0:T(8,128)} %copy-done.14) | copy-start | bytes 1572868
  100.3 20.2 %copy-start.17 = (f32[1024,128]{1,0:T(8,128)S(1)}, f32[1024,128]{1,0:T(8,128)}, u32[]{:S(2)}) copy-start(f32[1024,128]{1,0:T(8,128)} %copy-done.16) | copy-start | bytes 1572868
  100.3 20.2 %copy-start.19 = (f32[1024,128]{1,0:T(8,128)S(1)}, f32[1024,128]{1,0:T(8,128)}, u32[]{:S(2)}) copy-start(f32[1024,128]{1,0:T(8,128)} %copy-done.18) | copy-start | bytes 1572868
  103.8 16.7 %collective-permute-start.11 = (f32[512,128]{1,0:T(8,128)S(1)}, f32[512,128]{1,0:T(8,128)S(1)}, u32[]{:S(2)}, u32[]{:S(2)}) collective-permute-start(f32[512,128]{1,0:T(8,128)S(1)} %get-tuple-element.57), channel_id=1, source_target_pairs={{0,8},{8,0},{16,24},{24,16},{32,40},{40,32},{48,56},{56,48},{64,72... | collective-permute-start | bytes 786440 | tf_op jit(solution)/shard_map/ppermute | solution.py:434
  104.7 15.7 %collective-permute-start.12 = (f32[512,128]{1,0:T(8,128)S(1)}, f32[512,128]{1,0:T(8,128)S(1)}, u32[]{:S(2)}, u32[]{:S(2)}) collective-permute-start(f32[512,128]{1,0:T(8,128)S(1)} %get-tuple-element.58), channel_id=1, source_target_pairs={{8,16},{16,8},{24,32},{32,24},{40,48},{48,40},{56,64},{64,56},{72,... | collective-permute-start | bytes 786440 | tf_op jit(solution)/shard_map/ppermute | solution.py:435
  107.3 13.1 %collective-permute-start.13 = (f32[72,128]{1,0:T(8,128)S(1)}, f32[72,128]{1,0:T(8,128)S(1)}, u32[]{:S(2)}, u32[]{:S(2)}) collective-permute-start(f32[72,128]{1,0:T(8,128)S(1)} %get-tuple-element.59), channel_id=1, source_target_pairs={{1,2},{2,1},{3,4},{4,3},{5,6},{6,5},{7,0},{0,7},{9,10},{10,9},{11,... | collective-permute-start | bytes 110600 | tf_op jit(solution)/shard_map/ppermute | solution.py:436
  111.5 8.9 %collective-permute-start.14 = (f32[72,128]{1,0:T(8,128)S(1)}, f32[72,128]{1,0:T(8,128)S(1)}, u32[]{:S(2)}, u32[]{:S(2)}) collective-permute-start(f32[72,128]{1,0:T(8,128)S(1)} %get-tuple-element.59), channel_id=1, source_target_pairs={{0,1},{1,0},{2,3},{3,2},{4,5},{5,4},{6,7},{7,6},{8,9},{9,8},{10,11... | collective-permute-start | bytes 110600 | tf_op jit(solution)/shard_map/ppermute | solution.py:437
  111.5 2.1 %collective-permute-start.15 = (f32[32,128]{1,0:T(8,128)S(1)}, f32[32,128]{1,0:T(8,128)S(1)}, u32[]{:S(2)}, u32[]{:S(2)}) collective-permute-start(f32[32,128]{1,0:T(8,128)S(1)} %get-tuple-element.60), channel_id=1, source_target_pairs={{0,128},{1,129},{2,130},{3,131},{4,132},{5,133},{6,134},{7,135},{8... | collective-permute-start | bytes 49160 | tf_op jit(solution)/shard_map/ppermute | solution.py:438
  (8 other events, 6.4 us)

commit v5 on v4

v5 whole, which is shorter than its diff:
```python
import functools

import jax
import jax.numpy as jnp
from jax import lax
from jax.experimental import pallas as pl
from jax.experimental.pallas import tpu as pltpu
from jax.sharding import PartitionSpec as P

LANES = 128
SUBS = 8
BATCH = 4
VMEM_LIMIT = 20 * 1024 * 1024
VMEM_WHOLE = 58 * 1024 * 1024


def split3(x):
    hi = x.astype(jnp.bfloat16)
    rest = x - hi.astype(jnp.float32)
    mid = rest.astype(jnp.bfloat16)
    low = (rest - mid.astype(jnp.float32)).astype(jnp.bfloat16)
    return [hi, mid, low]


def pack_kernel(slots, rows_hbm, owner_hbm, cell_hbm, out_ref, rows_ref, owner_ref, cell_ref, sems):
    steps, count, width = rows_ref.shape
    owners = count
    parts = width // LANES
    stride = out_ref.shape[0] // owners
    small = [
        pltpu.make_async_copy(owner_hbm, owner_ref, sems.at[steps]),
        pltpu.make_async_copy(cell_hbm, cell_ref, sems.at[steps + 1]),
    ]
    large = [
        pltpu.make_async_copy(rows_hbm.at[step], rows_ref.at[step], sems.at[step]) for step in range(steps)
    ]
    for copy in small + large:
        copy.start()
    dest = lax.broadcasted_iota(jnp.int32, (owners, count), 0)
    lane = lax.broadcasted_iota(jnp.int32, (owners, count), 1)
    before = (dest < lane).astype(jnp.bfloat16)
    cells = jnp.zeros((owners, LANES), jnp.float32)
    for copy in small:
        copy.wait()
    for step in range(steps):
        hits = owner_ref[step] == dest
        hits_f = hits.astype(jnp.float32)
        prior = jnp.dot(hits_f.astype(jnp.bfloat16), before, preferred_element_type=jnp.float32)
        large[step].wait()
        terms = jnp.concatenate(split3(rows_ref[step]), axis=0)
        marks = (cell_ref[step] + 1).astype(jnp.float32)
        for k in range(slots):
            slot = step * slots + k
            pick = jnp.where(prior == float(k), hits_f, 0.0)
            pick_b = pick.astype(jnp.bfloat16)
            out = jnp.dot(
                jnp.concatenate([pick_b] * 3, axis=1), terms, preferred_element_type=jnp.float32
            )
            for part in range(parts):
                out_ref[pl.ds(slot * parts + part, owners, stride=stride), :] = out[
                    :, part * LANES : (part + 1) * LANES
                ]
            mark = jnp.sum(pick * marks, axis=1, keepdims=True)
            cells = jnp.where(lane == slot, mark, cells)
    out_ref[pl.ds(stride - 1, owners, stride=stride), :] = cells


def spread_rows(step, slots, got_ref, width):
    parts = width // LANES
    stride = parts * slots * 3 + 1
    sources = got_ref.shape[0] // stride
    marks = got_ref[pl.ds(stride - 1, sources, stride=stride), :]
    where_to = lax.broadcasted_iota(jnp.int32, (sources, SUBS * LANES), 1)
    terms, onehots = [], []
    for k in range(slots):
        slot = step * slots + k
        cols = []
        for part in range(parts):
            block = got_ref[pl.ds(slot * parts + part, sources, stride=stride), :]
            cols.append(block.T)
        turned = jnp.concatenate(cols, axis=0)
        terms += split3(turned)
        cell = marks[:, slot : slot + 1].astype(jnp.int32) - 1
        onehot = (cell == where_to).astype(jnp.float32).astype(jnp.bfloat16)
        onehots += [onehot] * 3
    return jnp.dot(
        jnp.concatenate(terms, axis=1),
        jnp.concatenate(onehots, axis=0),
        preferred_element_type=jnp.float32,
    )


def column_halves(load, fields, groups, ys, halves):
    lane = lax.broadcasted_iota(jnp.int32, (SUBS, LANES), 1)
    for f in range(fields):
        for group in groups:
            for y in ys:
                at = group * SUBS + y
                plane = load(f, group, y)
                turned = plane if at == 0 else pltpu.roll(plane, at, 1)
                here = (lane == at) | (lane == (at - 1) % LANES)
                halves[2 * f + at % 2] = jnp.where(here, turned, halves[2 * f + at % 2])
    return halves


def columns_store(halves, rim, column_ref, fields):
    even = lax.broadcasted_iota(jnp.int32, (SUBS, LANES), 1) % 2 == 0
    for f in range(fields):
        a, b = halves[2 * f], halves[2 * f + 1]
        column_ref[f * SUBS : (f + 1) * SUBS, :] = jnp.where(even, a, b)
        column_ref[(fields + f) * SUBS : (fields + f + 1) * SUBS, :] = jnp.where(even, b, a)
    column_ref[2 * fields * SUBS :, :] = rim


def column_corrections(lon_even, first_ref, second_ref, own_ref, up_rim, fields):
    even = lax.broadcasted_iota(jnp.int32, (SUBS, LANES), 1) % 2 == 0

    def rows(i):
        one, two = first_ref[i * SUBS : (i + 1) * SUBS, :], second_ref[i * SUBS : (i + 1) * SUBS, :]
        return jnp.where(lon_even, one, two), jnp.where(lon_even, two, one)

    rim = pltpu.roll(rows(2 * fields)[0], 1, 1)
    halves = []
    for f in range(fields):
        from_west = pltpu.roll(rows(fields + f)[0], 1, 1)
        from_east = pltpu.roll(rows(f)[1], LANES - 1, 1)
        own_west = own_ref[f * SUBS : (f + 1) * SUBS, :]
        own_east = own_ref[(fields + f) * SUBS : (fields + f + 1) * SUBS, :]
        west = rim * (own_west - from_west)
        east = up_rim * (from_east - own_east)
        halves += [jnp.where(even, west, east), jnp.where(even, east, west)]
    return halves


def turn_to_first(col, at):
    return col if at == 0 else pltpu.roll(col, LANES - at, 1)


def rows_of(base, group):
    if isinstance(group, int):
        return pl.ds(base + group * SUBS, SUBS)
    return pl.ds(pl.multiple_of(base + group * SUBS, SUBS), SUBS)


def slabs_store(lat_even, m_ref, first_ref, second_ref, width):
    for i in range(width // SUBS):
        rows = slice(i * SUBS, (i + 1) * SUBS)
        south = m_ref[rows, :]
        north = m_ref[(SUBS - 1) * width + i * SUBS : (SUBS - 1) * width + (i + 1) * SUBS, :]
        first_ref[rows, :] = jnp.where(lat_even, north, south)
        second_ref[rows, :] = jnp.where(lat_even, south, north)


def parity(ref, i):
    return jnp.full((SUBS, LANES), ref[i], jnp.int32) == 0


def low_store(m_ref, low_ref, fields, levels):
    for f in range(fields):
        low_ref[f * SUBS : (f + 1) * SUBS, :] = m_ref[
            pl.ds(f * levels + levels - 1, SUBS, stride=fields * levels), :
        ]


def first_kernel(
    step, slots, fields, levels, odd_ref, got_ref, mask_ref, rim_ref, m_ref, slab1_ref, slab2_ref, column_ref, low_ref
):
    width = fields * levels
    out = spread_rows(step, slots, got_ref, width)
    for y in range(SUBS):
        m_ref[y * width : (y + 1) * width, :] = out[:, y * LANES : (y + 1) * LANES] * mask_ref[y : y + 1, :]
    slabs_store(parity(odd_ref, 0), m_ref, slab1_ref, slab2_ref, width)
    halves = column_halves(
        lambda f, group, y: m_ref[rows_of((y * fields + f) * levels, group), :],
        fields,
        range(levels // SUBS),
        range(SUBS),
        [jnp.zeros((SUBS, LANES), jnp.float32)] * (2 * fields),
    )
    columns_store(halves, rim_ref[step * SUBS : (step + 1) * SUBS, :], column_ref, fields)
    low_store(m_ref, low_ref, fields, levels)


def forcing_kernel(step, slots, width, got_ref, f_ref):
    out = spread_rows(step, slots, got_ref, width)
    for y in range(SUBS):
        f_ref[y * width : (y + 1) * width, :] = out[:, y * LANES : (y + 1) * LANES]


def rim_kernel(vel_ref, dif_ref, rim_ref, vel_row, dif_row, sems):
    copies = [
        pltpu.make_async_copy(src.at[:, 1, :, SUBS - 1, :], dst, sems.at[i])
        for i, (src, dst) in enumerate(((vel_ref, vel_row), (dif_ref, dif_row)))
    ]
    for copy in copies:
        copy.start()
    for copy in copies:
        copy.wait()
    steps, levels, lanes = vel_row.shape
    rim_ref[...] = (jnp.minimum(vel_row[...], 0.0) - dif_row[...]).reshape(steps * levels, lanes)


def coefficient_kernel(steps, levels, vel_ref, dif_ref, open_ref, mask_ref, *outs):
    tables, (rim_ref, up_rim_ref, mask_column_ref) = outs[:-3], outs[-3:]
    lane = lax.broadcasted_iota(jnp.int32, (SUBS, LANES), 1)
    tall = lax.broadcasted_iota(jnp.int32, (levels, LANES), 1)
    for step in range(steps):
        up_e_ref, down_w_ref, up_n_ref, down_n_ref = tables[4 * step : 4 * step + 4]
        east, north = 2 * step * levels * SUBS, (2 * step + 1) * levels * SUBS
        rim = jnp.zeros((SUBS, LANES), jnp.float32)
        up_rim = rim
        for y in range(SUBS):
            rows = slice(y * levels, (y + 1) * levels)
            w = vel_ref[pl.ds(east + y, levels, stride=SUBS), :]
            k = dif_ref[pl.ds(east + y, levels, stride=SUBS), :]
            up = jnp.maximum(w, 0.0) + k
            down = jnp.minimum(w, 0.0) - k
            for group in range(levels // SUBS):
                at = group * SUBS + y
                part = slice(group * SUBS, (group + 1) * SUBS)
                rim = jnp.where(lane == (at - 1) % LANES, pltpu.roll(down[part, :], at, 1) if at else down[part, :], rim)
                up_rim = jnp.where(lane == (at - 1) % LANES, pltpu.roll(up[part, :], at, 1) if at else up[part, :], up_rim)
            up_e_ref[rows, :] = jnp.where(tall == LANES - 1, 0.0, up)
            down_w_ref[rows, :] = jnp.where(tall == 0, 0.0, pltpu.roll(down, 1, 1))
            w = vel_ref[pl.ds(north + y, levels, stride=SUBS), :]
            k = dif_ref[pl.ds(north + y, levels, stride=SUBS), :]
            up = jnp.maximum(w, 0.0) + k
            up_n_ref[rows, :] = up * open_ref[...] if y == SUBS - 1 else up
            down_n_ref[rows, :] = jnp.minimum(w, 0.0) - k
        rim_ref[step * SUBS : (step + 1) * SUBS, :] = rim
        up_rim_ref[step * SUBS : (step + 1) * SUBS, :] = up_rim
    west, east = jnp.zeros((SUBS, LANES), jnp.float32), jnp.zeros((SUBS, LANES), jnp.float32)
    for group in range(levels // SUBS):
        for y in range(SUBS):
            at = group * SUBS + y
            row = jnp.broadcast_to(mask_ref[y : y + 1, :], (SUBS, LANES))
            turned = pltpu.roll(row, at, 1) if at else row
            west = jnp.where(lane == at, turned, west)
            east = jnp.where(lane == (at - 1) % LANES, turned, east)
    mask_column_ref[:SUBS, :] = west
    mask_column_ref[SUBS:, :] = east


def settled(f, group, y, at, p_ref, m_ref, halves, edge, coupled, up_n_ref, rim_row, from_south, from_north, fields, levels):
    rows = rows_of((y * fields + f) * levels, group)
    result = p_ref[rows, :] + jnp.where(edge, turn_to_first(halves[2 * f + at % 2], at), 0.0)
    if y == 0:
        result = result + rim_row(group) * (m_ref[rows, :] - from_south(f, group))
    if y == SUBS - 1:
        up = up_n_ref[rows_of(y * levels, group), :]
        result = result + up * (from_north(f, group) - m_ref[rows, :])
    if isinstance(group, int) and group == 0:
        sub = lax.broadcasted_iota(jnp.int32, (SUBS, LANES), 0)
        result = result + jnp.where(sub == 0, coupled(f, y), 0.0)
    return result


def slab_readers(lat_even, slab1_ref, slab2_ref, levels):
    def south(f, group):
        rows = rows_of(f * levels, group)
        return jnp.where(lat_even, slab2_ref[rows, :], slab1_ref[rows, :])

    def north(f, group):
        rows = rows_of(f * levels, group)
        return jnp.where(lat_even, slab1_ref[rows, :], slab2_ref[rows, :])

    return south, north


def coupling(air_ref, sea_ref, from_low_ref, fields):
    sea = sea_ref[...]
    planes = []
    for g in range(fields):
        total = jnp.zeros((SUBS, LANES), jnp.float32)
        for f in range(fields):
            total = total + air_ref[f, g] * from_low_ref[f * SUBS : (f + 1) * SUBS, :]
        planes.append(sea * total)
    return planes


def partial_kernel(settle, step, fields, levels, mix_ref, odd_ref, m_ref, tables, forcing_ref, before, outs):
    up_e_ref, down_w_ref, up_n_ref, down_n_ref = tables
    width = fields * levels
    lane = lax.broadcasted_iota(jnp.int32, (SUBS, LANES), 1)
    edge = (lane == 0) | (lane == LANES - 1)
    batches = levels // (SUBS * BATCH)
    if settle:
        old_p_ref, old_m_ref, old_up_n_ref, slab1_ref, slab2_ref, half_ref, couple_ref, rim_ref, mask_ref = before
        south, north = slab_readers(parity(odd_ref, 0), slab1_ref, slab2_ref, levels)

        def settle_batch(group0, halves):
            for u in range(BATCH):
                group = group0 + u
                for y in range(SUBS):
                    for f in range(fields):
                        plane = settled(
                            f,
                            group,
                            y,
                            u * SUBS + y,
                            old_p_ref,
                            old_m_ref,
                            halves,
                            edge,
                            lambda f, y: couple_ref[f * SUBS + y : f * SUBS + y + 1, :],
                            old_up_n_ref,
                            lambda group: rim_ref[rows_of((step + 1) * levels, group), :],
                            south,
                            north,
                            fields,
                            levels,
                        )
                        m_ref[rows_of((y * fields + f) * levels, group), :] = plane * mask_ref[y : y + 1, :]
            return tuple(pltpu.roll(h, LANES - BATCH * SUBS, 1) for h in halves)

        halves = settle_batch(0, [half_ref[i * SUBS : (i + 1) * SUBS, :] for i in range(2 * fields)])
        lax.fori_loop(1, batches, lambda i, halves: settle_batch(i * BATCH, halves), halves)
    p_ref = outs[0]
    mix = [[mix_ref[f, g] for g in range(fields)] for f in range(fields)]

    def body(i, carry):
        for u in range(BATCH):
            group = i * BATCH + u
            for y in range(SUBS):
                up_e = up_e_ref[rows_of(y * levels, group), :]
                down_w = down_w_ref[rows_of(y * levels, group), :]
                planes = [m_ref[rows_of(y * width + f * levels, group), :] for f in range(fields)]
                for g in range(fields):
                    m = planes[g]
                    rows = rows_of(y * width + g * levels, group)
                    result = m if forcing_ref is None else m + forcing_ref[rows, :]
                    for f in range(fields):
                        result = result + mix[f][g] * planes[f]
                    result = result + up_e * (pltpu.roll(m, LANES - 1, 1) - m)
                    result = result + down_w * (m - pltpu.roll(m, 1, 1))
                    if y < SUBS - 1:
                        up_n = up_n_ref[rows_of(y * levels, group), :]
                        result = result + up_n * (m_ref[rows_of((y + 1) * width + g * levels, group), :] - m)
                    if y > 0:
                        down_s = down_n_ref[rows_of((y - 1) * levels, group), :]
                        result = result + down_s * (m - m_ref[rows_of((y - 1) * width + g * levels, group), :])
                    p_ref[rows, :] = result
        return carry

    lax.fori_loop(0, batches, body, 0)
    if len(outs) > 1:
        halves = column_halves(
            lambda f, group, y: p_ref[rows_of((y * fields + f) * levels, group), :],
            fields,
            range(levels // SUBS),
            range(SUBS),
            [jnp.zeros((SUBS, LANES), jnp.float32)] * (2 * fields),
        )
        for i, half in enumerate(halves):
            outs[1][i * SUBS : (i + 1) * SUBS, :] = half


def start_kernel(step, fields, levels, mix_ref, odd_ref, m_ref, a_ref, b_ref, c_ref, d_ref, f_ref, *outs):
    partial_kernel(False, step, fields, levels, mix_ref, odd_ref, m_ref, (a_ref, b_ref, c_ref, d_ref), f_ref, None, outs)


def inner_kernel(last, step, fields, levels, mix_ref, odd_ref, a_ref, b_ref, c_ref, d_ref, *rest):
    tables = (a_ref, b_ref, c_ref, d_ref)
    before, rest = rest[:9], rest[9:]
    f_ref = None
    if not last:
        f_ref, rest = rest[0], rest[1:]
    partial_kernel(True, step, fields, levels, mix_ref, odd_ref, rest[0], tables, f_ref, before, rest[1:])


def edge_kernel(
    step,
    fields,
    levels,
    air_ref,
    odd_ref,
    p_ref,
    p_half_ref,
    m_ref,
    up_n_ref,
    own_column_ref,
    rim_ref,
    up_rim_ref,
    north_rim_ref,
    sea_ref,
    mask_ref,
    mask_column_ref,
    from_slab1_ref,
    from_slab2_ref,
    from_column1_ref,
    from_column2_ref,
    from_low_ref,
    slab1_ref,
    slab2_ref,
    column_ref,
    low_ref,
    half_ref,
    couple_ref,
):
    lane = lax.broadcasted_iota(jnp.int32, (SUBS, LANES), 1)
    edge = (lane == 0) | (lane == LANES - 1)
    even = lane % 2 == 0
    lat_even, lon_even = parity(odd_ref, 0), parity(odd_ref, 1)
    south, north = slab_readers(lat_even, from_slab1_ref, from_slab2_ref, levels)
    coupled = coupling(air_ref, sea_ref, from_low_ref, fields)
    for g in range(fields):
        couple_ref[g * SUBS : (g + 1) * SUBS, :] = coupled[g]
    halves = column_corrections(
        lon_even,
        from_column1_ref,
        from_column2_ref,
        own_column_ref,
        up_rim_ref[step * SUBS : (step + 1) * SUBS, :],
        fields,
    )
    for i, half in enumerate(halves):
        half_ref[i * SUBS : (i + 1) * SUBS, :] = half
    west, east = mask_column_ref[:SUBS, :], mask_column_ref[SUBS:, :]
    masks = [jnp.where(even, west, east), jnp.where(even, east, west)]
    following = [
        (p_half_ref[i * SUBS : (i + 1) * SUBS, :] + half) * masks[i % 2] for i, half in enumerate(halves)
    ]
    groups = levels // SUBS

    def plane(f, group, y):
        full = settled(
            f,
            group,
            y,
            group * SUBS + y,
            p_ref,
            m_ref,
            halves,
            edge,
            lambda f, y: coupled[f][y : y + 1, :],
            up_n_ref,
            lambda group: north_rim_ref[rows_of(step * levels, group), :],
            south,
            north,
            fields,
            levels,
        )
        return full * mask_ref[y : y + 1, :]

    for f in range(fields):
        for group in range(groups):
            ends = [plane(f, group, 0), plane(f, group, SUBS - 1)]
            rows = rows_of(f * levels, group)
            slab1_ref[rows, :] = jnp.where(lat_even, ends[1], ends[0])
            slab2_ref[rows, :] = jnp.where(lat_even, ends[0], ends[1])
            whole = {0: ends[0], SUBS - 1: ends[1]}
            if group == 0 or group == groups - 1:
                for y in range(1, SUBS - 1):
                    whole[y] = plane(f, group, y)
            if group == groups - 1:
                for y in range(SUBS):
                    low_ref[f * SUBS + y : f * SUBS + y + 1, :] = whole[y][SUBS - 1 :, :]
            ys = range(SUBS) if group == 0 else (0, SUBS - 1)
            part = column_halves(
                lambda _, group, y, whole=whole: whole[y], 1, (group,), ys, following[2 * f : 2 * f + 2]
            )
            following[2 * f : 2 * f + 2] = part
    columns_store(following, rim_ref[(step - 1) * SUBS : step * SUBS, :], column_ref, fields)


def last_kernel(
    fields,
    levels,
    air_ref,
    odd_ref,
    p_ref,
    m_ref,
    up_n_ref,
    own_column_ref,
    up_rim_ref,
    north_rim_ref,
    sea_ref,
    from_slab1_ref,
    from_slab2_ref,
    from_column1_ref,
    from_column2_ref,
    from_low_ref,
    sent_ref,
    out_ref,
    sems,
):
    lane = lax.broadcasted_iota(jnp.int32, (SUBS, LANES), 1)
    edge = (lane == 0) | (lane == LANES - 1)
    south, north = slab_readers(parity(odd_ref, 0), from_slab1_ref, from_slab2_ref, levels)
    coupled = coupling(air_ref, sea_ref, from_low_ref, fields)
    halves = column_corrections(
        parity(odd_ref, 1), from_column1_ref, from_column2_ref, own_column_ref, up_rim_ref[:SUBS, :], fields
    )
    batches = levels // (SUBS * BATCH)

    def pieces(i):
        for f in range(fields):
            rows = pl.ds((f * levels + i * BATCH * SUBS) * SUBS, BATCH * SUBS * SUBS)
            yield pltpu.make_async_copy(out_ref.at[rows], sent_ref.at[rows], sems.at[f * batches + i])

    def batch(i, halves):
        for u in range(BATCH):
            group = i * BATCH + u
            for y in range(SUBS):
                for f in range(fields):
                    out_ref[pl.ds(f * levels * SUBS + y + group * (SUBS * SUBS), SUBS, stride=SUBS), :] = settled(
                        f,
                        group,
                        y,
                        u * SUBS + y,
                        p_ref,
                        m_ref,
                        halves,
                        edge,
                        lambda f, y: coupled[f][y : y + 1, :],
                        up_n_ref,
                        lambda group: north_rim_ref[rows_of(0, group), :],
                        south,
                        north,
                        fields,
                        levels,
                    )
        for copy in pieces(i):
            copy.start()
        return tuple(pltpu.roll(h, LANES - BATCH * SUBS, 1) for h in halves)

    lax.fori_loop(1, batches, batch, batch(0, halves))
    for i in range(batches):
        for copy in pieces(i):
            copy.wait()


def params(limit=VMEM_LIMIT):
    return pltpu.CompilerParams(vmem_limit_bytes=limit)


def swaps(axis, start, closed):
    count = lax.axis_size(axis)
    pairs = []
    for i in range(start, count if closed else count - 1, 2):
        j = (i + 1) % count
        pairs += [(i, j), (j, i)]
    return pairs


def shards(innovations, obs_owner, obs_cell, velocity, diffusion, mixing, air_sea, sea_mask):
    lat_count = lax.axis_size("lat")
    lon_count = lax.axis_size("lon")
    owners = lat_count * lon_count
    steps, levels, lat_rows, lon_cols = (velocity.shape[i] for i in (1, 3, 4, 5))
    fields = mixing.shape[1]
    width = fields * levels
    count = innovations.shape[2]
    slots = 2
    assert (lat_rows, lon_cols, levels, count, owners, steps) == (SUBS, LANES, LANES, LANES, LANES, 3)
    f32 = functools.partial(jax.ShapeDtypeStruct, dtype=jnp.float32)
    stride = steps * slots * width // LANES + 1

    is_ocean = lax.axis_index("comp") == 1
    sea_float = sea_mask.astype(jnp.float32)
    mask = jnp.where(is_ocean, sea_float, jnp.ones_like(sea_float))
    opened = jnp.full((1, lon_cols), lax.axis_index("lat") < lat_count - 1, jnp.float32)
    smem = pl.BlockSpec(memory_space=pltpu.SMEM)
    vmem = pl.BlockSpec(memory_space=pltpu.VMEM)
    anywhere = pl.BlockSpec(memory_space=pltpu.HBM)
    speeds, diffuse = velocity[0], diffusion[0]

    north_rims = pl.pallas_call(
        rim_kernel,
        out_shape=f32((steps * levels, LANES)),
        in_specs=[anywhere] * 2,
        scratch_shapes=[pltpu.VMEM((steps, levels, LANES), jnp.float32)] * 2 + [pltpu.SemaphoreType.DMA((2,))],
        compiler_params=params(VMEM_WHOLE),
        name="rim",
    )(speeds, diffuse)
    north_rims = lax.ppermute(
        north_rims, "lat", [(i, i + 1) for i in range(lat_count - 1)]
    )

    sent = pl.pallas_call(
        functools.partial(pack_kernel, slots),
        out_shape=f32((owners * stride, LANES)),
        in_specs=[anywhere] * 3,
        scratch_shapes=[
            pltpu.VMEM((steps, count, width), jnp.float32),
            pltpu.VMEM((steps, 1, count), jnp.int32),
            pltpu.VMEM((steps, 1, count), jnp.int32),
            pltpu.SemaphoreType.DMA((steps + 2,)),
        ],
        compiler_params=params(VMEM_WHOLE),
        name="pack",
    )(
        innovations[0],
        obs_owner.reshape(steps, 1, count),
        obs_cell.reshape(steps, 1, count),
    )
    got = lax.all_to_all(
        sent.reshape(owners, 1, stride * LANES), ("lat", "lon"), split_axis=0, concat_axis=0, tiled=True
    ).reshape(owners * stride, LANES)

    table = f32((levels * SUBS, LANES))
    *tables, east_rims, up_rims, mask_columns = pl.pallas_call(
        functools.partial(coefficient_kernel, steps, levels),
        out_shape=[table] * (4 * steps) + [f32((steps * SUBS, LANES))] * 2 + [f32((2 * SUBS, LANES))],
        compiler_params=params(),
        cost_estimate=pl.CostEstimate(flops=1 << 22, bytes_accessed=1 << 23, transcendentals=0),
        name="coefficients",
    )(
        speeds.reshape(steps * 2 * levels * SUBS, LANES),
        diffuse.reshape(steps * 2 * levels * SUBS, LANES),
        opened,
        mask,
    )
    odd = jnp.stack([lax.axis_index("lat") % 2, lax.axis_index("lon") % 2]).astype(jnp.int32)
    whole = f32((width * SUBS, LANES))
    half = f32((2 * fields * SUBS, LANES))
    low_shape = f32((fields * SUBS, LANES))
    message = [f32((width, LANES)), f32((width, LANES)), f32(((2 * fields + 1) * SUBS, LANES)), low_shape]
    busy = pl.CostEstimate(flops=1 << 25, bytes_accessed=1 << 23, transcendentals=0)

    m, *edges = pl.pallas_call(
        functools.partial(first_kernel, steps - 1, slots, fields, levels),
        out_shape=[whole, *message],
        in_specs=[smem] + [vmem] * 3,
        compiler_params=params(),
        name="first",
    )(odd, got, mask, east_rims)
    before = None
    for step in reversed(range(steps)):
        slab1, slab2, columns, low = edges
        halos = [
            lax.ppermute(slab1, "lat", swaps("lat", 0, False)),
            lax.ppermute(slab2, "lat", swaps("lat", 1, False)),
            lax.ppermute(columns, "lon", swaps("lon", 1, True)),
            lax.ppermute(columns, "lon", swaps("lon", 0, True)),
            lax.ppermute(low, "comp", [(0, 1)]),
        ]
        last = step == 0
        forcing = []
        if not last:
            forcing.append(
                pl.pallas_call(
                    functools.partial(forcing_kernel, step - 1, slots, width),
                    out_shape=whole,
                    compiler_params=params(),
                    cost_estimate=busy,
                    name="forcing",
                )(got)
            )
        step_tables = tables[4 * step : 4 * step + 4]
        if before is None:
            p, p_half = pl.pallas_call(
                functools.partial(start_kernel, step, fields, levels),
                out_shape=[whole, half],
                in_specs=[smem] * 2 + [vmem] * 6,
                compiler_params=params(),
                cost_estimate=busy,
                name="start",
            )(mixing[0], odd, m, *step_tables, *forcing)
        else:
            operands = [mixing[0], odd, *step_tables, *before, *forcing]
            m, p, *rest = pl.pallas_call(
                functools.partial(inner_kernel, last, step, fields, levels),
                out_shape=[whole, whole] + [half] * (not last),
                in_specs=[smem] * 2 + [vmem] * (len(operands) - 2),
                compiler_params=params(),
                cost_estimate=busy,
                name="inner",
            )(*operands)
            if not last:
                (p_half,) = rest
        if last:
            break
        operands = [
            air_sea,
            odd,
            p,
            p_half,
            m,
            step_tables[2],
            columns,
            east_rims,
            up_rims,
            north_rims,
            sea_float,
            mask,
            mask_columns,
            *halos,
        ]
        *edges, halves, coupled = pl.pallas_call(
            functools.partial(edge_kernel, step, fields, levels),
            out_shape=[*message, half, low_shape],
            in_specs=[smem] * 2 + [vmem] * (len(operands) - 2),
            compiler_params=params(),
            name="edge",
        )(*operands)
        before = [p, m, step_tables[2], halos[0], halos[1], halves, coupled, north_rims, mask]
    operands = [air_sea, odd, p, m, tables[2], columns, up_rims, north_rims, sea_float, *halos]
    m = pl.pallas_call(
        functools.partial(last_kernel, fields, levels),
        out_shape=whole,
        in_specs=[smem] * 2 + [vmem] * (len(operands) - 2),
        out_specs=anywhere,
        scratch_shapes=[
            pltpu.VMEM((width * SUBS, LANES), jnp.float32),
            pltpu.SemaphoreType.DMA((width // (BATCH * SUBS),)),
        ],
        compiler_params=params(),
        name="last",
    )(*operands)
    return m.reshape(1, fields, levels, lat_rows, lon_cols)


def solution(mesh):
    return jax.shard_map(
        shards,
        mesh=mesh,
        in_specs=(
            P("comp", None, ("lat", "lon"), None),
            P("comp", None, ("lat", "lon"), None),
            P("comp", None, ("lat", "lon")),
            P("comp", None, None, None, "lat", "lon"),
            P("comp", None, None, None, "lat", "lon"),
            P("comp", None, None),
            P(),
            P("lat", "lon"),
        ),
        out_specs=P("comp", None, None, "lat", "lon"),
        check_vma=False,
    )
```

time: 125 us -> 129 us (1.032)
  Pallas kernels: 21.5 us -> 29.2 us
  waiting for transfers between devices: 42.3 us -> 38.2 us
    ppermute x3, waiting for transfers between devices: 16.4 us -> 4.09 us  [shards(): lax.ppermute(columns, 'lon', swaps('lon', 1, True))]
    pallas_call x3 -> x6, Pallas kernels: 10.6 us -> 17.2 us  [the longest x2 6.7 us: shards(): pl.pallas_call(functools.partial(inner_kernel, last, step, fields, levels...]
    ppermute x1, waiting for transfers between devices: 0.01 us -> 4.82 us  [shards(): lax.ppermute(north_rims, 'lat', [(i, i + 1) for i in range(lat_count - 1)])]
    all_to_all x1, waiting for transfers between devices: 25.1 us -> 29.2 us  [shards(): lax.all_to_all(sent.reshape(owners, 1, stride * LANES), ('lat', 'lon'), s...]
    ppermute x1, starting transfers between devices: 3.43 us -> 2.05 us  [shards(): lax.ppermute(north_rims, 'lat', [(i, i + 1) for i in range(lat_count - 1)])]
  transfers between devices with their start and end apart: 17 -> 17, of which waited for: 5 -> 4; matrix products, arithmetic and copies ran while one was open for 0% -> 0% of each run, Pallas kernels for 6% -> 12%
where the time goes in v5:
time: 129 us; the launch traced here: 127 us
  starting transfers between devices  48 us (37%)
  waiting for transfers between devices  38.2 us (30%)
  Pallas kernels  29.2 us (23%)
  local copies, waits for them, and re-layouts  11.1 us (9%)
    all_to_all x1, waiting for transfers between devices, shards(): lax.all_to_all(sent.reshape(owners, 1, stride * LANES), ('lat', 'lon'), s...  29.2 us
    all_to_all x1, starting transfers between devices, shards(): lax.all_to_all(sent.reshape(owners, 1, stride * LANES), ('lat', 'lon'), s...  15.5 us
    ppermute x3, starting transfers between devices, shards(): lax.ppermute(columns, 'lon', swaps('lon', 1, True))  11.5 us
    unnamed x46, local copies, waits for them, and re-layouts  11.1 us
    ppermute x3, starting transfers between devices, shards(): lax.ppermute(slab2, 'lat', swaps('lat', 1, False))  10.4 us
    pallas_call x2, Pallas kernels, shards(): pl.pallas_call(functools.partial(inner_kernel, last, step, fields, levels...  6.7 us
    pallas_call x2, Pallas kernels, shards(): pl.pallas_call(functools.partial(edge_kernel, step, fields, levels), out_...  5.27 us
    ppermute x1, waiting for transfers between devices, shards(): lax.ppermute(north_rims, 'lat', [(i, i + 1) for i in range(lat_count - 1)])  4.82 us
  transfers between devices with their start and end apart: 17, of which 4 were waited for; matrix products, arithmetic and copies ran while one was open for 0% of the time, Pallas kernels for 12%

profile of v5, /device:TPU:8, one launch (start us, length us, event | category | flops | bytes accessed | tf_op | source)
XLA Modules:
  0.0 127.2 jit_solution(10706476240946011398)
XLA Ops:
  0.0 3.2 %pack.1 = f32[3200,128]{1,0:T(8,128)} custom-call(f32[3,128,512]{2,1,0:T(8,128)} %bitcast.24, s32[3,1,128]{2,1,0:T(1,128)} %bitcast.25, s32[3,1,128]{2,1,0:T(1,128)} %bitcast.26), custom_call_target="tpu_custom_call" | custom-call | tf_op jit(solution)/shard_map/pack/pallas_call | solution.py:580
  3.2 15.5 %all-to-all-start = ((f32[128,1,3200]{2,1,0:T(1,128)}), f32[128,1,3200]{2,1,0:T(1,128)S(1)}, u32[]{:S(2)}, u32[]{:S(2)}) async-start(f32[128,1,3200]{2,1,0:T(1,128)} %bitcast.23), calls=%async_computation | async-start | bytes 3276800 | tf_op jit(solution)/shard_map/all_to_all | solution.py:597
  18.7 1.9 %copy-done = f32[1,3,2,128,8,128]{5,4,3,2,1,0:T(8,128)S(1)} copy-done((f32[1,3,2,128,8,128]{5,4,3,2,1,0:T(8,128)S(1)}, f32[1,3,2,128,8,128]{5,4,3,2,1,0:T(8,128)}, u32[]{:S(2)}) %copy-start) | copy-done | bytes 3145752
  20.6 1.9 %copy-done.1 = f32[1,3,2,128,8,128]{5,4,3,2,1,0:T(8,128)S(1)} copy-done((f32[1,3,2,128,8,128]{5,4,3,2,1,0:T(8,128)S(1)}, f32[1,3,2,128,8,128]{5,4,3,2,1,0:T(8,128)}, u32[]{:S(2)}) %copy-start.1) | copy-done | bytes 3145752
  22.5 2.2 %coefficients.1 = (f32[1024,128]{1,0:T(8,128)S(1)}, f32[1024,128]{1,0:T(8,128)S(1)}, f32[1024,128]{1,0:T(8,128)S(1)}, f32[1024,128]{1,0:T(8,128)S(1)}, f32[1024,...) custom-call(f32[6144,128]{1,0:T(8,128)S(1)} %bitcast.17, ...), custom_call_target="tpu_custom_call" | custom-call | flops 4194304 | bytes 8388608 | tf_op jit(solution)/shard_map/coefficients/pallas_call | solution.py:602
  32.1 29.2 %all-to-all-done = f32[128,1,3200]{2,1,0:T(1,128)S(1)} async-done(((f32[128,1,3200]{2,1,0:T(1,128)}), f32[128,1,3200]{2,1,0:T(1,128)S(1)}, u32[]{:S(2)}, u32[]{:S(2)}) %all-to-all-start) | async-done | bytes 1638432 | tf_op jit(solution)/shard_map/all_to_all | solution.py:597
  61.3 2.7 %first.1 = (f32[4096,128]{1,0:T(8,128)S(1)}, f32[512,128]{1,0:T(8,128)}, f32[512,128]{1,0:T(8,128)}, f32[72,128]{1,0:T(8,128)S(1)}, f32[32,128]{1,0:T(8,128)S(1)}) custom-call(s32[2]{0:T(128)S(1)} %pad_add_fusion.odd_ref, f32[3200,128]{1,0:T(8,128)S(1)} %bitcast.13, f32[8,128]{1,0:T(8,128)S(1)} %broadcast_select_fusion.mask_ref.rest_8_, ...), custom_call_target="tpu_custom_call" | custom-call | tf_op jit(solution)/shard_map/first/pallas_call | solution.py:621
  64.0 5.4 %collective-permute-start.1 = (f32[512,128]{1,0:T(8,128)}, f32[512,128]{1,0:T(8,128)S(1)}, u32[]{:S(2)}, u32[]{:S(2)}) collective-permute-start(f32[512,128]{1,0:T(8,128)} %get-tuple-element.60), channel_id=1, source_target_pairs={{8,16},{16,8},{24,32},{32,24},{40,48},{48,40},{56,64},{64,56},{72,... | collective-permute-start | bytes 786440 | tf_op jit(solution)/shard_map/ppermute | solution.py:633
  69.4 1.8 %rim.1 = f32[384,128]{1,0:T(8,128)} custom-call(f32[3,2,128,8,128]{4,3,2,1,0:T(8,128)} %bitcast.16, f32[3,2,128,8,128]{4,3,2,1,0:T(8,128)} %bitcast.18), custom_call_target="tpu_custom_call" | custom-call | tf_op jit(solution)/shard_map/rim/pallas_call | solution.py:568
  71.2 2.1 %collective-permute-start.2 = (f32[384,128]{1,0:T(8,128)}, f32[384,128]{1,0:T(8,128)S(1)}, u32[]{:S(2)}, u32[]{:S(2)}) collective-permute-start(f32[384,128]{1,0:T(8,128)} %rim.1), channel_id=1, source_target_pairs={{0,8},{8,16},{16,24},{24,32},{32,40},{40,48},{48,56},{56,64},{64,7... | collective-permute-start | bytes 589832 | tf_op jit(solution)/shard_map/ppermute | solution.py:576
  73.2 0.9 collective-permute-start.4
  74.2 3.4 %collective-permute-start.3 = (f32[72,128]{1,0:T(8,128)S(1)}, f32[72,128]{1,0:T(8,128)S(1)}, u32[]{:S(2)}, u32[]{:S(2)}) collective-permute-start(f32[72,128]{1,0:T(8,128)S(1)} %get-tuple-element.62.own_column_ref), channel_id=1, source_target_pairs={{1,2},{2,1},{3,4},{4,3},{5,6},{6,5},{7,0},{0,7},{9,10},{10,9},{11,... | collective-permute-start | bytes 110600 | tf_op jit(solution)/shard_map/ppermute | solution.py:634
  77.6 4.8 %collective-permute-done.2.north_rim_ref.rest_7_ = f32[384,128]{1,0:T(8,128)S(1)} collective-permute-done((f32[384,128]{1,0:T(8,128)}, f32[384,128]{1,0:T(8,128)S(1)}, u32[]{:S(2)}, u32[]{:S(2)}) %collective-permute-start.2) | collective-permute-done | bytes 196640 | tf_op jit(solution)/shard_map/ppermute | solution.py:576
  82.4 1.3 %collective-permute-start.5 = (f32[32,128]{1,0:T(8,128)S(1)}, f32[32,128]{1,0:T(8,128)S(1)}, u32[]{:S(2)}, u32[]{:S(2)}) collective-permute-start(f32[32,128]{1,0:T(8,128)S(1)} %get-tuple-element.65), channel_id=1, source_target_pairs={{0,128},{1,129},{2,130},{3,131},{4,132},{5,133},{6,134},{7,135},{8... | collective-permute-start | bytes 49160 | tf_op jit(solution)/shard_map/ppermute | solution.py:636
  83.7 1.1 forcing.2.f_ref
  84.9 2.8 %start.1 = (f32[4096,128]{1,0:T(8,128)S(1)}, f32[64,128]{1,0:T(8,128)S(1)}) custom-call(f32[4,4]{1,0:T(4,128)S(1)} %bitcast.20, s32[2]{0:T(128)S(1)} %pad_add_fusion.odd_ref, f32[4096,128]{1,0:T(8,128)S(1)} %get-tuple-element.53.m_ref.rest_1_, f32[1024,128]{1,0:T(8,128)S(1)} %copy-done.15, f32[1024,128]{1,0:T(8,128)S(1)} %copy-done.17, ...), custom_call_target="tpu_custom_call" | custom-call | flops 33554432 | bytes 8388608 | tf_op jit(solution)/shard_map/start/pallas_call | solution.py:652
  87.7 2.6 %edge.2 = (f32[512,128]{1,0:T(8,128)S(1)}, f32[512,128]{1,0:T(8,128)S(1)}, f32[72,128]{1,0:T(8,128)S(1)}, f32[32,128]{1,0:T(8,128)S(1)}, f32[64,128]{1,0:T(8,128)S(1)}, /*index=5*/f32[32,128]{1,0:T(8,128)S(1)}) custom-call(f32[4,4]{1,0:T(4,128)S(1)} %copy-done.20, s32[2]{0:T(128)S(1)} %pad_add_fusion.odd_ref, ...), custom_call_target="tpu_custom_call" | custom-call | tf_op jit(solution)/shard_map/edge/pallas_call | solution.py:690
  90.4 1.3 %collective-permute-start.6 = (f32[512,128]{1,0:T(8,128)S(1)}, f32[512,128]{1,0:T(8,128)S(1)}, u32[]{:S(2)}, u32[]{:S(2)}) collective-permute-start(f32[512,128]{1,0:T(8,128)S(1)} %get-tuple-element.70), channel_id=1, source_target_pairs={{0,8},{8,0},{16,24},{24,16},{32,40},{40,32},{48,56},{56,48},{64,72... | collective-permute-start | bytes 786440 | tf_op jit(solution)/shard_map/ppermute | solution.py:632
  91.7 2.5 %collective-permute-start.7 = (f32[512,128]{1,0:T(8,128)S(1)}, f32[512,128]{1,0:T(8,128)S(1)}, u32[]{:S(2)}, u32[]{:S(2)}) collective-permute-start(f32[512,128]{1,0:T(8,128)S(1)} %get-tuple-element.71), channel_id=1, source_target_pairs={{8,16},{16,8},{24,32},{32,24},{40,48},{48,40},{56,64},{64,56},{72,... | collective-permute-start | bytes 786440 | tf_op jit(solution)/shard_map/ppermute | solution.py:633
  94.4 3.9 %collective-permute-start.8 = (f32[72,128]{1,0:T(8,128)S(1)}, f32[72,128]{1,0:T(8,128)S(1)}, u32[]{:S(2)}, u32[]{:S(2)}) collective-permute-start(f32[72,128]{1,0:T(8,128)S(1)} %get-tuple-element.73.own_column_ref), channel_id=1, source_target_pairs={{1,2},{2,1},{3,4},{4,3},{5,6},{6,5},{7,0},{0,7},{9,10},{10,9},{11,... | collective-permute-start | bytes 110600 | tf_op jit(solution)/shard_map/ppermute | solution.py:634
  98.3 1.3 %collective-permute-start.10 = (f32[32,128]{1,0:T(8,128)S(1)}, f32[32,128]{1,0:T(8,128)S(1)}, u32[]{:S(2)}, u32[]{:S(2)}) collective-permute-start(f32[32,128]{1,0:T(8,128)S(1)} %get-tuple-element.74), channel_id=1, source_target_pairs={{0,128},{1,129},{2,130},{3,131},{4,132},{5,133},{6,134},{7,135},{8... | collective-permute-start | bytes 49160 | tf_op jit(solution)/shard_map/ppermute | solution.py:636
  99.5 1.1 forcing.3.rest_9_
  100.7 3.7 %inner.2 = (f32[4096,128]{1,0:T(8,128)S(1)}, f32[4096,128]{1,0:T(8,128)S(1)}, f32[64,128]{1,0:T(8,128)S(1)}) custom-call(f32[4,4]{1,0:T(4,128)S(1)} %bitcast.21, s32[2]{0:T(128)S(1)} %pad_add_fusion.odd_ref, f32[1024,128]{1,0:T(8,128)S(1)} %copy-done.9, f32[1024,128]{1,0:T(8,128)S(1)} %copy-done.11, ...), custom_call_target="tpu_custom_call" | custom-call | flops 33554432 | bytes 8388608 | tf_op jit(solution)/shard_map/inner/pallas_call | solution.py:662
  104.4 1.6 %collective-permute-done.8.from_column1_ref = f32[72,128]{1,0:T(8,128)S(1)} collective-permute-done((f32[72,128]{1,0:T(8,128)S(1)}, f32[72,128]{1,0:T(8,128)S(1)}, u32[]{:S(2)}, u32[]{:S(2)}) %collective-permute-start.8) | collective-permute-done | bytes 36896 | tf_op jit(solution)/shard_map/ppermute | solution.py:634
  106.1 2.6 %edge.3 = (f32[512,128]{1,0:T(8,128)S(1)}, f32[512,128]{1,0:T(8,128)S(1)}, f32[72,128]{1,0:T(8,128)S(1)}, f32[32,128]{1,0:T(8,128)S(1)}, f32[64,128]{1,0:T(8,128)S(1)}, /*index=5*/f32[32,128]{1,0:T(8,128)S(1)}) custom-call(f32[4,4]{1,0:T(4,128)S(1)} %copy-done.20, s32[2]{0:T(128)S(1)} %pad_add_fusion.odd_ref, ...), custom_call_target="tpu_custom_call" | custom-call | tf_op jit(solution)/shard_map/edge/pallas_call | solution.py:690
  108.8 2.3 %collective-permute-start.11 = (f32[512,128]{1,0:T(8,128)S(1)}, f32[512,128]{1,0:T(8,128)S(1)}, u32[]{:S(2)}, u32[]{:S(2)}) collective-permute-start(f32[512,128]{1,0:T(8,128)S(1)} %get-tuple-element.80), channel_id=1, source_target_pairs={{0,8},{8,0},{16,24},{24,16},{32,40},{40,32},{48,56},{56,48},{64,72... | collective-permute-start | bytes 786440 | tf_op jit(solution)/shard_map/ppermute | solution.py:632
  111.1 2.5 %collective-permute-start.12 = (f32[512,128]{1,0:T(8,128)S(1)}, f32[512,128]{1,0:T(8,128)S(1)}, u32[]{:S(2)}, u32[]{:S(2)}) collective-permute-start(f32[512,128]{1,0:T(8,128)S(1)} %get-tuple-element.81), channel_id=1, source_target_pairs={{8,16},{16,8},{24,32},{32,24},{40,48},{48,40},{56,64},{64,56},{72,... | collective-permute-start | bytes 786440 | tf_op jit(solution)/shard_map/ppermute | solution.py:633
  113.6 4.2 %collective-permute-start.13 = (f32[72,128]{1,0:T(8,128)S(1)}, f32[72,128]{1,0:T(8,128)S(1)}, u32[]{:S(2)}, u32[]{:S(2)}) collective-permute-start(f32[72,128]{1,0:T(8,128)S(1)} %get-tuple-element.79.own_column_ref), channel_id=1, source_target_pairs={{1,2},{2,1},{3,4},{4,3},{5,6},{6,5},{7,0},{0,7},{9,10},{10,9},{11,... | collective-permute-start | bytes 110600 | tf_op jit(solution)/shard_map/ppermute | solution.py:634
  117.9 1.3 %collective-permute-start.15 = (f32[32,128]{1,0:T(8,128)S(1)}, f32[32,128]{1,0:T(8,128)S(1)}, u32[]{:S(2)}, u32[]{:S(2)}) collective-permute-start(f32[32,128]{1,0:T(8,128)S(1)} %get-tuple-element.82), channel_id=1, source_target_pairs={{0,128},{1,129},{2,130},{3,131},{4,132},{5,133},{6,134},{7,135},{8... | collective-permute-start | bytes 49160 | tf_op jit(solution)/shard_map/ppermute | solution.py:636
  119.2 2.9 %inner.3 = (f32[4096,128]{1,0:T(8,128)S(1)}, f32[4096,128]{1,0:T(8,128)S(1)}) custom-call(f32[4,4]{1,0:T(4,128)S(1)} %bitcast.22, s32[2]{0:T(128)S(1)} %pad_add_fusion.odd_ref, f32[1024,128]{1,0:T(8,128)S(1)} %copy-done.3, f32[1024,128]{1,0:T(8,128)S(1)} %copy-done.5, f32[1024,128]{1,0:T(8,128)S(1)} %get-tuple-element.46.c_ref.up_n_ref, ...), custom_call_target="tpu_custom_call" | custom-call | flops 33554432 | bytes 8388608 | tf_op jit(solution)/shard_map/inner/pallas_call | solution.py:662
  122.2 2.5 %collective-permute-done.13.from_column1_ref = f32[72,128]{1,0:T(8,128)S(1)} collective-permute-done((f32[72,128]{1,0:T(8,128)S(1)}, f32[72,128]{1,0:T(8,128)S(1)}, u32[]{:S(2)}, u32[]{:S(2)}) %collective-permute-start.13) | collective-permute-done | bytes 36896 | tf_op jit(solution)/shard_map/ppermute | solution.py:634
  124.6 2.4 %last.1 = f32[4096,128]{1,0:T(8,128)} custom-call(f32[4,4]{1,0:T(4,128)S(1)} %copy-done.20, s32[2]{0:T(128)S(1)} %pad_add_fusion.odd_ref, f32[4096,128]{1,0:T(8,128)S(1)} %get-tuple-element.77.p_ref, f32[4096,128]{1,0:T(8,128)S(1)} %get-tuple-element.78.m_ref, f32[1024,128]{1,0:T(8,128)S(1)} %get-tuple-element.46.c_ref.up_n_ref, ...), custom_call_target="tpu_custom_call" | custom-call | tf_op jit(solution)/shard_map/last/pallas_call | solution.py:699
  (64 shorter events, 7.6 us)
Async XLA Ops:
  3.2 15.5 %copy-start.22 = (s32[8,128]{1,0:T(8,128)S(1)}, s32[8,128]{1,0:T(8,128)}, u32[]{:S(2)}) copy-start(s32[8,128]{1,0:T(8,128)} %param.15) | copy-start | bytes 12292
  3.2 58.1 %all-to-all-start = ((f32[128,1,3200]{2,1,0:T(1,128)}), f32[128,1,3200]{2,1,0:T(1,128)S(1)}, u32[]{:S(2)}, u32[]{:S(2)}) async-start(f32[128,1,3200]{2,1,0:T(1,128)} %bitcast.23), calls=%async_computation | async-start | bytes 3276800 | tf_op jit(solution)/shard_map/all_to_all | solution.py:597
  18.7 1.9 %copy-start = (f32[1,3,2,128,8,128]{5,4,3,2,1,0:T(8,128)S(1)}, f32[1,3,2,128,8,128]{5,4,3,2,1,0:T(8,128)}, u32[]{:S(2)}) copy-start(f32[1,3,2,128,8,128]{5,4,3,2,1,0:T(8,128)} %param.11) | copy-start | bytes 9437188
  20.6 1.9 %copy-start.1 = (f32[1,3,2,128,8,128]{5,4,3,2,1,0:T(8,128)S(1)}, f32[1,3,2,128,8,128]{5,4,3,2,1,0:T(8,128)}, u32[]{:S(2)}) copy-start(f32[1,3,2,128,8,128]{5,4,3,2,1,0:T(8,128)} %param.12) | copy-start | bytes 9437188
  25.5 0.8 copy-start.4
  64.0 23.7 %collective-permute-start = (f32[512,128]{1,0:T(8,128)}, f32[512,128]{1,0:T(8,128)S(1)}, u32[]{:S(2)}, u32[]{:S(2)}) collective-permute-start(f32[512,128]{1,0:T(8,128)} %get-tuple-element.59), channel_id=1, source_target_pairs={{0,8},{8,0},{16,24},{24,16},{32,40},{40,32},{48,56},{56,48},{64,72... | collective-permute-start | bytes 786440 | tf_op jit(solution)/shard_map/ppermute | solution.py:632
  64.0 23.8 %collective-permute-start.1 = (f32[512,128]{1,0:T(8,128)}, f32[512,128]{1,0:T(8,128)S(1)}, u32[]{:S(2)}, u32[]{:S(2)}) collective-permute-start(f32[512,128]{1,0:T(8,128)} %get-tuple-element.60), channel_id=1, source_target_pairs={{8,16},{16,8},{24,32},{32,24},{40,48},{48,40},{56,64},{64,56},{72,... | collective-permute-start | bytes 786440 | tf_op jit(solution)/shard_map/ppermute | solution.py:633
  71.1 13.7 %copy-start.15 = (f32[1024,128]{1,0:T(8,128)S(1)}, f32[1024,128]{1,0:T(8,128)}, u32[]{:S(2)}) copy-start(f32[1024,128]{1,0:T(8,128)} %copy-done.14) | copy-start | bytes 1572868
  71.1 13.7 %copy-start.17 = (f32[1024,128]{1,0:T(8,128)S(1)}, f32[1024,128]{1,0:T(8,128)}, u32[]{:S(2)}) copy-start(f32[1024,128]{1,0:T(8,128)} %copy-done.16) | copy-start | bytes 1572868
  71.1 13.7 %copy-start.19 = (f32[1024,128]{1,0:T(8,128)S(1)}, f32[1024,128]{1,0:T(8,128)}, u32[]{:S(2)}) copy-start(f32[1024,128]{1,0:T(8,128)} %copy-done.18) | copy-start | bytes 1572868
  71.2 13.7 %copy-start.21 = (f32[1,4,4]{2,1,0:T(4,128)S(1)}, f32[1,4,4]{2,1,0:T(4,128)}, u32[]{:S(2)}) copy-start(f32[1,4,4]{2,1,0:T(4,128)} %param.13) | copy-start | bytes 196
  71.2 11.2 %collective-permute-start.2 = (f32[384,128]{1,0:T(8,128)}, f32[384,128]{1,0:T(8,128)S(1)}, u32[]{:S(2)}, u32[]{:S(2)}) collective-permute-start(f32[384,128]{1,0:T(8,128)} %rim.1), channel_id=1, source_target_pairs={{0,8},{8,16},{16,24},{24,32},{32,40},{40,48},{48,56},{56,64},{64,7... | collective-permute-start | bytes 589832 | tf_op jit(solution)/shard_map/ppermute | solution.py:576
  73.2 14.5 %collective-permute-start.4 = (f32[72,128]{1,0:T(8,128)S(1)}, f32[72,128]{1,0:T(8,128)S(1)}, u32[]{:S(2)}, u32[]{:S(2)}) collective-permute-start(f32[72,128]{1,0:T(8,128)S(1)} %get-tuple-element.62.own_column_ref), channel_id=1, source_target_pairs={{0,1},{1,0},{2,3},{3,2},{4,5},{5,4},{6,7},{7,6},{8,9},{9,8},{10,11... | collective-permute-start | bytes 110600 | tf_op jit(solution)/shard_map/ppermute | solution.py:635
  74.2 13.5 %collective-permute-start.3 = (f32[72,128]{1,0:T(8,128)S(1)}, f32[72,128]{1,0:T(8,128)S(1)}, u32[]{:S(2)}, u32[]{:S(2)}) collective-permute-start(f32[72,128]{1,0:T(8,128)S(1)} %get-tuple-element.62.own_column_ref), channel_id=1, source_target_pairs={{1,2},{2,1},{3,4},{4,3},{5,6},{6,5},{7,0},{0,7},{9,10},{10,9},{11,... | collective-permute-start | bytes 110600 | tf_op jit(solution)/shard_map/ppermute | solution.py:634
  82.4 5.3 %collective-permute-start.5 = (f32[32,128]{1,0:T(8,128)S(1)}, f32[32,128]{1,0:T(8,128)S(1)}, u32[]{:S(2)}, u32[]{:S(2)}) collective-permute-start(f32[32,128]{1,0:T(8,128)S(1)} %get-tuple-element.65), channel_id=1, source_target_pairs={{0,128},{1,129},{2,130},{3,131},{4,132},{5,133},{6,134},{7,135},{8... | collective-permute-start | bytes 49160 | tf_op jit(solution)/shard_map/ppermute | solution.py:636
  84.8 2.9 %copy-start.20 = (f32[4,4]{1,0:T(4,128)S(1)}, f32[4,4]{1,0:T(4,128)}, u32[]{:S(2)}) copy-start(f32[4,4]{1,0:T(4,128)} %air_ref.5) | copy-start | bytes 196
  90.4 10.3 %copy-start.9 = (f32[1024,128]{1,0:T(8,128)S(1)}, f32[1024,128]{1,0:T(8,128)}, u32[]{:S(2)}) copy-start(f32[1024,128]{1,0:T(8,128)} %copy-done.8) | copy-start | bytes 1572868
  90.4 10.3 %copy-start.11 = (f32[1024,128]{1,0:T(8,128)S(1)}, f32[1024,128]{1,0:T(8,128)}, u32[]{:S(2)}) copy-start(f32[1024,128]{1,0:T(8,128)} %copy-done.10) | copy-start | bytes 1572868
  90.4 10.3 %copy-start.13 = (f32[1024,128]{1,0:T(8,128)S(1)}, f32[1024,128]{1,0:T(8,128)}, u32[]{:S(2)}) copy-start(f32[1024,128]{1,0:T(8,128)} %copy-done.12) | copy-start | bytes 1572868
  90.4 15.7 %collective-permute-start.6 = (f32[512,128]{1,0:T(8,128)S(1)}, f32[512,128]{1,0:T(8,128)S(1)}, u32[]{:S(2)}, u32[]{:S(2)}) collective-permute-start(f32[512,128]{1,0:T(8,128)S(1)} %get-tuple-element.70), channel_id=1, source_target_pairs={{0,8},{8,0},{16,24},{24,16},{32,40},{40,32},{48,56},{56,48},{64,72... | collective-permute-start | bytes 786440 | tf_op jit(solution)/shard_map/ppermute | solution.py:632
  91.7 14.4 %collective-permute-start.7 = (f32[512,128]{1,0:T(8,128)S(1)}, f32[512,128]{1,0:T(8,128)S(1)}, u32[]{:S(2)}, u32[]{:S(2)}) collective-permute-start(f32[512,128]{1,0:T(8,128)S(1)} %get-tuple-element.71), channel_id=1, source_target_pairs={{8,16},{16,8},{24,32},{32,24},{40,48},{48,40},{56,64},{64,56},{72,... | collective-permute-start | bytes 786440 | tf_op jit(solution)/shard_map/ppermute | solution.py:633
  94.3 10.2 %collective-permute-start.9 = (f32[72,128]{1,0:T(8,128)S(1)}, f32[72,128]{1,0:T(8,128)S(1)}, u32[]{:S(2)}, u32[]{:S(2)}) collective-permute-start(f32[72,128]{1,0:T(8,128)S(1)} %get-tuple-element.73.own_column_ref), channel_id=1, source_target_pairs={{0,1},{1,0},{2,3},{3,2},{4,5},{5,4},{6,7},{7,6},{8,9},{9,8},{10,11... | collective-permute-start | bytes 110600 | tf_op jit(solution)/shard_map/ppermute | solution.py:635
  94.4 11.7 %collective-permute-start.8 = (f32[72,128]{1,0:T(8,128)S(1)}, f32[72,128]{1,0:T(8,128)S(1)}, u32[]{:S(2)}, u32[]{:S(2)}) collective-permute-start(f32[72,128]{1,0:T(8,128)S(1)} %get-tuple-element.73.own_column_ref), channel_id=1, source_target_pairs={{1,2},{2,1},{3,4},{4,3},{5,6},{6,5},{7,0},{0,7},{9,10},{10,9},{11,... | collective-permute-start | bytes 110600 | tf_op jit(solution)/shard_map/ppermute | solution.py:634
  98.3 6.2 %collective-permute-start.10 = (f32[32,128]{1,0:T(8,128)S(1)}, f32[32,128]{1,0:T(8,128)S(1)}, u32[]{:S(2)}, u32[]{:S(2)}) collective-permute-start(f32[32,128]{1,0:T(8,128)S(1)} %get-tuple-element.74), channel_id=1, source_target_pairs={{0,128},{1,129},{2,130},{3,131},{4,132},{5,133},{6,134},{7,135},{8... | collective-permute-start | bytes 49160 | tf_op jit(solution)/shard_map/ppermute | solution.py:636
  106.1 13.1 %copy-start.3 = (f32[1024,128]{1,0:T(8,128)S(1)}, f32[1024,128]{1,0:T(8,128)}, u32[]{:S(2)}) copy-start(f32[1024,128]{1,0:T(8,128)} %copy-done.2) | copy-start | bytes 1572868
  106.1 13.1 %copy-start.5 = (f32[1024,128]{1,0:T(8,128)S(1)}, f32[1024,128]{1,0:T(8,128)}, u32[]{:S(2)}) copy-start(f32[1024,128]{1,0:T(8,128)} %copy-done.4) | copy-start | bytes 1572868
  106.1 13.1 %copy-start.7 = (f32[1024,128]{1,0:T(8,128)S(1)}, f32[1024,128]{1,0:T(8,128)}, u32[]{:S(2)}) copy-start(f32[1024,128]{1,0:T(8,128)} %copy-done.6) | copy-start | bytes 1572868
  108.8 15.9 %collective-permute-start.11 = (f32[512,128]{1,0:T(8,128)S(1)}, f32[512,128]{1,0:T(8,128)S(1)}, u32[]{:S(2)}, u32[]{:S(2)}) collective-permute-start(f32[512,128]{1,0:T(8,128)S(1)} %get-tuple-element.80), channel_id=1, source_target_pairs={{0,8},{8,0},{16,24},{24,16},{32,40},{40,32},{48,56},{56,48},{64,72... | collective-permute-start | bytes 786440 | tf_op jit(solution)/shard_map/ppermute | solution.py:632
  111.1 13.6 %collective-permute-start.12 = (f32[512,128]{1,0:T(8,128)S(1)}, f32[512,128]{1,0:T(8,128)S(1)}, u32[]{:S(2)}, u32[]{:S(2)}) collective-permute-start(f32[512,128]{1,0:T(8,128)S(1)} %get-tuple-element.81), channel_id=1, source_target_pairs={{8,16},{16,8},{24,32},{32,24},{40,48},{48,40},{56,64},{64,56},{72,... | collective-permute-start | bytes 786440 | tf_op jit(solution)/shard_map/ppermute | solution.py:633
  113.5 8.6 %collective-permute-start.14 = (f32[72,128]{1,0:T(8,128)S(1)}, f32[72,128]{1,0:T(8,128)S(1)}, u32[]{:S(2)}, u32[]{:S(2)}) collective-permute-start(f32[72,128]{1,0:T(8,128)S(1)} %get-tuple-element.79.own_column_ref), channel_id=1, source_target_pairs={{0,1},{1,0},{2,3},{3,2},{4,5},{5,4},{6,7},{7,6},{8,9},{9,8},{10,11... | collective-permute-start | bytes 110600 | tf_op jit(solution)/shard_map/ppermute | solution.py:635
  113.6 11.0 %collective-permute-start.13 = (f32[72,128]{1,0:T(8,128)S(1)}, f32[72,128]{1,0:T(8,128)S(1)}, u32[]{:S(2)}, u32[]{:S(2)}) collective-permute-start(f32[72,128]{1,0:T(8,128)S(1)} %get-tuple-element.79.own_column_ref), channel_id=1, source_target_pairs={{1,2},{2,1},{3,4},{4,3},{5,6},{6,5},{7,0},{0,7},{9,10},{10,9},{11,... | collective-permute-start | bytes 110600 | tf_op jit(solution)/shard_map/ppermute | solution.py:634
  117.9 4.3 %collective-permute-start.15 = (f32[32,128]{1,0:T(8,128)S(1)}, f32[32,128]{1,0:T(8,128)S(1)}, u32[]{:S(2)}, u32[]{:S(2)}) collective-permute-start(f32[32,128]{1,0:T(8,128)S(1)} %get-tuple-element.82), channel_id=1, source_target_pairs={{0,128},{1,129},{2,130},{3,131},{4,132},{5,133},{6,134},{7,135},{8... | collective-permute-start | bytes 49160 | tf_op jit(solution)/shard_map/ppermute | solution.py:636
  (8 other events, 6.4 us)

commit v6 on v5

--- a/solution.py
+++ b/solution.py
@@ -10,7 +10,7 @@
 LANES = 128
 SUBS = 8
 BATCH = 4
-VMEM_LIMIT = 20 * 1024 * 1024
+VMEM_LIMIT = 12 * 1024 * 1024
 VMEM_WHOLE = 58 * 1024 * 1024
 
 
@@ -163,7 +163,7 @@
 
 
 def first_kernel(
-    step, slots, fields, levels, odd_ref, got_ref, mask_ref, rim_ref, m_ref, slab1_ref, slab2_ref, column_ref, low_ref
+    step, slots, fields, levels, odd_ref, got_ref, mask_ref, rim_ref, _, m_ref, slab1_ref, slab2_ref, column_ref, low_ref
 ):
     width = fields * levels
     out = spread_rows(step, slots, got_ref, width)
@@ -396,6 +396,7 @@
     low_ref,
     half_ref,
     couple_ref,
+    next_ref,
 ):
     lane = lax.broadcasted_iota(jnp.int32, (SUBS, LANES), 1)
     edge = (lane == 0) | (lane == LANES - 1)
@@ -444,22 +445,16 @@
 
     for f in range(fields):
         for group in range(groups):
-            ends = [plane(f, group, 0), plane(f, group, SUBS - 1)]
-            rows = rows_of(f * levels, group)
-            slab1_ref[rows, :] = jnp.where(lat_even, ends[1], ends[0])
-            slab2_ref[rows, :] = jnp.where(lat_even, ends[0], ends[1])
-            whole = {0: ends[0], SUBS - 1: ends[1]}
-            if group == 0 or group == groups - 1:
-                for y in range(1, SUBS - 1):
-                    whole[y] = plane(f, group, y)
-            if group == groups - 1:
-                for y in range(SUBS):
-                    low_ref[f * SUBS + y : f * SUBS + y + 1, :] = whole[y][SUBS - 1 :, :]
-            ys = range(SUBS) if group == 0 else (0, SUBS - 1)
-            part = column_halves(
-                lambda _, group, y, whole=whole: whole[y], 1, (group,), ys, following[2 * f : 2 * f + 2]
-            )
-            following[2 * f : 2 * f + 2] = part
+            for y in range(SUBS) if group in (0, groups - 1) else (0, SUBS - 1):
+                next_ref[rows_of((y * fields + f) * levels, group), :] = plane(f, group, y)
+    slabs_store(lat_even, next_ref, slab1_ref, slab2_ref, fields * levels)
+    low_store(next_ref, low_ref, fields, levels)
+
+    def load(f, group, y):
+        return next_ref[rows_of((y * fields + f) * levels, group), :]
+
+    following = column_halves(load, fields, range(groups), (0, SUBS - 1), following)
+    following = column_halves(load, fields, (0,), range(1, SUBS - 1), following)
     columns_store(following, rim_ref[(step - 1) * SUBS : step * SUBS, :], column_ref, fields)
 
 
@@ -621,10 +616,10 @@
     m, *edges = pl.pallas_call(
         functools.partial(first_kernel, steps - 1, slots, fields, levels),
         out_shape=[whole, *message],
-        in_specs=[smem] + [vmem] * 3,
+        in_specs=[smem] + [vmem] * 3 + [anywhere],
         compiler_params=params(),
         name="first",
-    )(odd, got, mask, east_rims)
+    )(odd, got, mask, east_rims, north_rims)
     before = None
     for step in reversed(range(steps)):
         slab1, slab2, columns, low = edges
@@ -691,6 +686,7 @@
             functools.partial(edge_kernel, step, fields, levels),
             out_shape=[*message, half, low_shape],
             in_specs=[smem] * 2 + [vmem] * (len(operands) - 2),
+            scratch_shapes=[pltpu.VMEM((width * SUBS, LANES), jnp.float32)],
             compiler_params=params(),
             name="edge",
         )(*operands)

time: 129 us -> 120 us (0.930)
  waiting for transfers between devices: 38.2 us -> 33.1 us
  Pallas kernels: 29.2 us -> 25.4 us
    all_to_all x1, waiting for transfers between devices: 29.2 us -> 1.23 us  [shards(): lax.all_to_all(sent.reshape(owners, 1, stride * LANES), ('lat', 'lon'), s...]
    ppermute x1, waiting for transfers between devices: 4.82 us -> 23.4 us  [shards(): lax.ppermute(north_rims, 'lat', [(i, i + 1) for i in range(lat_count - 1)])]
    ppermute x3, waiting for transfers between devices: 4.09 us -> 8.43 us  [shards(): lax.ppermute(columns, 'lon', swaps('lon', 1, True))]
    pallas_call x2, Pallas kernels: 5.27 us -> 2.25 us  [shards(): pl.pallas_call(functools.partial(edge_kernel, step, fields, levels), out_...]
    ppermute x3, starting transfers between devices: 10.4 us -> 8.54 us  [shards(): lax.ppermute(slab2, 'lat', swaps('lat', 1, False))]
    ppermute x1, starting transfers between devices: 2.05 us -> 3.43 us  [shards(): lax.ppermute(north_rims, 'lat', [(i, i + 1) for i in range(lat_count - 1)])]
  transfers between devices with their start and end apart: 17 -> 17, of which waited for: 4 -> 5; matrix products, arithmetic and copies ran while one was open for 0% -> 0% of each run, Pallas kernels for 12% -> 13%
where the time goes in v6:
time: 120 us; the launch traced here: 118 us
  starting transfers between devices  48.1 us (40%)
  waiting for transfers between devices  33.1 us (28%)
  Pallas kernels  25.4 us (21%)
  local copies, waits for them, and re-layouts  11.1 us (9%)
    ppermute x1, waiting for transfers between devices, shards(): lax.ppermute(north_rims, 'lat', [(i, i + 1) for i in range(lat_count - 1)])  23.4 us
    all_to_all x1, starting transfers between devices, shards(): lax.all_to_all(sent.reshape(owners, 1, stride * LANES), ('lat', 'lon'), s...  15.5 us
    ppermute x3, starting transfers between devices, shards(): lax.ppermute(columns, 'lon', swaps('lon', 1, True))  12.2 us
    unnamed x46, local copies, waits for them, and re-layouts  11.1 us
    ppermute x3, starting transfers between devices, shards(): lax.ppermute(slab2, 'lat', swaps('lat', 1, False))  8.54 us
    ppermute x3, waiting for transfers between devices, shards(): lax.ppermute(columns, 'lon', swaps('lon', 1, True))  8.43 us
    pallas_call x2, Pallas kernels, shards(): pl.pallas_call(functools.partial(inner_kernel, last, step, fields, levels...  6.61 us
    ppermute x3, starting transfers between devices, shards(): lax.ppermute(low, 'comp', [(0, 1)])  3.84 us
  transfers between devices with their start and end apart: 17, of which 5 were waited for; matrix products, arithmetic and copies ran while one was open for 0% of the time, Pallas kernels for 13%

profile of v6, /device:TPU:8, one launch (start us, length us, event | category | flops | bytes accessed | tf_op | source)
XLA Modules:
  0.0 118.4 jit_solution(2500313241673086001)
XLA Ops:
  0.0 3.2 %pack.1 = f32[3200,128]{1,0:T(8,128)} custom-call(f32[3,128,512]{2,1,0:T(8,128)} %bitcast.24, s32[3,1,128]{2,1,0:T(1,128)} %bitcast.25, s32[3,1,128]{2,1,0:T(1,128)} %bitcast.26), custom_call_target="tpu_custom_call" | custom-call | tf_op jit(solution)/shard_map/pack/pallas_call | solution.py:575
  3.2 15.5 %all-to-all-start = ((f32[128,1,3200]{2,1,0:T(1,128)}), f32[128,1,3200]{2,1,0:T(1,128)S(1)}, u32[]{:S(2)}, u32[]{:S(2)}) async-start(f32[128,1,3200]{2,1,0:T(1,128)} %bitcast.23), calls=%async_computation | async-start | bytes 3276800 | tf_op jit(solution)/shard_map/all_to_all | solution.py:592
  18.7 1.8 %rim.1 = f32[384,128]{1,0:T(8,128)} custom-call(f32[3,2,128,8,128]{4,3,2,1,0:T(8,128)} %bitcast.16, f32[3,2,128,8,128]{4,3,2,1,0:T(8,128)} %bitcast.18), custom_call_target="tpu_custom_call" | custom-call | tf_op jit(solution)/shard_map/rim/pallas_call | solution.py:563
  20.4 3.4 %collective-permute-start = (f32[384,128]{1,0:T(8,128)}, f32[384,128]{1,0:T(8,128)S(1)}, u32[]{:S(2)}, u32[]{:S(2)}) collective-permute-start(f32[384,128]{1,0:T(8,128)} %rim.1), channel_id=1, source_target_pairs={{0,8},{8,16},{16,24},{24,32},{32,40},{40,48},{48,56},{56,64},{64,7... | collective-permute-start | bytes 589832 | tf_op jit(solution)/shard_map/ppermute | solution.py:571
  23.9 1.9 %copy-done = f32[1,3,2,128,8,128]{5,4,3,2,1,0:T(8,128)S(1)} copy-done((f32[1,3,2,128,8,128]{5,4,3,2,1,0:T(8,128)S(1)}, f32[1,3,2,128,8,128]{5,4,3,2,1,0:T(8,128)}, u32[]{:S(2)}) %copy-start) | copy-done | bytes 3145752
  25.8 1.9 %copy-done.1 = f32[1,3,2,128,8,128]{5,4,3,2,1,0:T(8,128)S(1)} copy-done((f32[1,3,2,128,8,128]{5,4,3,2,1,0:T(8,128)S(1)}, f32[1,3,2,128,8,128]{5,4,3,2,1,0:T(8,128)}, u32[]{:S(2)}) %copy-start.1) | copy-done | bytes 3145752
  27.7 2.2 %coefficients.1 = (f32[1024,128]{1,0:T(8,128)S(1)}, f32[1024,128]{1,0:T(8,128)S(1)}, f32[1024,128]{1,0:T(8,128)S(1)}, f32[1024,128]{1,0:T(8,128)S(1)}, f32[1024,...) custom-call(f32[6144,128]{1,0:T(8,128)S(1)} %bitcast.17, ...), custom_call_target="tpu_custom_call" | custom-call | flops 4194304 | bytes 8388608 | tf_op jit(solution)/shard_map/coefficients/pallas_call | solution.py:597
  37.3 23.4 %collective-permute-done._.north_rim_ref.rest_7_ = f32[384,128]{1,0:T(8,128)S(1)} collective-permute-done((f32[384,128]{1,0:T(8,128)}, f32[384,128]{1,0:T(8,128)S(1)}, u32[]{:S(2)}, u32[]{:S(2)}) %collective-permute-start) | collective-permute-done | bytes 196640 | tf_op jit(solution)/shard_map/ppermute | solution.py:571
  60.7 1.2 %all-to-all-done = f32[128,1,3200]{2,1,0:T(1,128)S(1)} async-done(((f32[128,1,3200]{2,1,0:T(1,128)}), f32[128,1,3200]{2,1,0:T(1,128)S(1)}, u32[]{:S(2)}, u32[]{:S(2)}) %all-to-all-start) | async-done | bytes 1638432 | tf_op jit(solution)/shard_map/all_to_all | solution.py:592
  61.9 1.9 %first.1 = (f32[4096,128]{1,0:T(8,128)S(1)}, f32[512,128]{1,0:T(8,128)S(1)}, f32[512,128]{1,0:T(8,128)S(1)}, f32[72,128]{1,0:T(8,128)S(1)}, f32[32,128]{1,0:T(8,128)S(1)}) custom-call(s32[2]{0:T(128)S(1)} %pad_add_fusion.odd_ref, f32[3200,128]{1,0:T(8,128)S(1)} %bitcast.13, f32[8,128]{1,0:T(8,128)S(1)} %broadcast_select_fusion.mask_ref.rest_8_, ...), custom_call_target="tpu_custom_call" | custom-call | tf_op jit(solution)/shard_map/first/pallas_call | solution.py:616
  64.0 4.7 %collective-permute-start.2 = (f32[512,128]{1,0:T(8,128)S(1)}, f32[512,128]{1,0:T(8,128)S(1)}, u32[]{:S(2)}, u32[]{:S(2)}) collective-permute-start(f32[512,128]{1,0:T(8,128)S(1)} %get-tuple-element.60), channel_id=1, source_target_pairs={{8,16},{16,8},{24,32},{32,24},{40,48},{48,40},{56,64},{64,56},{72,... | collective-permute-start | bytes 786440 | tf_op jit(solution)/shard_map/ppermute | solution.py:628
  69.7 4.0 %collective-permute-start.3 = (f32[72,128]{1,0:T(8,128)S(1)}, f32[72,128]{1,0:T(8,128)S(1)}, u32[]{:S(2)}, u32[]{:S(2)}) collective-permute-start(f32[72,128]{1,0:T(8,128)S(1)} %get-tuple-element.62.own_column_ref), channel_id=1, source_target_pairs={{1,2},{2,1},{3,4},{4,3},{5,6},{6,5},{7,0},{0,7},{9,10},{10,9},{11,... | collective-permute-start | bytes 110600 | tf_op jit(solution)/shard_map/ppermute | solution.py:629
  73.7 1.3 %collective-permute-start.5 = (f32[32,128]{1,0:T(8,128)S(1)}, f32[32,128]{1,0:T(8,128)S(1)}, u32[]{:S(2)}, u32[]{:S(2)}) collective-permute-start(f32[32,128]{1,0:T(8,128)S(1)} %get-tuple-element.65), channel_id=1, source_target_pairs={{0,128},{1,129},{2,130},{3,131},{4,132},{5,133},{6,134},{7,135},{8... | collective-permute-start | bytes 49160 | tf_op jit(solution)/shard_map/ppermute | solution.py:631
  75.0 1.1 forcing.2.f_ref
  76.1 2.9 %start.1 = (f32[4096,128]{1,0:T(8,128)S(1)}, f32[64,128]{1,0:T(8,128)S(1)}) custom-call(f32[4,4]{1,0:T(4,128)S(1)} %bitcast.20, s32[2]{0:T(128)S(1)} %pad_add_fusion.odd_ref, f32[4096,128]{1,0:T(8,128)S(1)} %get-tuple-element.53.m_ref.rest_1_, f32[1024,128]{1,0:T(8,128)S(1)} %copy-done.15, f32[1024,128]{1,0:T(8,128)S(1)} %copy-done.17, ...), custom_call_target="tpu_custom_call" | custom-call | flops 33554432 | bytes 8388608 | tf_op jit(solution)/shard_map/start/pallas_call | solution.py:647
  79.1 2.0 %collective-permute-done.3.from_column1_ref = f32[72,128]{1,0:T(8,128)S(1)} collective-permute-done((f32[72,128]{1,0:T(8,128)S(1)}, f32[72,128]{1,0:T(8,128)S(1)}, u32[]{:S(2)}, u32[]{:S(2)}) %collective-permute-start.3) | collective-permute-done | bytes 36896 | tf_op jit(solution)/shard_map/ppermute | solution.py:629
  81.1 1.1 edge.2
  82.3 1.8 %collective-permute-start.6 = (f32[512,128]{1,0:T(8,128)S(1)}, f32[512,128]{1,0:T(8,128)S(1)}, u32[]{:S(2)}, u32[]{:S(2)}) collective-permute-start(f32[512,128]{1,0:T(8,128)S(1)} %get-tuple-element.70), channel_id=1, source_target_pairs={{0,8},{8,0},{16,24},{24,16},{32,40},{40,32},{48,56},{56,48},{64,72... | collective-permute-start | bytes 786440 | tf_op jit(solution)/shard_map/ppermute | solution.py:627
  84.0 1.9 %collective-permute-start.7 = (f32[512,128]{1,0:T(8,128)S(1)}, f32[512,128]{1,0:T(8,128)S(1)}, u32[]{:S(2)}, u32[]{:S(2)}) collective-permute-start(f32[512,128]{1,0:T(8,128)S(1)} %get-tuple-element.71), channel_id=1, source_target_pairs={{8,16},{16,8},{24,32},{32,24},{40,48},{48,40},{56,64},{64,56},{72,... | collective-permute-start | bytes 786440 | tf_op jit(solution)/shard_map/ppermute | solution.py:628
  86.1 4.3 %collective-permute-start.8 = (f32[72,128]{1,0:T(8,128)S(1)}, f32[72,128]{1,0:T(8,128)S(1)}, u32[]{:S(2)}, u32[]{:S(2)}) collective-permute-start(f32[72,128]{1,0:T(8,128)S(1)} %get-tuple-element.73.own_column_ref), channel_id=1, source_target_pairs={{1,2},{2,1},{3,4},{4,3},{5,6},{6,5},{7,0},{0,7},{9,10},{10,9},{11,... | collective-permute-start | bytes 110600 | tf_op jit(solution)/shard_map/ppermute | solution.py:629
  90.4 1.3 %collective-permute-start.10 = (f32[32,128]{1,0:T(8,128)S(1)}, f32[32,128]{1,0:T(8,128)S(1)}, u32[]{:S(2)}, u32[]{:S(2)}) collective-permute-start(f32[32,128]{1,0:T(8,128)S(1)} %get-tuple-element.74), channel_id=1, source_target_pairs={{0,128},{1,129},{2,130},{3,131},{4,132},{5,133},{6,134},{7,135},{8... | collective-permute-start | bytes 49160 | tf_op jit(solution)/shard_map/ppermute | solution.py:631
  91.6 1.1 forcing.3.rest_9_
  92.8 3.6 %inner.2 = (f32[4096,128]{1,0:T(8,128)S(1)}, f32[4096,128]{1,0:T(8,128)S(1)}, f32[64,128]{1,0:T(8,128)S(1)}) custom-call(f32[4,4]{1,0:T(4,128)S(1)} %bitcast.21, s32[2]{0:T(128)S(1)} %pad_add_fusion.odd_ref, f32[1024,128]{1,0:T(8,128)S(1)} %copy-done.9, f32[1024,128]{1,0:T(8,128)S(1)} %copy-done.11, ...), custom_call_target="tpu_custom_call" | custom-call | flops 33554432 | bytes 8388608 | tf_op jit(solution)/shard_map/inner/pallas_call | solution.py:657
  96.4 3.4 %collective-permute-done.8.from_column1_ref = f32[72,128]{1,0:T(8,128)S(1)} collective-permute-done((f32[72,128]{1,0:T(8,128)S(1)}, f32[72,128]{1,0:T(8,128)S(1)}, u32[]{:S(2)}, u32[]{:S(2)}) %collective-permute-start.8) | collective-permute-done | bytes 36896 | tf_op jit(solution)/shard_map/ppermute | solution.py:629
  99.9 1.1 edge.3
  101.0 1.7 %collective-permute-start.11 = (f32[512,128]{1,0:T(8,128)S(1)}, f32[512,128]{1,0:T(8,128)S(1)}, u32[]{:S(2)}, u32[]{:S(2)}) collective-permute-start(f32[512,128]{1,0:T(8,128)S(1)} %get-tuple-element.80), channel_id=1, source_target_pairs={{0,8},{8,0},{16,24},{24,16},{32,40},{40,32},{48,56},{56,48},{64,72... | collective-permute-start | bytes 786440 | tf_op jit(solution)/shard_map/ppermute | solution.py:627
  102.7 1.9 %collective-permute-start.12 = (f32[512,128]{1,0:T(8,128)S(1)}, f32[512,128]{1,0:T(8,128)S(1)}, u32[]{:S(2)}, u32[]{:S(2)}) collective-permute-start(f32[512,128]{1,0:T(8,128)S(1)} %get-tuple-element.81), channel_id=1, source_target_pairs={{8,16},{16,8},{24,32},{32,24},{40,48},{48,40},{56,64},{64,56},{72,... | collective-permute-start | bytes 786440 | tf_op jit(solution)/shard_map/ppermute | solution.py:628
  104.7 3.9 %collective-permute-start.13 = (f32[72,128]{1,0:T(8,128)S(1)}, f32[72,128]{1,0:T(8,128)S(1)}, u32[]{:S(2)}, u32[]{:S(2)}) collective-permute-start(f32[72,128]{1,0:T(8,128)S(1)} %get-tuple-element.79.own_column_ref), channel_id=1, source_target_pairs={{1,2},{2,1},{3,4},{4,3},{5,6},{6,5},{7,0},{0,7},{9,10},{10,9},{11,... | collective-permute-start | bytes 110600 | tf_op jit(solution)/shard_map/ppermute | solution.py:629
  108.6 1.3 %collective-permute-start.15 = (f32[32,128]{1,0:T(8,128)S(1)}, f32[32,128]{1,0:T(8,128)S(1)}, u32[]{:S(2)}, u32[]{:S(2)}) collective-permute-start(f32[32,128]{1,0:T(8,128)S(1)} %get-tuple-element.82), channel_id=1, source_target_pairs={{0,128},{1,129},{2,130},{3,131},{4,132},{5,133},{6,134},{7,135},{8... | collective-permute-start | bytes 49160 | tf_op jit(solution)/shard_map/ppermute | solution.py:631
  109.9 3.0 %inner.3 = (f32[4096,128]{1,0:T(8,128)S(1)}, f32[4096,128]{1,0:T(8,128)S(1)}) custom-call(f32[4,4]{1,0:T(4,128)S(1)} %bitcast.22, s32[2]{0:T(128)S(1)} %pad_add_fusion.odd_ref, f32[1024,128]{1,0:T(8,128)S(1)} %copy-done.3, f32[1024,128]{1,0:T(8,128)S(1)} %copy-done.5, f32[1024,128]{1,0:T(8,128)S(1)} %get-tuple-element.46.c_ref.up_n_ref, ...), custom_call_target="tpu_custom_call" | custom-call | flops 33554432 | bytes 8388608 | tf_op jit(solution)/shard_map/inner/pallas_call | solution.py:657
  112.9 3.0 %collective-permute-done.13.from_column1_ref = f32[72,128]{1,0:T(8,128)S(1)} collective-permute-done((f32[72,128]{1,0:T(8,128)S(1)}, f32[72,128]{1,0:T(8,128)S(1)}, u32[]{:S(2)}, u32[]{:S(2)}) %collective-permute-start.13) | collective-permute-done | bytes 36896 | tf_op jit(solution)/shard_map/ppermute | solution.py:629
  115.9 2.4 %last.1 = f32[4096,128]{1,0:T(8,128)} custom-call(f32[4,4]{1,0:T(4,128)S(1)} %copy-done.20, s32[2]{0:T(128)S(1)} %pad_add_fusion.odd_ref, f32[4096,128]{1,0:T(8,128)S(1)} %get-tuple-element.77.p_ref, f32[4096,128]{1,0:T(8,128)S(1)} %get-tuple-element.78.m_ref, f32[1024,128]{1,0:T(8,128)S(1)} %get-tuple-element.46.c_ref.up_n_ref, ...), custom_call_target="tpu_custom_call" | custom-call | tf_op jit(solution)/shard_map/last/pallas_call | solution.py:695
  (64 shorter events, 8.6 us)
Async XLA Ops:
  3.2 58.8 %all-to-all-start = ((f32[128,1,3200]{2,1,0:T(1,128)}), f32[128,1,3200]{2,1,0:T(1,128)S(1)}, u32[]{:S(2)}, u32[]{:S(2)}) async-start(f32[128,1,3200]{2,1,0:T(1,128)} %bitcast.23), calls=%async_computation | async-start | bytes 3276800 | tf_op jit(solution)/shard_map/all_to_all | solution.py:592
  18.6 5.2 %copy-start.22 = (s32[8,128]{1,0:T(8,128)S(1)}, s32[8,128]{1,0:T(8,128)}, u32[]{:S(2)}) copy-start(s32[8,128]{1,0:T(8,128)} %param.15) | copy-start | bytes 12292
  20.4 40.3 %collective-permute-start = (f32[384,128]{1,0:T(8,128)}, f32[384,128]{1,0:T(8,128)S(1)}, u32[]{:S(2)}, u32[]{:S(2)}) collective-permute-start(f32[384,128]{1,0:T(8,128)} %rim.1), channel_id=1, source_target_pairs={{0,8},{8,16},{16,24},{24,32},{32,40},{40,48},{48,56},{56,64},{64,7... | collective-permute-start | bytes 589832 | tf_op jit(solution)/shard_map/ppermute | solution.py:571
  23.9 1.9 %copy-start = (f32[1,3,2,128,8,128]{5,4,3,2,1,0:T(8,128)S(1)}, f32[1,3,2,128,8,128]{5,4,3,2,1,0:T(8,128)}, u32[]{:S(2)}) copy-start(f32[1,3,2,128,8,128]{5,4,3,2,1,0:T(8,128)} %param.11) | copy-start | bytes 9437188
  25.8 1.9 %copy-start.1 = (f32[1,3,2,128,8,128]{5,4,3,2,1,0:T(8,128)S(1)}, f32[1,3,2,128,8,128]{5,4,3,2,1,0:T(8,128)}, u32[]{:S(2)}) copy-start(f32[1,3,2,128,8,128]{5,4,3,2,1,0:T(8,128)} %param.12) | copy-start | bytes 9437188
  30.7 0.8 copy-start.4
  63.9 12.2 %copy-start.15 = (f32[1024,128]{1,0:T(8,128)S(1)}, f32[1024,128]{1,0:T(8,128)}, u32[]{:S(2)}) copy-start(f32[1024,128]{1,0:T(8,128)} %copy-done.14) | copy-start | bytes 1572868
  63.9 12.2 %copy-start.17 = (f32[1024,128]{1,0:T(8,128)S(1)}, f32[1024,128]{1,0:T(8,128)}, u32[]{:S(2)}) copy-start(f32[1024,128]{1,0:T(8,128)} %copy-done.16) | copy-start | bytes 1572868
  63.9 12.2 %copy-start.19 = (f32[1024,128]{1,0:T(8,128)S(1)}, f32[1024,128]{1,0:T(8,128)}, u32[]{:S(2)}) copy-start(f32[1024,128]{1,0:T(8,128)} %copy-done.18) | copy-start | bytes 1572868
  63.9 12.2 %copy-start.21 = (f32[1,4,4]{2,1,0:T(4,128)S(1)}, f32[1,4,4]{2,1,0:T(4,128)}, u32[]{:S(2)}) copy-start(f32[1,4,4]{2,1,0:T(4,128)} %param.13) | copy-start | bytes 196
  63.9 17.2 %collective-permute-start.1 = (f32[512,128]{1,0:T(8,128)S(1)}, f32[512,128]{1,0:T(8,128)S(1)}, u32[]{:S(2)}, u32[]{:S(2)}) collective-permute-start(f32[512,128]{1,0:T(8,128)S(1)} %get-tuple-element.59), channel_id=1, source_target_pairs={{0,8},{8,0},{16,24},{24,16},{32,40},{40,32},{48,56},{56,48},{64,72... | collective-permute-start | bytes 786440 | tf_op jit(solution)/shard_map/ppermute | solution.py:627
  64.0 17.1 %collective-permute-start.2 = (f32[512,128]{1,0:T(8,128)S(1)}, f32[512,128]{1,0:T(8,128)S(1)}, u32[]{:S(2)}, u32[]{:S(2)}) collective-permute-start(f32[512,128]{1,0:T(8,128)S(1)} %get-tuple-element.60), channel_id=1, source_target_pairs={{8,16},{16,8},{24,32},{32,24},{40,48},{48,40},{56,64},{64,56},{72,... | collective-permute-start | bytes 786440 | tf_op jit(solution)/shard_map/ppermute | solution.py:628
  68.7 10.3 %collective-permute-start.4 = (f32[72,128]{1,0:T(8,128)S(1)}, f32[72,128]{1,0:T(8,128)S(1)}, u32[]{:S(2)}, u32[]{:S(2)}) collective-permute-start(f32[72,128]{1,0:T(8,128)S(1)} %get-tuple-element.62.own_column_ref), channel_id=1, source_target_pairs={{0,1},{1,0},{2,3},{3,2},{4,5},{5,4},{6,7},{7,6},{8,9},{9,8},{10,11... | collective-permute-start | bytes 110600 | tf_op jit(solution)/shard_map/ppermute | solution.py:630
  69.7 11.4 %collective-permute-start.3 = (f32[72,128]{1,0:T(8,128)S(1)}, f32[72,128]{1,0:T(8,128)S(1)}, u32[]{:S(2)}, u32[]{:S(2)}) collective-permute-start(f32[72,128]{1,0:T(8,128)S(1)} %get-tuple-element.62.own_column_ref), channel_id=1, source_target_pairs={{1,2},{2,1},{3,4},{4,3},{5,6},{6,5},{7,0},{0,7},{9,10},{10,9},{11,... | collective-permute-start | bytes 110600 | tf_op jit(solution)/shard_map/ppermute | solution.py:629
  73.7 5.4 %collective-permute-start.5 = (f32[32,128]{1,0:T(8,128)S(1)}, f32[32,128]{1,0:T(8,128)S(1)}, u32[]{:S(2)}, u32[]{:S(2)}) collective-permute-start(f32[32,128]{1,0:T(8,128)S(1)} %get-tuple-element.65), channel_id=1, source_target_pairs={{0,128},{1,129},{2,130},{3,131},{4,132},{5,133},{6,134},{7,135},{8... | collective-permute-start | bytes 49160 | tf_op jit(solution)/shard_map/ppermute | solution.py:631
  76.1 5.0 %copy-start.20 = (f32[4,4]{1,0:T(4,128)S(1)}, f32[4,4]{1,0:T(4,128)}, u32[]{:S(2)}) copy-start(f32[4,4]{1,0:T(4,128)} %air_ref.5) | copy-start | bytes 196
  82.3 10.5 %copy-start.9 = (f32[1024,128]{1,0:T(8,128)S(1)}, f32[1024,128]{1,0:T(8,128)}, u32[]{:S(2)}) copy-start(f32[1024,128]{1,0:T(8,128)} %copy-done.8) | copy-start | bytes 1572868
  82.3 10.5 %copy-start.11 = (f32[1024,128]{1,0:T(8,128)S(1)}, f32[1024,128]{1,0:T(8,128)}, u32[]{:S(2)}) copy-start(f32[1024,128]{1,0:T(8,128)} %copy-done.10) | copy-start | bytes 1572868
  82.3 10.5 %copy-start.13 = (f32[1024,128]{1,0:T(8,128)S(1)}, f32[1024,128]{1,0:T(8,128)}, u32[]{:S(2)}) copy-start(f32[1024,128]{1,0:T(8,128)} %copy-done.12) | copy-start | bytes 1572868
  82.3 17.5 %collective-permute-start.6 = (f32[512,128]{1,0:T(8,128)S(1)}, f32[512,128]{1,0:T(8,128)S(1)}, u32[]{:S(2)}, u32[]{:S(2)}) collective-permute-start(f32[512,128]{1,0:T(8,128)S(1)} %get-tuple-element.70), channel_id=1, source_target_pairs={{0,8},{8,0},{16,24},{24,16},{32,40},{40,32},{48,56},{56,48},{64,72... | collective-permute-start | bytes 786440 | tf_op jit(solution)/shard_map/ppermute | solution.py:627
  84.0 15.8 %collective-permute-start.7 = (f32[512,128]{1,0:T(8,128)S(1)}, f32[512,128]{1,0:T(8,128)S(1)}, u32[]{:S(2)}, u32[]{:S(2)}) collective-permute-start(f32[512,128]{1,0:T(8,128)S(1)} %get-tuple-element.71), channel_id=1, source_target_pairs={{8,16},{16,8},{24,32},{32,24},{40,48},{48,40},{56,64},{64,56},{72,... | collective-permute-start | bytes 786440 | tf_op jit(solution)/shard_map/ppermute | solution.py:628
  86.0 10.5 %collective-permute-start.9 = (f32[72,128]{1,0:T(8,128)S(1)}, f32[72,128]{1,0:T(8,128)S(1)}, u32[]{:S(2)}, u32[]{:S(2)}) collective-permute-start(f32[72,128]{1,0:T(8,128)S(1)} %get-tuple-element.73.own_column_ref), channel_id=1, source_target_pairs={{0,1},{1,0},{2,3},{3,2},{4,5},{5,4},{6,7},{7,6},{8,9},{9,8},{10,11... | collective-permute-start | bytes 110600 | tf_op jit(solution)/shard_map/ppermute | solution.py:630
  86.1 13.8 %collective-permute-start.8 = (f32[72,128]{1,0:T(8,128)S(1)}, f32[72,128]{1,0:T(8,128)S(1)}, u32[]{:S(2)}, u32[]{:S(2)}) collective-permute-start(f32[72,128]{1,0:T(8,128)S(1)} %get-tuple-element.73.own_column_ref), channel_id=1, source_target_pairs={{1,2},{2,1},{3,4},{4,3},{5,6},{6,5},{7,0},{0,7},{9,10},{10,9},{11,... | collective-permute-start | bytes 110600 | tf_op jit(solution)/shard_map/ppermute | solution.py:629
  90.4 6.1 %collective-permute-start.10 = (f32[32,128]{1,0:T(8,128)S(1)}, f32[32,128]{1,0:T(8,128)S(1)}, u32[]{:S(2)}, u32[]{:S(2)}) collective-permute-start(f32[32,128]{1,0:T(8,128)S(1)} %get-tuple-element.74), channel_id=1, source_target_pairs={{0,128},{1,129},{2,130},{3,131},{4,132},{5,133},{6,134},{7,135},{8... | collective-permute-start | bytes 49160 | tf_op jit(solution)/shard_map/ppermute | solution.py:631
  99.8 10.0 %copy-start.3 = (f32[1024,128]{1,0:T(8,128)S(1)}, f32[1024,128]{1,0:T(8,128)}, u32[]{:S(2)}) copy-start(f32[1024,128]{1,0:T(8,128)} %copy-done.2) | copy-start | bytes 1572868
  99.8 10.0 %copy-start.5 = (f32[1024,128]{1,0:T(8,128)S(1)}, f32[1024,128]{1,0:T(8,128)}, u32[]{:S(2)}) copy-start(f32[1024,128]{1,0:T(8,128)} %copy-done.4) | copy-start | bytes 1572868
  99.9 10.0 %copy-start.7 = (f32[1024,128]{1,0:T(8,128)S(1)}, f32[1024,128]{1,0:T(8,128)}, u32[]{:S(2)}) copy-start(f32[1024,128]{1,0:T(8,128)} %copy-done.6) | copy-start | bytes 1572868
  101.0 14.8 %collective-permute-start.11 = (f32[512,128]{1,0:T(8,128)S(1)}, f32[512,128]{1,0:T(8,128)S(1)}, u32[]{:S(2)}, u32[]{:S(2)}) collective-permute-start(f32[512,128]{1,0:T(8,128)S(1)} %get-tuple-element.80), channel_id=1, source_target_pairs={{0,8},{8,0},{16,24},{24,16},{32,40},{40,32},{48,56},{56,48},{64,72... | collective-permute-start | bytes 786440 | tf_op jit(solution)/shard_map/ppermute | solution.py:627
  102.7 13.2 %collective-permute-start.12 = (f32[512,128]{1,0:T(8,128)S(1)}, f32[512,128]{1,0:T(8,128)S(1)}, u32[]{:S(2)}, u32[]{:S(2)}) collective-permute-start(f32[512,128]{1,0:T(8,128)S(1)} %get-tuple-element.81), channel_id=1, source_target_pairs={{8,16},{16,8},{24,32},{32,24},{40,48},{48,40},{56,64},{64,56},{72,... | collective-permute-start | bytes 786440 | tf_op jit(solution)/shard_map/ppermute | solution.py:628
  104.6 8.3 %collective-permute-start.14 = (f32[72,128]{1,0:T(8,128)S(1)}, f32[72,128]{1,0:T(8,128)S(1)}, u32[]{:S(2)}, u32[]{:S(2)}) collective-permute-start(f32[72,128]{1,0:T(8,128)S(1)} %get-tuple-element.79.own_column_ref), channel_id=1, source_target_pairs={{0,1},{1,0},{2,3},{3,2},{4,5},{5,4},{6,7},{7,6},{8,9},{9,8},{10,11... | collective-permute-start | bytes 110600 | tf_op jit(solution)/shard_map/ppermute | solution.py:630
  104.7 11.1 %collective-permute-start.13 = (f32[72,128]{1,0:T(8,128)S(1)}, f32[72,128]{1,0:T(8,128)S(1)}, u32[]{:S(2)}, u32[]{:S(2)}) collective-permute-start(f32[72,128]{1,0:T(8,128)S(1)} %get-tuple-element.79.own_column_ref), channel_id=1, source_target_pairs={{1,2},{2,1},{3,4},{4,3},{5,6},{6,5},{7,0},{0,7},{9,10},{10,9},{11,... | collective-permute-start | bytes 110600 | tf_op jit(solution)/shard_map/ppermute | solution.py:629
  108.6 4.3 %collective-permute-start.15 = (f32[32,128]{1,0:T(8,128)S(1)}, f32[32,128]{1,0:T(8,128)S(1)}, u32[]{:S(2)}, u32[]{:S(2)}) collective-permute-start(f32[32,128]{1,0:T(8,128)S(1)} %get-tuple-element.82), channel_id=1, source_target_pairs={{0,128},{1,129},{2,130},{3,131},{4,132},{5,133},{6,134},{7,135},{8... | collective-permute-start | bytes 49160 | tf_op jit(solution)/shard_map/ppermute | solution.py:631
  (8 other events, 6.4 us)

commit v7 on v6

--- a/solution.py
+++ b/solution.py
@@ -14,12 +14,9 @@
 VMEM_WHOLE = 58 * 1024 * 1024
 
 
-def split3(x):
-    hi = x.astype(jnp.bfloat16)
-    rest = x - hi.astype(jnp.float32)
-    mid = rest.astype(jnp.bfloat16)
-    low = (rest - mid.astype(jnp.float32)).astype(jnp.bfloat16)
-    return [hi, mid, low]
+def split(x):
+    high = x.astype(jnp.bfloat16)
+    return [high, (x - high.astype(jnp.float32)).astype(jnp.bfloat16)]
 
 
 def pack_kernel(slots, rows_hbm, owner_hbm, cell_hbm, out_ref, rows_ref, owner_ref, cell_ref, sems):
@@ -47,14 +44,14 @@
         hits_f = hits.astype(jnp.float32)
         prior = jnp.dot(hits_f.astype(jnp.bfloat16), before, preferred_element_type=jnp.float32)
         large[step].wait()
-        terms = jnp.concatenate(split3(rows_ref[step]), axis=0)
+        terms = jnp.concatenate(split(rows_ref[step]), axis=0)
         marks = (cell_ref[step] + 1).astype(jnp.float32)
         for k in range(slots):
             slot = step * slots + k
             pick = jnp.where(prior == float(k), hits_f, 0.0)
             pick_b = pick.astype(jnp.bfloat16)
             out = jnp.dot(
-                jnp.concatenate([pick_b] * 3, axis=1), terms, preferred_element_type=jnp.float32
+                jnp.concatenate([pick_b] * 2, axis=1), terms, preferred_element_type=jnp.float32
             )
             for part in range(parts):
                 out_ref[pl.ds(slot * parts + part, owners, stride=stride), :] = out[
@@ -79,10 +76,10 @@
             block = got_ref[pl.ds(slot * parts + part, sources, stride=stride), :]
             cols.append(block.T)
         turned = jnp.concatenate(cols, axis=0)
-        terms += split3(turned)
+        terms += split(turned)
         cell = marks[:, slot : slot + 1].astype(jnp.int32) - 1
         onehot = (cell == where_to).astype(jnp.float32).astype(jnp.bfloat16)
-        onehots += [onehot] * 3
+        onehots += [onehot] * 2
     return jnp.dot(
         jnp.concatenate(terms, axis=1),
         jnp.concatenate(onehots, axis=0),
@@ -163,7 +160,7 @@
 
 
 def first_kernel(
-    step, slots, fields, levels, odd_ref, got_ref, mask_ref, rim_ref, _, m_ref, slab1_ref, slab2_ref, column_ref, low_ref
+    step, slots, fields, levels, odd_ref, got_ref, mask_ref, rim_ref, m_ref, slab1_ref, slab2_ref, column_ref, low_ref
 ):
     width = fields * levels
     out = spread_rows(step, slots, got_ref, width)
@@ -185,6 +182,10 @@
     out = spread_rows(step, slots, got_ref, width)
     for y in range(SUBS):
         f_ref[y * width : (y + 1) * width, :] = out[:, y * LANES : (y + 1) * LANES]
+
+
+def copy_kernel(from_ref, to_ref):
+    to_ref[...] = from_ref[...]
 
 
 def rim_kernel(vel_ref, dif_ref, rim_ref, vel_row, dif_row, sems):
@@ -572,6 +573,13 @@
         north_rims, "lat", [(i, i + 1) for i in range(lat_count - 1)]
     )
 
+    north_rims = pl.pallas_call(
+        copy_kernel,
+        out_shape=f32((steps * levels, LANES)),
+        compiler_params=params(),
+        cost_estimate=pl.CostEstimate(flops=int(2e9), bytes_accessed=1 << 19, transcendentals=0),
+        name="rims",
+    )(north_rims)
     sent = pl.pallas_call(
         functools.partial(pack_kernel, slots),
         out_shape=f32((owners * stride, LANES)),
@@ -616,10 +624,10 @@
     m, *edges = pl.pallas_call(
         functools.partial(first_kernel, steps - 1, slots, fields, levels),
         out_shape=[whole, *message],
-        in_specs=[smem] + [vmem] * 3 + [anywhere],
+        in_specs=[smem] + [vmem] * 3,
         compiler_params=params(),
         name="first",
-    )(odd, got, mask, east_rims, north_rims)
+    )(odd, got, mask, east_rims)
     before = None
     for step in reversed(range(steps)):
         slab1, slab2, columns, low = edges

time: 120 us -> 118 us (0.983)
  waiting for transfers between devices: 33.1 us -> 31.2 us
  Pallas kernels: 25.4 us -> 24.1 us
    all_to_all x1, waiting for transfers between devices: 1.23 us -> 24.7 us  [shards(): lax.all_to_all(sent.reshape(owners, 1, stride * LANES), ('lat', 'lon'), s...]
    ppermute x1, waiting for transfers between devices: 23.4 us -> 0.01 us  [shards(): lax.ppermute(north_rims, 'lat', [(i, i + 1) for i in range(lat_count - 1)])]
    ppermute x3, starting transfers between devices: 8.54 us -> 10.6 us  [shards(): lax.ppermute(slab2, 'lat', swaps('lat', 1, False))]
    ppermute x3, waiting for transfers between devices: 8.43 us -> 6.47 us  [shards(): lax.ppermute(columns, 'lon', swaps('lon', 1, True))]
  transfers between devices with their start and end apart: 17 -> 17, of which waited for: 5 -> 4; matrix products, arithmetic and copies ran while one was open for 0% -> 0% of each run, Pallas kernels for 13% -> 14%
where the time goes in v7:
time: 118 us; the launch traced here: 117 us
  starting transfers between devices  49.2 us (42%)
  waiting for transfers between devices  31.2 us (26%)
  Pallas kernels  24.1 us (20%)
  local copies, waits for them, and re-layouts  11.5 us (10%)
    all_to_all x1, waiting for transfers between devices, shards(): lax.all_to_all(sent.reshape(owners, 1, stride * LANES), ('lat', 'lon'), s...  24.7 us
    all_to_all x1, starting transfers between devices, shards(): lax.all_to_all(sent.reshape(owners, 1, stride * LANES), ('lat', 'lon'), s...  15.5 us
    ppermute x3, starting transfers between devices, shards(): lax.ppermute(columns, 'lon', swaps('lon', 1, True))  12.2 us
    unnamed x46, local copies, waits for them, and re-layouts  11.5 us
    ppermute x3, starting transfers between devices, shards(): lax.ppermute(slab2, 'lat', swaps('lat', 1, False))  10.6 us
    ppermute x3, waiting for transfers between devices, shards(): lax.ppermute(columns, 'lon', swaps('lon', 1, True))  6.47 us
    pallas_call x2, Pallas kernels, shards(): pl.pallas_call(functools.partial(inner_kernel, last, step, fields, levels...  6.43 us
    ppermute x3, starting transfers between devices, shards(): lax.ppermute(low, 'comp', [(0, 1)])  4.02 us
  transfers between devices with their start and end apart: 17, of which 4 were waited for; matrix products, arithmetic and copies ran while one was open for 0% of the time, Pallas kernels for 14%

profile of v7, /device:TPU:8, one launch (start us, length us, event | category | flops | bytes accessed | tf_op | source)
XLA Modules:
  0.0 116.7 jit_solution(8432956516192705054)
XLA Ops:
  0.0 3.0 %pack.1 = f32[3200,128]{1,0:T(8,128)} custom-call(f32[3,128,512]{2,1,0:T(8,128)} %bitcast.24, s32[3,1,128]{2,1,0:T(1,128)} %bitcast.25, s32[3,1,128]{2,1,0:T(1,128)} %bitcast.26), custom_call_target="tpu_custom_call" | custom-call | tf_op jit(solution)/shard_map/pack/pallas_call | solution.py:583
  3.0 15.5 %all-to-all-start = ((f32[128,1,3200]{2,1,0:T(1,128)}), f32[128,1,3200]{2,1,0:T(1,128)S(1)}, u32[]{:S(2)}, u32[]{:S(2)}) async-start(f32[128,1,3200]{2,1,0:T(1,128)} %bitcast.23), calls=%async_computation | async-start | bytes 3276800 | tf_op jit(solution)/shard_map/all_to_all | solution.py:600
  18.4 1.8 %rim.1 = f32[384,128]{1,0:T(8,128)} custom-call(f32[3,2,128,8,128]{4,3,2,1,0:T(8,128)} %bitcast.16, f32[3,2,128,8,128]{4,3,2,1,0:T(8,128)} %bitcast.18), custom_call_target="tpu_custom_call" | custom-call | tf_op jit(solution)/shard_map/rim/pallas_call | solution.py:564
  20.2 3.4 %collective-permute-start.2 = (f32[384,128]{1,0:T(8,128)}, f32[384,128]{1,0:T(8,128)S(1)}, u32[]{:S(2)}, u32[]{:S(2)}) collective-permute-start(f32[384,128]{1,0:T(8,128)} %rim.1), channel_id=1, source_target_pairs={{0,8},{8,16},{16,24},{24,32},{32,40},{40,48},{48,56},{56,64},{64,7... | collective-permute-start | bytes 589832 | tf_op jit(solution)/shard_map/ppermute | solution.py:572
  23.7 1.9 %copy-done = f32[1,3,2,128,8,128]{5,4,3,2,1,0:T(8,128)S(1)} copy-done((f32[1,3,2,128,8,128]{5,4,3,2,1,0:T(8,128)S(1)}, f32[1,3,2,128,8,128]{5,4,3,2,1,0:T(8,128)}, u32[]{:S(2)}) %copy-start) | copy-done | bytes 3145752
  25.6 1.9 %copy-done.1 = f32[1,3,2,128,8,128]{5,4,3,2,1,0:T(8,128)S(1)} copy-done((f32[1,3,2,128,8,128]{5,4,3,2,1,0:T(8,128)S(1)}, f32[1,3,2,128,8,128]{5,4,3,2,1,0:T(8,128)}, u32[]{:S(2)}) %copy-start.1) | copy-done | bytes 3145752
  27.5 2.2 %coefficients.1 = (f32[1024,128]{1,0:T(8,128)S(1)}, f32[1024,128]{1,0:T(8,128)S(1)}, f32[1024,128]{1,0:T(8,128)S(1)}, f32[1024,128]{1,0:T(8,128)S(1)}, f32[1024,...) custom-call(f32[6144,128]{1,0:T(8,128)S(1)} %bitcast.17, ...), custom_call_target="tpu_custom_call" | custom-call | flops 4194304 | bytes 8388608 | tf_op jit(solution)/shard_map/coefficients/pallas_call | solution.py:605
  30.5 0.8 copy-done.4
  33.0 0.8 copy-done.10
  37.0 24.7 %all-to-all-done = f32[128,1,3200]{2,1,0:T(1,128)S(1)} async-done(((f32[128,1,3200]{2,1,0:T(1,128)}), f32[128,1,3200]{2,1,0:T(1,128)S(1)}, u32[]{:S(2)}, u32[]{:S(2)}) %all-to-all-start) | async-done | bytes 1638432 | tf_op jit(solution)/shard_map/all_to_all | solution.py:600
  61.7 1.7 %first.1 = (f32[4096,128]{1,0:T(8,128)S(1)}, f32[512,128]{1,0:T(8,128)S(1)}, f32[512,128]{1,0:T(8,128)S(1)}, f32[72,128]{1,0:T(8,128)S(1)}, f32[32,128]{1,0:T(8,128)S(1)}) custom-call(s32[2]{0:T(128)S(1)} %pad_add_fusion.odd_ref, f32[3200,128]{1,0:T(8,128)S(1)} %bitcast.13, f32[8,128]{1,0:T(8,128)S(1)} %broadcast_select_fusion.mask_ref.rest_8_, ...), custom_call_target="tpu_custom_call" | custom-call | tf_op jit(solution)/shard_map/first/pallas_call | solution.py:624
  63.5 4.7 %collective-permute-start.1 = (f32[512,128]{1,0:T(8,128)S(1)}, f32[512,128]{1,0:T(8,128)S(1)}, u32[]{:S(2)}, u32[]{:S(2)}) collective-permute-start(f32[512,128]{1,0:T(8,128)S(1)} %get-tuple-element.60), channel_id=1, source_target_pairs={{8,16},{16,8},{24,32},{32,24},{40,48},{48,40},{56,64},{64,56},{72,... | collective-permute-start | bytes 786440 | tf_op jit(solution)/shard_map/ppermute | solution.py:636
  68.2 0.9 collective-permute-start.4
  69.2 4.0 %collective-permute-start.3 = (f32[72,128]{1,0:T(8,128)S(1)}, f32[72,128]{1,0:T(8,128)S(1)}, u32[]{:S(2)}, u32[]{:S(2)}) collective-permute-start(f32[72,128]{1,0:T(8,128)S(1)} %get-tuple-element.62.own_column_ref), channel_id=1, source_target_pairs={{1,2},{2,1},{3,4},{4,3},{5,6},{6,5},{7,0},{0,7},{9,10},{10,9},{11,... | collective-permute-start | bytes 110600 | tf_op jit(solution)/shard_map/ppermute | solution.py:637
  73.2 1.3 %collective-permute-start.5 = (f32[32,128]{1,0:T(8,128)S(1)}, f32[32,128]{1,0:T(8,128)S(1)}, u32[]{:S(2)}, u32[]{:S(2)}) collective-permute-start(f32[32,128]{1,0:T(8,128)S(1)} %get-tuple-element.65), channel_id=1, source_target_pairs={{0,128},{1,129},{2,130},{3,131},{4,132},{5,133},{6,134},{7,135},{8... | collective-permute-start | bytes 49160 | tf_op jit(solution)/shard_map/ppermute | solution.py:639
  74.6 0.9 forcing.2.f_ref
  75.9 2.7 %start.1 = (f32[4096,128]{1,0:T(8,128)S(1)}, f32[64,128]{1,0:T(8,128)S(1)}) custom-call(f32[4,4]{1,0:T(4,128)S(1)} %bitcast.20, s32[2]{0:T(128)S(1)} %pad_add_fusion.odd_ref, f32[4096,128]{1,0:T(8,128)S(1)} %get-tuple-element.53.m_ref.rest_1_, f32[1024,128]{1,0:T(8,128)S(1)} %copy-done.15, f32[1024,128]{1,0:T(8,128)S(1)} %copy-done.17, ...), custom_call_target="tpu_custom_call" | custom-call | flops 33554432 | bytes 8388608 | tf_op jit(solution)/shard_map/start/pallas_call | solution.py:655
  79.3 1.1 edge.2
  80.4 1.6 %collective-permute-start.6 = (f32[512,128]{1,0:T(8,128)S(1)}, f32[512,128]{1,0:T(8,128)S(1)}, u32[]{:S(2)}, u32[]{:S(2)}) collective-permute-start(f32[512,128]{1,0:T(8,128)S(1)} %get-tuple-element.70), channel_id=1, source_target_pairs={{0,8},{8,0},{16,24},{24,16},{32,40},{40,32},{48,56},{56,48},{64,72... | collective-permute-start | bytes 786440 | tf_op jit(solution)/shard_map/ppermute | solution.py:635
  82.0 3.0 %collective-permute-start.7 = (f32[512,128]{1,0:T(8,128)S(1)}, f32[512,128]{1,0:T(8,128)S(1)}, u32[]{:S(2)}, u32[]{:S(2)}) collective-permute-start(f32[512,128]{1,0:T(8,128)S(1)} %get-tuple-element.71), channel_id=1, source_target_pairs={{8,16},{16,8},{24,32},{32,24},{40,48},{48,40},{56,64},{64,56},{72,... | collective-permute-start | bytes 786440 | tf_op jit(solution)/shard_map/ppermute | solution.py:636
  85.1 4.0 %collective-permute-start.8 = (f32[72,128]{1,0:T(8,128)S(1)}, f32[72,128]{1,0:T(8,128)S(1)}, u32[]{:S(2)}, u32[]{:S(2)}) collective-permute-start(f32[72,128]{1,0:T(8,128)S(1)} %get-tuple-element.73.own_column_ref), channel_id=1, source_target_pairs={{1,2},{2,1},{3,4},{4,3},{5,6},{6,5},{7,0},{0,7},{9,10},{10,9},{11,... | collective-permute-start | bytes 110600 | tf_op jit(solution)/shard_map/ppermute | solution.py:637
  89.1 1.5 %collective-permute-start.10 = (f32[32,128]{1,0:T(8,128)S(1)}, f32[32,128]{1,0:T(8,128)S(1)}, u32[]{:S(2)}, u32[]{:S(2)}) collective-permute-start(f32[32,128]{1,0:T(8,128)S(1)} %get-tuple-element.74), channel_id=1, source_target_pairs={{0,128},{1,129},{2,130},{3,131},{4,132},{5,133},{6,134},{7,135},{8... | collective-permute-start | bytes 49160 | tf_op jit(solution)/shard_map/ppermute | solution.py:639
  90.6 0.8 forcing.3.rest_9_
  91.5 3.6 %inner.2 = (f32[4096,128]{1,0:T(8,128)S(1)}, f32[4096,128]{1,0:T(8,128)S(1)}, f32[64,128]{1,0:T(8,128)S(1)}) custom-call(f32[4,4]{1,0:T(4,128)S(1)} %bitcast.21, s32[2]{0:T(128)S(1)} %pad_add_fusion.odd_ref, f32[1024,128]{1,0:T(8,128)S(1)} %copy-done.9, f32[1024,128]{1,0:T(8,128)S(1)} %copy-done.11, ...), custom_call_target="tpu_custom_call" | custom-call | flops 33554432 | bytes 8388608 | tf_op jit(solution)/shard_map/inner/pallas_call | solution.py:665
  95.1 2.3 %collective-permute-done.8.from_column1_ref = f32[72,128]{1,0:T(8,128)S(1)} collective-permute-done((f32[72,128]{1,0:T(8,128)S(1)}, f32[72,128]{1,0:T(8,128)S(1)}, u32[]{:S(2)}, u32[]{:S(2)}) %collective-permute-start.8) | collective-permute-done | bytes 36896 | tf_op jit(solution)/shard_map/ppermute | solution.py:637
  97.4 1.1 edge.3
  99.2 2.9 %collective-permute-start.12 = (f32[512,128]{1,0:T(8,128)S(1)}, f32[512,128]{1,0:T(8,128)S(1)}, u32[]{:S(2)}, u32[]{:S(2)}) collective-permute-start(f32[512,128]{1,0:T(8,128)S(1)} %get-tuple-element.81), channel_id=1, source_target_pairs={{8,16},{16,8},{24,32},{32,24},{40,48},{48,40},{56,64},{64,56},{72,... | collective-permute-start | bytes 786440 | tf_op jit(solution)/shard_map/ppermute | solution.py:636
  102.2 4.2 %collective-permute-start.13 = (f32[72,128]{1,0:T(8,128)S(1)}, f32[72,128]{1,0:T(8,128)S(1)}, u32[]{:S(2)}, u32[]{:S(2)}) collective-permute-start(f32[72,128]{1,0:T(8,128)S(1)} %get-tuple-element.79.own_column_ref), channel_id=1, source_target_pairs={{1,2},{2,1},{3,4},{4,3},{5,6},{6,5},{7,0},{0,7},{9,10},{10,9},{11,... | collective-permute-start | bytes 110600 | tf_op jit(solution)/shard_map/ppermute | solution.py:637
  106.4 1.3 %collective-permute-start.15 = (f32[32,128]{1,0:T(8,128)S(1)}, f32[32,128]{1,0:T(8,128)S(1)}, u32[]{:S(2)}, u32[]{:S(2)}) collective-permute-start(f32[32,128]{1,0:T(8,128)S(1)} %get-tuple-element.82), channel_id=1, source_target_pairs={{0,128},{1,129},{2,130},{3,131},{4,132},{5,133},{6,134},{7,135},{8... | collective-permute-start | bytes 49160 | tf_op jit(solution)/shard_map/ppermute | solution.py:639
  107.7 2.9 %inner.3 = (f32[4096,128]{1,0:T(8,128)S(1)}, f32[4096,128]{1,0:T(8,128)S(1)}) custom-call(f32[4,4]{1,0:T(4,128)S(1)} %bitcast.22, s32[2]{0:T(128)S(1)} %pad_add_fusion.odd_ref, f32[1024,128]{1,0:T(8,128)S(1)} %copy-done.3, f32[1024,128]{1,0:T(8,128)S(1)} %copy-done.5, f32[1024,128]{1,0:T(8,128)S(1)} %get-tuple-element.46.c_ref.up_n_ref, ...), custom_call_target="tpu_custom_call" | custom-call | flops 33554432 | bytes 8388608 | tf_op jit(solution)/shard_map/inner/pallas_call | solution.py:665
  110.6 3.6 %collective-permute-done.13.from_column1_ref = f32[72,128]{1,0:T(8,128)S(1)} collective-permute-done((f32[72,128]{1,0:T(8,128)S(1)}, f32[72,128]{1,0:T(8,128)S(1)}, u32[]{:S(2)}, u32[]{:S(2)}) %collective-permute-start.13) | collective-permute-done | bytes 36896 | tf_op jit(solution)/shard_map/ppermute | solution.py:637
  114.2 2.4 %last.1 = f32[4096,128]{1,0:T(8,128)} custom-call(f32[4,4]{1,0:T(4,128)S(1)} %copy-done.20, s32[2]{0:T(128)S(1)} %pad_add_fusion.odd_ref, f32[4096,128]{1,0:T(8,128)S(1)} %get-tuple-element.77.p_ref, f32[4096,128]{1,0:T(8,128)S(1)} %get-tuple-element.78.m_ref, f32[1024,128]{1,0:T(8,128)S(1)} %get-tuple-element.46.c_ref.up_n_ref, ...), custom_call_target="tpu_custom_call" | custom-call | tf_op jit(solution)/shard_map/last/pallas_call | solution.py:703
  (65 shorter events, 7.9 us)
Async XLA Ops:
  3.0 58.8 %all-to-all-start = ((f32[128,1,3200]{2,1,0:T(1,128)}), f32[128,1,3200]{2,1,0:T(1,128)S(1)}, u32[]{:S(2)}, u32[]{:S(2)}) async-start(f32[128,1,3200]{2,1,0:T(1,128)} %bitcast.23), calls=%async_computation | async-start | bytes 3276800 | tf_op jit(solution)/shard_map/all_to_all | solution.py:600
  18.4 5.2 %copy-start.22 = (s32[8,128]{1,0:T(8,128)S(1)}, s32[8,128]{1,0:T(8,128)}, u32[]{:S(2)}) copy-start(s32[8,128]{1,0:T(8,128)} %param.15) | copy-start | bytes 12292
  20.2 53.0 %collective-permute-start.2 = (f32[384,128]{1,0:T(8,128)}, f32[384,128]{1,0:T(8,128)S(1)}, u32[]{:S(2)}, u32[]{:S(2)}) collective-permute-start(f32[384,128]{1,0:T(8,128)} %rim.1), channel_id=1, source_target_pairs={{0,8},{8,16},{16,24},{24,32},{32,40},{40,48},{48,56},{56,64},{64,7... | collective-permute-start | bytes 589832 | tf_op jit(solution)/shard_map/ppermute | solution.py:572
  23.7 1.9 %copy-start = (f32[1,3,2,128,8,128]{5,4,3,2,1,0:T(8,128)S(1)}, f32[1,3,2,128,8,128]{5,4,3,2,1,0:T(8,128)}, u32[]{:S(2)}) copy-start(f32[1,3,2,128,8,128]{5,4,3,2,1,0:T(8,128)} %param.11) | copy-start | bytes 9437188
  25.6 1.9 %copy-start.1 = (f32[1,3,2,128,8,128]{5,4,3,2,1,0:T(8,128)S(1)}, f32[1,3,2,128,8,128]{5,4,3,2,1,0:T(8,128)}, u32[]{:S(2)}) copy-start(f32[1,3,2,128,8,128]{5,4,3,2,1,0:T(8,128)} %param.12) | copy-start | bytes 9437188
  30.5 0.8 copy-start.4
  63.4 15.9 %collective-permute-start = (f32[512,128]{1,0:T(8,128)S(1)}, f32[512,128]{1,0:T(8,128)S(1)}, u32[]{:S(2)}, u32[]{:S(2)}) collective-permute-start(f32[512,128]{1,0:T(8,128)S(1)} %get-tuple-element.59), channel_id=1, source_target_pairs={{0,8},{8,0},{16,24},{24,16},{32,40},{40,32},{48,56},{56,48},{64,72... | collective-permute-start | bytes 786440 | tf_op jit(solution)/shard_map/ppermute | solution.py:635
  63.5 15.8 %collective-permute-start.1 = (f32[512,128]{1,0:T(8,128)S(1)}, f32[512,128]{1,0:T(8,128)S(1)}, u32[]{:S(2)}, u32[]{:S(2)}) collective-permute-start(f32[512,128]{1,0:T(8,128)S(1)} %get-tuple-element.60), channel_id=1, source_target_pairs={{8,16},{16,8},{24,32},{32,24},{40,48},{48,40},{56,64},{64,56},{72,... | collective-permute-start | bytes 786440 | tf_op jit(solution)/shard_map/ppermute | solution.py:636
  68.2 10.4 %collective-permute-start.4 = (f32[72,128]{1,0:T(8,128)S(1)}, f32[72,128]{1,0:T(8,128)S(1)}, u32[]{:S(2)}, u32[]{:S(2)}) collective-permute-start(f32[72,128]{1,0:T(8,128)S(1)} %get-tuple-element.62.own_column_ref), channel_id=1, source_target_pairs={{0,1},{1,0},{2,3},{3,2},{4,5},{5,4},{6,7},{7,6},{8,9},{9,8},{10,11... | collective-permute-start | bytes 110600 | tf_op jit(solution)/shard_map/ppermute | solution.py:638
  69.2 10.1 %collective-permute-start.3 = (f32[72,128]{1,0:T(8,128)S(1)}, f32[72,128]{1,0:T(8,128)S(1)}, u32[]{:S(2)}, u32[]{:S(2)}) collective-permute-start(f32[72,128]{1,0:T(8,128)S(1)} %get-tuple-element.62.own_column_ref), channel_id=1, source_target_pairs={{1,2},{2,1},{3,4},{4,3},{5,6},{6,5},{7,0},{0,7},{9,10},{10,9},{11,... | collective-permute-start | bytes 110600 | tf_op jit(solution)/shard_map/ppermute | solution.py:637
  73.2 5.4 %collective-permute-start.5 = (f32[32,128]{1,0:T(8,128)S(1)}, f32[32,128]{1,0:T(8,128)S(1)}, u32[]{:S(2)}, u32[]{:S(2)}) collective-permute-start(f32[32,128]{1,0:T(8,128)S(1)} %get-tuple-element.65), channel_id=1, source_target_pairs={{0,128},{1,129},{2,130},{3,131},{4,132},{5,133},{6,134},{7,135},{8... | collective-permute-start | bytes 49160 | tf_op jit(solution)/shard_map/ppermute | solution.py:639
  74.5 1.0 copy-start.15
  74.5 1.2 %copy-start.17 = (f32[1024,128]{1,0:T(8,128)S(1)}, f32[1024,128]{1,0:T(8,128)}, u32[]{:S(2)}) copy-start(f32[1024,128]{1,0:T(8,128)} %copy-done.16) | copy-start | bytes 1572868
  74.5 1.3 %copy-start.19 = (f32[1024,128]{1,0:T(8,128)S(1)}, f32[1024,128]{1,0:T(8,128)}, u32[]{:S(2)}) copy-start(f32[1024,128]{1,0:T(8,128)} %copy-done.18) | copy-start | bytes 1572868
  74.5 1.3 %copy-start.21 = (f32[1,4,4]{2,1,0:T(4,128)S(1)}, f32[1,4,4]{2,1,0:T(4,128)}, u32[]{:S(2)}) copy-start(f32[1,4,4]{2,1,0:T(4,128)} %param.13) | copy-start | bytes 196
  75.9 3.4 %copy-start.20 = (f32[4,4]{1,0:T(4,128)S(1)}, f32[4,4]{1,0:T(4,128)}, u32[]{:S(2)}) copy-start(f32[4,4]{1,0:T(4,128)} %air_ref.5) | copy-start | bytes 196
  80.4 11.1 %copy-start.9 = (f32[1024,128]{1,0:T(8,128)S(1)}, f32[1024,128]{1,0:T(8,128)}, u32[]{:S(2)}) copy-start(f32[1024,128]{1,0:T(8,128)} %copy-done.8) | copy-start | bytes 1572868
  80.4 11.1 %copy-start.11 = (f32[1024,128]{1,0:T(8,128)S(1)}, f32[1024,128]{1,0:T(8,128)}, u32[]{:S(2)}) copy-start(f32[1024,128]{1,0:T(8,128)} %copy-done.10) | copy-start | bytes 1572868
  80.4 11.1 %copy-start.13 = (f32[1024,128]{1,0:T(8,128)S(1)}, f32[1024,128]{1,0:T(8,128)}, u32[]{:S(2)}) copy-start(f32[1024,128]{1,0:T(8,128)} %copy-done.12) | copy-start | bytes 1572868
  80.4 16.9 %collective-permute-start.6 = (f32[512,128]{1,0:T(8,128)S(1)}, f32[512,128]{1,0:T(8,128)S(1)}, u32[]{:S(2)}, u32[]{:S(2)}) collective-permute-start(f32[512,128]{1,0:T(8,128)S(1)} %get-tuple-element.70), channel_id=1, source_target_pairs={{0,8},{8,0},{16,24},{24,16},{32,40},{40,32},{48,56},{56,48},{64,72... | collective-permute-start | bytes 786440 | tf_op jit(solution)/shard_map/ppermute | solution.py:635
  82.0 15.4 %collective-permute-start.7 = (f32[512,128]{1,0:T(8,128)S(1)}, f32[512,128]{1,0:T(8,128)S(1)}, u32[]{:S(2)}, u32[]{:S(2)}) collective-permute-start(f32[512,128]{1,0:T(8,128)S(1)} %get-tuple-element.71), channel_id=1, source_target_pairs={{8,16},{16,8},{24,32},{32,24},{40,48},{48,40},{56,64},{64,56},{72,... | collective-permute-start | bytes 786440 | tf_op jit(solution)/shard_map/ppermute | solution.py:636
  85.0 10.0 %collective-permute-start.9 = (f32[72,128]{1,0:T(8,128)S(1)}, f32[72,128]{1,0:T(8,128)S(1)}, u32[]{:S(2)}, u32[]{:S(2)}) collective-permute-start(f32[72,128]{1,0:T(8,128)S(1)} %get-tuple-element.73.own_column_ref), channel_id=1, source_target_pairs={{0,1},{1,0},{2,3},{3,2},{4,5},{5,4},{6,7},{7,6},{8,9},{9,8},{10,11... | collective-permute-start | bytes 110600 | tf_op jit(solution)/shard_map/ppermute | solution.py:638
  85.1 12.2 %collective-permute-start.8 = (f32[72,128]{1,0:T(8,128)S(1)}, f32[72,128]{1,0:T(8,128)S(1)}, u32[]{:S(2)}, u32[]{:S(2)}) collective-permute-start(f32[72,128]{1,0:T(8,128)S(1)} %get-tuple-element.73.own_column_ref), channel_id=1, source_target_pairs={{1,2},{2,1},{3,4},{4,3},{5,6},{6,5},{7,0},{0,7},{9,10},{10,9},{11,... | collective-permute-start | bytes 110600 | tf_op jit(solution)/shard_map/ppermute | solution.py:637
  89.1 5.9 %collective-permute-start.10 = (f32[32,128]{1,0:T(8,128)S(1)}, f32[32,128]{1,0:T(8,128)S(1)}, u32[]{:S(2)}, u32[]{:S(2)}) collective-permute-start(f32[32,128]{1,0:T(8,128)S(1)} %get-tuple-element.74), channel_id=1, source_target_pairs={{0,128},{1,129},{2,130},{3,131},{4,132},{5,133},{6,134},{7,135},{8... | collective-permute-start | bytes 49160 | tf_op jit(solution)/shard_map/ppermute | solution.py:639
  97.4 10.3 %copy-start.3 = (f32[1024,128]{1,0:T(8,128)S(1)}, f32[1024,128]{1,0:T(8,128)}, u32[]{:S(2)}) copy-start(f32[1024,128]{1,0:T(8,128)} %copy-done.2) | copy-start | bytes 1572868
  97.4 10.3 %copy-start.5 = (f32[1024,128]{1,0:T(8,128)S(1)}, f32[1024,128]{1,0:T(8,128)}, u32[]{:S(2)}) copy-start(f32[1024,128]{1,0:T(8,128)} %copy-done.4) | copy-start | bytes 1572868
  97.4 10.3 %copy-start.7 = (f32[1024,128]{1,0:T(8,128)S(1)}, f32[1024,128]{1,0:T(8,128)}, u32[]{:S(2)}) copy-start(f32[1024,128]{1,0:T(8,128)} %copy-done.6) | copy-start | bytes 1572868
  98.5 15.7 %collective-permute-start.11 = (f32[512,128]{1,0:T(8,128)S(1)}, f32[512,128]{1,0:T(8,128)S(1)}, u32[]{:S(2)}, u32[]{:S(2)}) collective-permute-start(f32[512,128]{1,0:T(8,128)S(1)} %get-tuple-element.80), channel_id=1, source_target_pairs={{0,8},{8,0},{16,24},{24,16},{32,40},{40,32},{48,56},{56,48},{64,72... | collective-permute-start | bytes 786440 | tf_op jit(solution)/shard_map/ppermute | solution.py:635
  99.2 15.0 %collective-permute-start.12 = (f32[512,128]{1,0:T(8,128)S(1)}, f32[512,128]{1,0:T(8,128)S(1)}, u32[]{:S(2)}, u32[]{:S(2)}) collective-permute-start(f32[512,128]{1,0:T(8,128)S(1)} %get-tuple-element.81), channel_id=1, source_target_pairs={{8,16},{16,8},{24,32},{32,24},{40,48},{48,40},{56,64},{64,56},{72,... | collective-permute-start | bytes 786440 | tf_op jit(solution)/shard_map/ppermute | solution.py:636
  102.1 8.5 %collective-permute-start.14 = (f32[72,128]{1,0:T(8,128)S(1)}, f32[72,128]{1,0:T(8,128)S(1)}, u32[]{:S(2)}, u32[]{:S(2)}) collective-permute-start(f32[72,128]{1,0:T(8,128)S(1)} %get-tuple-element.79.own_column_ref), channel_id=1, source_target_pairs={{0,1},{1,0},{2,3},{3,2},{4,5},{5,4},{6,7},{7,6},{8,9},{9,8},{10,11... | collective-permute-start | bytes 110600 | tf_op jit(solution)/shard_map/ppermute | solution.py:638
  102.2 12.0 %collective-permute-start.13 = (f32[72,128]{1,0:T(8,128)S(1)}, f32[72,128]{1,0:T(8,128)S(1)}, u32[]{:S(2)}, u32[]{:S(2)}) collective-permute-start(f32[72,128]{1,0:T(8,128)S(1)} %get-tuple-element.79.own_column_ref), channel_id=1, source_target_pairs={{1,2},{2,1},{3,4},{4,3},{5,6},{6,5},{7,0},{0,7},{9,10},{10,9},{11,... | collective-permute-start | bytes 110600 | tf_op jit(solution)/shard_map/ppermute | solution.py:637
  106.4 4.2 %collective-permute-start.15 = (f32[32,128]{1,0:T(8,128)S(1)}, f32[32,128]{1,0:T(8,128)S(1)}, u32[]{:S(2)}, u32[]{:S(2)}) collective-permute-start(f32[32,128]{1,0:T(8,128)S(1)} %get-tuple-element.82), channel_id=1, source_target_pairs={{0,128},{1,129},{2,130},{3,131},{4,132},{5,133},{6,134},{7,135},{8... | collective-permute-start | bytes 49160 | tf_op jit(solution)/shard_map/ppermute | solution.py:639
  (8 other events, 6.4 us)

commit v8 on v7

--- a/solution.py
+++ b/solution.py
@@ -9,7 +9,7 @@
 
 LANES = 128
 SUBS = 8
-BATCH = 4
+BATCH = 16
 VMEM_LIMIT = 12 * 1024 * 1024
 VMEM_WHOLE = 58 * 1024 * 1024
 
@@ -349,7 +349,7 @@
             lambda f, group, y: p_ref[rows_of((y * fields + f) * levels, group), :],
             fields,
             range(levels // SUBS),
-            range(SUBS),
+            range(1, SUBS - 1),
             [jnp.zeros((SUBS, LANES), jnp.float32)] * (2 * fields),
         )
         for i, half in enumerate(halves):

time: 118 us -> 118 us (level)
  waiting for transfers between devices: 31.2 us -> 32.5 us
    ppermute x3, waiting for transfers between devices: 6.47 us -> 7.75 us  [shards(): lax.ppermute(columns, 'lon', swaps('lon', 1, True))]
  transfers between devices with their start and end apart: 17 -> 17, of which waited for: 4 -> 4; matrix products, arithmetic and copies ran while one was open for 0% -> 0% of each run, Pallas kernels for 14% -> 13%
where the time goes in v8:
time: 118 us; the launch traced here: 117 us
  starting transfers between devices  49.4 us (42%)
  waiting for transfers between devices  32.5 us (28%)
  Pallas kernels  23 us (19%)
  local copies, waits for them, and re-layouts  11.5 us (10%)
    all_to_all x1, waiting for transfers between devices, shards(): lax.all_to_all(sent.reshape(owners, 1, stride * LANES), ('lat', 'lon'), s...  24.7 us
    all_to_all x1, starting transfers between devices, shards(): lax.all_to_all(sent.reshape(owners, 1, stride * LANES), ('lat', 'lon'), s...  15.5 us
    ppermute x3, starting transfers between devices, shards(): lax.ppermute(columns, 'lon', swaps('lon', 1, True))  12.2 us
    unnamed x46, local copies, waits for them, and re-layouts  11.5 us
    ppermute x3, starting transfers between devices, shards(): lax.ppermute(slab2, 'lat', swaps('lat', 1, False))  10.8 us
    ppermute x3, waiting for transfers between devices, shards(): lax.ppermute(columns, 'lon', swaps('lon', 1, True))  7.75 us
    pallas_call x2, Pallas kernels, shards(): pl.pallas_call(functools.partial(inner_kernel, last, step, fields, levels...  5.39 us
    ppermute x3, starting transfers between devices, shards(): lax.ppermute(low, 'comp', [(0, 1)])  3.84 us
  transfers between devices with their start and end apart: 17, of which 4 were waited for; matrix products, arithmetic and copies ran while one was open for 0% of the time, Pallas kernels for 13%

profile of v8, /device:TPU:8, one launch (start us, length us, event | category | flops | bytes accessed | tf_op | source)
XLA Modules:
  0.0 117.1 jit_solution(9783349949754092574)
XLA Ops:
  0.0 3.0 %pack.1 = f32[3200,128]{1,0:T(8,128)} custom-call(f32[3,128,512]{2,1,0:T(8,128)} %bitcast.24, s32[3,1,128]{2,1,0:T(1,128)} %bitcast.25, s32[3,1,128]{2,1,0:T(1,128)} %bitcast.26), custom_call_target="tpu_custom_call" | custom-call | tf_op jit(solution)/shard_map/pack/pallas_call | solution.py:583
  3.0 15.5 %all-to-all-start = ((f32[128,1,3200]{2,1,0:T(1,128)}), f32[128,1,3200]{2,1,0:T(1,128)S(1)}, u32[]{:S(2)}, u32[]{:S(2)}) async-start(f32[128,1,3200]{2,1,0:T(1,128)} %bitcast.23), calls=%async_computation | async-start | bytes 3276800 | tf_op jit(solution)/shard_map/all_to_all | solution.py:600
  18.4 1.8 %rim.1 = f32[384,128]{1,0:T(8,128)} custom-call(f32[3,2,128,8,128]{4,3,2,1,0:T(8,128)} %bitcast.16, f32[3,2,128,8,128]{4,3,2,1,0:T(8,128)} %bitcast.18), custom_call_target="tpu_custom_call" | custom-call | tf_op jit(solution)/shard_map/rim/pallas_call | solution.py:564
  20.2 3.4 %collective-permute-start.2 = (f32[384,128]{1,0:T(8,128)}, f32[384,128]{1,0:T(8,128)S(1)}, u32[]{:S(2)}, u32[]{:S(2)}) collective-permute-start(f32[384,128]{1,0:T(8,128)} %rim.1), channel_id=1, source_target_pairs={{0,8},{8,16},{16,24},{24,32},{32,40},{40,48},{48,56},{56,64},{64,7... | collective-permute-start | bytes 589832 | tf_op jit(solution)/shard_map/ppermute | solution.py:572
  23.7 1.9 %copy-done = f32[1,3,2,128,8,128]{5,4,3,2,1,0:T(8,128)S(1)} copy-done((f32[1,3,2,128,8,128]{5,4,3,2,1,0:T(8,128)S(1)}, f32[1,3,2,128,8,128]{5,4,3,2,1,0:T(8,128)}, u32[]{:S(2)}) %copy-start) | copy-done | bytes 3145752
  25.6 1.9 %copy-done.1 = f32[1,3,2,128,8,128]{5,4,3,2,1,0:T(8,128)S(1)} copy-done((f32[1,3,2,128,8,128]{5,4,3,2,1,0:T(8,128)S(1)}, f32[1,3,2,128,8,128]{5,4,3,2,1,0:T(8,128)}, u32[]{:S(2)}) %copy-start.1) | copy-done | bytes 3145752
  27.5 2.2 %coefficients.1 = (f32[1024,128]{1,0:T(8,128)S(1)}, f32[1024,128]{1,0:T(8,128)S(1)}, f32[1024,128]{1,0:T(8,128)S(1)}, f32[1024,128]{1,0:T(8,128)S(1)}, f32[1024,...) custom-call(f32[6144,128]{1,0:T(8,128)S(1)} %bitcast.17, ...), custom_call_target="tpu_custom_call" | custom-call | flops 4194304 | bytes 8388608 | tf_op jit(solution)/shard_map/coefficients/pallas_call | solution.py:605
  30.5 0.8 copy-done.4
  37.0 24.7 %all-to-all-done = f32[128,1,3200]{2,1,0:T(1,128)S(1)} async-done(((f32[128,1,3200]{2,1,0:T(1,128)}), f32[128,1,3200]{2,1,0:T(1,128)S(1)}, u32[]{:S(2)}, u32[]{:S(2)}) %all-to-all-start) | async-done | bytes 1638432 | tf_op jit(solution)/shard_map/all_to_all | solution.py:600
  61.7 1.7 %first.1 = (f32[4096,128]{1,0:T(8,128)S(1)}, f32[512,128]{1,0:T(8,128)S(1)}, f32[512,128]{1,0:T(8,128)S(1)}, f32[72,128]{1,0:T(8,128)S(1)}, f32[32,128]{1,0:T(8,128)S(1)}) custom-call(s32[2]{0:T(128)S(1)} %pad_add_fusion.odd_ref, f32[3200,128]{1,0:T(8,128)S(1)} %bitcast.13, f32[8,128]{1,0:T(8,128)S(1)} %broadcast_select_fusion.mask_ref.rest_8_, ...), custom_call_target="tpu_custom_call" | custom-call | tf_op jit(solution)/shard_map/first/pallas_call | solution.py:624
  63.5 4.7 %collective-permute-start.1 = (f32[512,128]{1,0:T(8,128)S(1)}, f32[512,128]{1,0:T(8,128)S(1)}, u32[]{:S(2)}, u32[]{:S(2)}) collective-permute-start(f32[512,128]{1,0:T(8,128)S(1)} %get-tuple-element.60), channel_id=1, source_target_pairs={{8,16},{16,8},{24,32},{32,24},{40,48},{48,40},{56,64},{64,56},{72,... | collective-permute-start | bytes 786440 | tf_op jit(solution)/shard_map/ppermute | solution.py:636
  68.2 0.9 collective-permute-start.4
  69.2 4.0 %collective-permute-start.3 = (f32[72,128]{1,0:T(8,128)S(1)}, f32[72,128]{1,0:T(8,128)S(1)}, u32[]{:S(2)}, u32[]{:S(2)}) collective-permute-start(f32[72,128]{1,0:T(8,128)S(1)} %get-tuple-element.62.own_column_ref), channel_id=1, source_target_pairs={{1,2},{2,1},{3,4},{4,3},{5,6},{6,5},{7,0},{0,7},{9,10},{10,9},{11,... | collective-permute-start | bytes 110600 | tf_op jit(solution)/shard_map/ppermute | solution.py:637
  73.2 1.3 %collective-permute-start.5 = (f32[32,128]{1,0:T(8,128)S(1)}, f32[32,128]{1,0:T(8,128)S(1)}, u32[]{:S(2)}, u32[]{:S(2)}) collective-permute-start(f32[32,128]{1,0:T(8,128)S(1)} %get-tuple-element.65), channel_id=1, source_target_pairs={{0,128},{1,129},{2,130},{3,131},{4,132},{5,133},{6,134},{7,135},{8... | collective-permute-start | bytes 49160 | tf_op jit(solution)/shard_map/ppermute | solution.py:639
  74.6 0.9 forcing.2.f_ref
  75.9 2.4 %start.1 = (f32[4096,128]{1,0:T(8,128)S(1)}, f32[64,128]{1,0:T(8,128)S(1)}) custom-call(f32[4,4]{1,0:T(4,128)S(1)} %bitcast.20, s32[2]{0:T(128)S(1)} %pad_add_fusion.odd_ref, f32[4096,128]{1,0:T(8,128)S(1)} %get-tuple-element.53.m_ref.rest_1_, f32[1024,128]{1,0:T(8,128)S(1)} %copy-done.15, f32[1024,128]{1,0:T(8,128)S(1)} %copy-done.17, ...), custom_call_target="tpu_custom_call" | custom-call | flops 33554432 | bytes 8388608 | tf_op jit(solution)/shard_map/start/pallas_call | solution.py:655
  78.3 0.9 collective-permute-done.3.from_column1_ref
  79.3 1.1 edge.2
  80.4 1.6 %collective-permute-start.6 = (f32[512,128]{1,0:T(8,128)S(1)}, f32[512,128]{1,0:T(8,128)S(1)}, u32[]{:S(2)}, u32[]{:S(2)}) collective-permute-start(f32[512,128]{1,0:T(8,128)S(1)} %get-tuple-element.70), channel_id=1, source_target_pairs={{0,8},{8,0},{16,24},{24,16},{32,40},{40,32},{48,56},{56,48},{64,72... | collective-permute-start | bytes 786440 | tf_op jit(solution)/shard_map/ppermute | solution.py:635
  82.0 3.0 %collective-permute-start.7 = (f32[512,128]{1,0:T(8,128)S(1)}, f32[512,128]{1,0:T(8,128)S(1)}, u32[]{:S(2)}, u32[]{:S(2)}) collective-permute-start(f32[512,128]{1,0:T(8,128)S(1)} %get-tuple-element.71), channel_id=1, source_target_pairs={{8,16},{16,8},{24,32},{32,24},{40,48},{48,40},{56,64},{64,56},{72,... | collective-permute-start | bytes 786440 | tf_op jit(solution)/shard_map/ppermute | solution.py:636
  85.3 4.0 %collective-permute-start.8 = (f32[72,128]{1,0:T(8,128)S(1)}, f32[72,128]{1,0:T(8,128)S(1)}, u32[]{:S(2)}, u32[]{:S(2)}) collective-permute-start(f32[72,128]{1,0:T(8,128)S(1)} %get-tuple-element.73.own_column_ref), channel_id=1, source_target_pairs={{1,2},{2,1},{3,4},{4,3},{5,6},{6,5},{7,0},{0,7},{9,10},{10,9},{11,... | collective-permute-start | bytes 110600 | tf_op jit(solution)/shard_map/ppermute | solution.py:637
  89.3 1.3 %collective-permute-start.10 = (f32[32,128]{1,0:T(8,128)S(1)}, f32[32,128]{1,0:T(8,128)S(1)}, u32[]{:S(2)}, u32[]{:S(2)}) collective-permute-start(f32[32,128]{1,0:T(8,128)S(1)} %get-tuple-element.74), channel_id=1, source_target_pairs={{0,128},{1,129},{2,130},{3,131},{4,132},{5,133},{6,134},{7,135},{8... | collective-permute-start | bytes 49160 | tf_op jit(solution)/shard_map/ppermute | solution.py:639
  90.6 0.8 forcing.3.rest_9_
  91.5 2.9 %inner.2 = (f32[4096,128]{1,0:T(8,128)S(1)}, f32[4096,128]{1,0:T(8,128)S(1)}, f32[64,128]{1,0:T(8,128)S(1)}) custom-call(f32[4,4]{1,0:T(4,128)S(1)} %bitcast.21, s32[2]{0:T(128)S(1)} %pad_add_fusion.odd_ref, f32[1024,128]{1,0:T(8,128)S(1)} %copy-done.9, f32[1024,128]{1,0:T(8,128)S(1)} %copy-done.11, ...), custom_call_target="tpu_custom_call" | custom-call | flops 33554432 | bytes 8388608 | tf_op jit(solution)/shard_map/inner/pallas_call | solution.py:665
  94.4 2.9 %collective-permute-done.8.from_column1_ref = f32[72,128]{1,0:T(8,128)S(1)} collective-permute-done((f32[72,128]{1,0:T(8,128)S(1)}, f32[72,128]{1,0:T(8,128)S(1)}, u32[]{:S(2)}, u32[]{:S(2)}) %collective-permute-start.8) | collective-permute-done | bytes 36896 | tf_op jit(solution)/shard_map/ppermute | solution.py:637
  97.4 1.1 edge.3
  99.2 3.1 %collective-permute-start.12 = (f32[512,128]{1,0:T(8,128)S(1)}, f32[512,128]{1,0:T(8,128)S(1)}, u32[]{:S(2)}, u32[]{:S(2)}) collective-permute-start(f32[512,128]{1,0:T(8,128)S(1)} %get-tuple-element.81), channel_id=1, source_target_pairs={{8,16},{16,8},{24,32},{32,24},{40,48},{48,40},{56,64},{64,56},{72,... | collective-permute-start | bytes 786440 | tf_op jit(solution)/shard_map/ppermute | solution.py:636
  102.4 4.2 %collective-permute-start.13 = (f32[72,128]{1,0:T(8,128)S(1)}, f32[72,128]{1,0:T(8,128)S(1)}, u32[]{:S(2)}, u32[]{:S(2)}) collective-permute-start(f32[72,128]{1,0:T(8,128)S(1)} %get-tuple-element.79.own_column_ref), channel_id=1, source_target_pairs={{1,2},{2,1},{3,4},{4,3},{5,6},{6,5},{7,0},{0,7},{9,10},{10,9},{11,... | collective-permute-start | bytes 110600 | tf_op jit(solution)/shard_map/ppermute | solution.py:637
  106.6 1.3 %collective-permute-start.15 = (f32[32,128]{1,0:T(8,128)S(1)}, f32[32,128]{1,0:T(8,128)S(1)}, u32[]{:S(2)}, u32[]{:S(2)}) collective-permute-start(f32[32,128]{1,0:T(8,128)S(1)} %get-tuple-element.82), channel_id=1, source_target_pairs={{0,128},{1,129},{2,130},{3,131},{4,132},{5,133},{6,134},{7,135},{8... | collective-permute-start | bytes 49160 | tf_op jit(solution)/shard_map/ppermute | solution.py:639
  107.9 2.5 %inner.3 = (f32[4096,128]{1,0:T(8,128)S(1)}, f32[4096,128]{1,0:T(8,128)S(1)}) custom-call(f32[4,4]{1,0:T(4,128)S(1)} %bitcast.22, s32[2]{0:T(128)S(1)} %pad_add_fusion.odd_ref, f32[1024,128]{1,0:T(8,128)S(1)} %copy-done.3, f32[1024,128]{1,0:T(8,128)S(1)} %copy-done.5, f32[1024,128]{1,0:T(8,128)S(1)} %get-tuple-element.46.c_ref.up_n_ref, ...), custom_call_target="tpu_custom_call" | custom-call | flops 33554432 | bytes 8388608 | tf_op jit(solution)/shard_map/inner/pallas_call | solution.py:665
  110.4 3.9 %collective-permute-done.13.from_column1_ref = f32[72,128]{1,0:T(8,128)S(1)} collective-permute-done((f32[72,128]{1,0:T(8,128)S(1)}, f32[72,128]{1,0:T(8,128)S(1)}, u32[]{:S(2)}, u32[]{:S(2)}) %collective-permute-start.13) | collective-permute-done | bytes 36896 | tf_op jit(solution)/shard_map/ppermute | solution.py:637
  114.3 2.6 %last.1 = f32[4096,128]{1,0:T(8,128)} custom-call(f32[4,4]{1,0:T(4,128)S(1)} %copy-done.20, s32[2]{0:T(128)S(1)} %pad_add_fusion.odd_ref, f32[4096,128]{1,0:T(8,128)S(1)} %get-tuple-element.77.p_ref, f32[4096,128]{1,0:T(8,128)S(1)} %get-tuple-element.78.m_ref, f32[1024,128]{1,0:T(8,128)S(1)} %get-tuple-element.46.c_ref.up_n_ref, ...), custom_call_target="tpu_custom_call" | custom-call | tf_op jit(solution)/shard_map/last/pallas_call | solution.py:703
  (65 shorter events, 8.2 us)
Async XLA Ops:
  3.0 58.8 %all-to-all-start = ((f32[128,1,3200]{2,1,0:T(1,128)}), f32[128,1,3200]{2,1,0:T(1,128)S(1)}, u32[]{:S(2)}, u32[]{:S(2)}) async-start(f32[128,1,3200]{2,1,0:T(1,128)} %bitcast.23), calls=%async_computation | async-start | bytes 3276800 | tf_op jit(solution)/shard_map/all_to_all | solution.py:600
  18.4 5.2 %copy-start.22 = (s32[8,128]{1,0:T(8,128)S(1)}, s32[8,128]{1,0:T(8,128)}, u32[]{:S(2)}) copy-start(s32[8,128]{1,0:T(8,128)} %param.15) | copy-start | bytes 12292
  20.2 53.0 %collective-permute-start.2 = (f32[384,128]{1,0:T(8,128)}, f32[384,128]{1,0:T(8,128)S(1)}, u32[]{:S(2)}, u32[]{:S(2)}) collective-permute-start(f32[384,128]{1,0:T(8,128)} %rim.1), channel_id=1, source_target_pairs={{0,8},{8,16},{16,24},{24,32},{32,40},{40,48},{48,56},{56,64},{64,7... | collective-permute-start | bytes 589832 | tf_op jit(solution)/shard_map/ppermute | solution.py:572
  23.7 1.9 %copy-start = (f32[1,3,2,128,8,128]{5,4,3,2,1,0:T(8,128)S(1)}, f32[1,3,2,128,8,128]{5,4,3,2,1,0:T(8,128)}, u32[]{:S(2)}) copy-start(f32[1,3,2,128,8,128]{5,4,3,2,1,0:T(8,128)} %param.11) | copy-start | bytes 9437188
  25.6 1.9 %copy-start.1 = (f32[1,3,2,128,8,128]{5,4,3,2,1,0:T(8,128)S(1)}, f32[1,3,2,128,8,128]{5,4,3,2,1,0:T(8,128)}, u32[]{:S(2)}) copy-start(f32[1,3,2,128,8,128]{5,4,3,2,1,0:T(8,128)} %param.12) | copy-start | bytes 9437188
  30.5 0.8 copy-start.4
  63.4 15.9 %collective-permute-start = (f32[512,128]{1,0:T(8,128)S(1)}, f32[512,128]{1,0:T(8,128)S(1)}, u32[]{:S(2)}, u32[]{:S(2)}) collective-permute-start(f32[512,128]{1,0:T(8,128)S(1)} %get-tuple-element.59), channel_id=1, source_target_pairs={{0,8},{8,0},{16,24},{24,16},{32,40},{40,32},{48,56},{56,48},{64,72... | collective-permute-start | bytes 786440 | tf_op jit(solution)/shard_map/ppermute | solution.py:635
  63.5 15.8 %collective-permute-start.1 = (f32[512,128]{1,0:T(8,128)S(1)}, f32[512,128]{1,0:T(8,128)S(1)}, u32[]{:S(2)}, u32[]{:S(2)}) collective-permute-start(f32[512,128]{1,0:T(8,128)S(1)} %get-tuple-element.60), channel_id=1, source_target_pairs={{8,16},{16,8},{24,32},{32,24},{40,48},{48,40},{56,64},{64,56},{72,... | collective-permute-start | bytes 786440 | tf_op jit(solution)/shard_map/ppermute | solution.py:636
  68.2 10.1 %collective-permute-start.4 = (f32[72,128]{1,0:T(8,128)S(1)}, f32[72,128]{1,0:T(8,128)S(1)}, u32[]{:S(2)}, u32[]{:S(2)}) collective-permute-start(f32[72,128]{1,0:T(8,128)S(1)} %get-tuple-element.62.own_column_ref), channel_id=1, source_target_pairs={{0,1},{1,0},{2,3},{3,2},{4,5},{5,4},{6,7},{7,6},{8,9},{9,8},{10,11... | collective-permute-start | bytes 110600 | tf_op jit(solution)/shard_map/ppermute | solution.py:638
  69.2 10.1 %collective-permute-start.3 = (f32[72,128]{1,0:T(8,128)S(1)}, f32[72,128]{1,0:T(8,128)S(1)}, u32[]{:S(2)}, u32[]{:S(2)}) collective-permute-start(f32[72,128]{1,0:T(8,128)S(1)} %get-tuple-element.62.own_column_ref), channel_id=1, source_target_pairs={{1,2},{2,1},{3,4},{4,3},{5,6},{6,5},{7,0},{0,7},{9,10},{10,9},{11,... | collective-permute-start | bytes 110600 | tf_op jit(solution)/shard_map/ppermute | solution.py:637
  73.2 5.1 %collective-permute-start.5 = (f32[32,128]{1,0:T(8,128)S(1)}, f32[32,128]{1,0:T(8,128)S(1)}, u32[]{:S(2)}, u32[]{:S(2)}) collective-permute-start(f32[32,128]{1,0:T(8,128)S(1)} %get-tuple-element.65), channel_id=1, source_target_pairs={{0,128},{1,129},{2,130},{3,131},{4,132},{5,133},{6,134},{7,135},{8... | collective-permute-start | bytes 49160 | tf_op jit(solution)/shard_map/ppermute | solution.py:639
  74.5 1.0 copy-start.15
  74.5 1.2 %copy-start.17 = (f32[1024,128]{1,0:T(8,128)S(1)}, f32[1024,128]{1,0:T(8,128)}, u32[]{:S(2)}) copy-start(f32[1024,128]{1,0:T(8,128)} %copy-done.16) | copy-start | bytes 1572868
  74.5 1.3 %copy-start.19 = (f32[1024,128]{1,0:T(8,128)S(1)}, f32[1024,128]{1,0:T(8,128)}, u32[]{:S(2)}) copy-start(f32[1024,128]{1,0:T(8,128)} %copy-done.18) | copy-start | bytes 1572868
  74.5 1.3 %copy-start.21 = (f32[1,4,4]{2,1,0:T(4,128)S(1)}, f32[1,4,4]{2,1,0:T(4,128)}, u32[]{:S(2)}) copy-start(f32[1,4,4]{2,1,0:T(4,128)} %param.13) | copy-start | bytes 196
  75.9 3.4 %copy-start.20 = (f32[4,4]{1,0:T(4,128)S(1)}, f32[4,4]{1,0:T(4,128)}, u32[]{:S(2)}) copy-start(f32[4,4]{1,0:T(4,128)} %air_ref.5) | copy-start | bytes 196
  80.4 11.1 %copy-start.9 = (f32[1024,128]{1,0:T(8,128)S(1)}, f32[1024,128]{1,0:T(8,128)}, u32[]{:S(2)}) copy-start(f32[1024,128]{1,0:T(8,128)} %copy-done.8) | copy-start | bytes 1572868
  80.4 11.1 %copy-start.11 = (f32[1024,128]{1,0:T(8,128)S(1)}, f32[1024,128]{1,0:T(8,128)}, u32[]{:S(2)}) copy-start(f32[1024,128]{1,0:T(8,128)} %copy-done.10) | copy-start | bytes 1572868
  80.4 11.1 %copy-start.13 = (f32[1024,128]{1,0:T(8,128)S(1)}, f32[1024,128]{1,0:T(8,128)}, u32[]{:S(2)}) copy-start(f32[1024,128]{1,0:T(8,128)} %copy-done.12) | copy-start | bytes 1572868
  80.4 16.9 %collective-permute-start.6 = (f32[512,128]{1,0:T(8,128)S(1)}, f32[512,128]{1,0:T(8,128)S(1)}, u32[]{:S(2)}, u32[]{:S(2)}) collective-permute-start(f32[512,128]{1,0:T(8,128)S(1)} %get-tuple-element.70), channel_id=1, source_target_pairs={{0,8},{8,0},{16,24},{24,16},{32,40},{40,32},{48,56},{56,48},{64,72... | collective-permute-start | bytes 786440 | tf_op jit(solution)/shard_map/ppermute | solution.py:635
  82.0 15.4 %collective-permute-start.7 = (f32[512,128]{1,0:T(8,128)S(1)}, f32[512,128]{1,0:T(8,128)S(1)}, u32[]{:S(2)}, u32[]{:S(2)}) collective-permute-start(f32[512,128]{1,0:T(8,128)S(1)} %get-tuple-element.71), channel_id=1, source_target_pairs={{8,16},{16,8},{24,32},{32,24},{40,48},{48,40},{56,64},{64,56},{72,... | collective-permute-start | bytes 786440 | tf_op jit(solution)/shard_map/ppermute | solution.py:636
  85.0 9.4 %collective-permute-start.9 = (f32[72,128]{1,0:T(8,128)S(1)}, f32[72,128]{1,0:T(8,128)S(1)}, u32[]{:S(2)}, u32[]{:S(2)}) collective-permute-start(f32[72,128]{1,0:T(8,128)S(1)} %get-tuple-element.73.own_column_ref), channel_id=1, source_target_pairs={{0,1},{1,0},{2,3},{3,2},{4,5},{5,4},{6,7},{7,6},{8,9},{9,8},{10,11... | collective-permute-start | bytes 110600 | tf_op jit(solution)/shard_map/ppermute | solution.py:638
  85.3 12.0 %collective-permute-start.8 = (f32[72,128]{1,0:T(8,128)S(1)}, f32[72,128]{1,0:T(8,128)S(1)}, u32[]{:S(2)}, u32[]{:S(2)}) collective-permute-start(f32[72,128]{1,0:T(8,128)S(1)} %get-tuple-element.73.own_column_ref), channel_id=1, source_target_pairs={{1,2},{2,1},{3,4},{4,3},{5,6},{6,5},{7,0},{0,7},{9,10},{10,9},{11,... | collective-permute-start | bytes 110600 | tf_op jit(solution)/shard_map/ppermute | solution.py:637
  89.3 5.1 %collective-permute-start.10 = (f32[32,128]{1,0:T(8,128)S(1)}, f32[32,128]{1,0:T(8,128)S(1)}, u32[]{:S(2)}, u32[]{:S(2)}) collective-permute-start(f32[32,128]{1,0:T(8,128)S(1)} %get-tuple-element.74), channel_id=1, source_target_pairs={{0,128},{1,129},{2,130},{3,131},{4,132},{5,133},{6,134},{7,135},{8... | collective-permute-start | bytes 49160 | tf_op jit(solution)/shard_map/ppermute | solution.py:639
  97.4 10.5 %copy-start.3 = (f32[1024,128]{1,0:T(8,128)S(1)}, f32[1024,128]{1,0:T(8,128)}, u32[]{:S(2)}) copy-start(f32[1024,128]{1,0:T(8,128)} %copy-done.2) | copy-start | bytes 1572868
  97.4 10.5 %copy-start.5 = (f32[1024,128]{1,0:T(8,128)S(1)}, f32[1024,128]{1,0:T(8,128)}, u32[]{:S(2)}) copy-start(f32[1024,128]{1,0:T(8,128)} %copy-done.4) | copy-start | bytes 1572868
  97.4 10.5 %copy-start.7 = (f32[1024,128]{1,0:T(8,128)S(1)}, f32[1024,128]{1,0:T(8,128)}, u32[]{:S(2)}) copy-start(f32[1024,128]{1,0:T(8,128)} %copy-done.6) | copy-start | bytes 1572868
  98.5 15.8 %collective-permute-start.11 = (f32[512,128]{1,0:T(8,128)S(1)}, f32[512,128]{1,0:T(8,128)S(1)}, u32[]{:S(2)}, u32[]{:S(2)}) collective-permute-start(f32[512,128]{1,0:T(8,128)S(1)} %get-tuple-element.80), channel_id=1, source_target_pairs={{0,8},{8,0},{16,24},{24,16},{32,40},{40,32},{48,56},{56,48},{64,72... | collective-permute-start | bytes 786440 | tf_op jit(solution)/shard_map/ppermute | solution.py:635
  99.2 15.1 %collective-permute-start.12 = (f32[512,128]{1,0:T(8,128)S(1)}, f32[512,128]{1,0:T(8,128)S(1)}, u32[]{:S(2)}, u32[]{:S(2)}) collective-permute-start(f32[512,128]{1,0:T(8,128)S(1)} %get-tuple-element.81), channel_id=1, source_target_pairs={{8,16},{16,8},{24,32},{32,24},{40,48},{48,40},{56,64},{64,56},{72,... | collective-permute-start | bytes 786440 | tf_op jit(solution)/shard_map/ppermute | solution.py:636
  102.3 8.1 %collective-permute-start.14 = (f32[72,128]{1,0:T(8,128)S(1)}, f32[72,128]{1,0:T(8,128)S(1)}, u32[]{:S(2)}, u32[]{:S(2)}) collective-permute-start(f32[72,128]{1,0:T(8,128)S(1)} %get-tuple-element.79.own_column_ref), channel_id=1, source_target_pairs={{0,1},{1,0},{2,3},{3,2},{4,5},{5,4},{6,7},{7,6},{8,9},{9,8},{10,11... | collective-permute-start | bytes 110600 | tf_op jit(solution)/shard_map/ppermute | solution.py:638
  102.4 11.9 %collective-permute-start.13 = (f32[72,128]{1,0:T(8,128)S(1)}, f32[72,128]{1,0:T(8,128)S(1)}, u32[]{:S(2)}, u32[]{:S(2)}) collective-permute-start(f32[72,128]{1,0:T(8,128)S(1)} %get-tuple-element.79.own_column_ref), channel_id=1, source_target_pairs={{1,2},{2,1},{3,4},{4,3},{5,6},{6,5},{7,0},{0,7},{9,10},{10,9},{11,... | collective-permute-start | bytes 110600 | tf_op jit(solution)/shard_map/ppermute | solution.py:637
  106.6 3.8 %collective-permute-start.15 = (f32[32,128]{1,0:T(8,128)S(1)}, f32[32,128]{1,0:T(8,128)S(1)}, u32[]{:S(2)}, u32[]{:S(2)}) collective-permute-start(f32[32,128]{1,0:T(8,128)S(1)} %get-tuple-element.82), channel_id=1, source_target_pairs={{0,128},{1,129},{2,130},{3,131},{4,132},{5,133},{6,134},{7,135},{8... | collective-permute-start | bytes 49160 | tf_op jit(solution)/shard_map/ppermute | solution.py:639
  (8 other events, 6.4 us)
